TPU v7x, 32 devices: a whole 2x2x4 slice. The times are simulated.
32 devices in a mesh: grp: 16 (over z, y, x), row: 2 (over core).
Axes of the slice: x: 2, y: 2, z: 4, core: 2. Of those that a mesh axis runs over, the one named last changes fastest.
Arguments:
- image_rows: bfloat16 [64, 16, 16, 512], P('grp', 'row'), may hold values from -6 to 6
- grad_out: bfloat16 [64, 16, 16, 512], P(('grp', 'row')), may hold values from -6 to 6
- code_ids: int32 [16384], P(('grp', 'row')), may hold values from 0 to 1023
- dead_flags: int32 [1024], replicated, may hold values from 0 to 1, as said below
- replace_ids: int32 [1024], replicated, may hold values from 0 to 16383
- latents: bfloat16 [16384, 256], P(('grp', 'row')), may hold values from -6 to 6
- codebook: float32 [1024, 256], P(('grp', 'row')), may hold values from -6 to 6
- norm1_gain: bfloat16 [512], replicated, may hold values from 0.5 to 1.5
- norm1_bias: bfloat16 [512], replicated, may hold values from -3 to 3
- conv1_kernel: bfloat16 [3, 3, 512, 512], replicated, may hold values from -0.09375 to 0.09375
- conv1_bias: bfloat16 [512], replicated, may hold values from -3 to 3
- norm2_gain: bfloat16 [512], replicated, may hold values from 0.5 to 1.5
- norm2_bias: bfloat16 [512], replicated, may hold values from -3 to 3
- conv2_kernel: bfloat16 [3, 3, 512, 512], replicated, may hold values from -0.09375 to 0.09375
- conv2_bias: bfloat16 [512], replicated, may hold values from -3 to 3
- norm3_gain: bfloat16 [512], replicated, may hold values from 0.5 to 1.5
- norm3_bias: bfloat16 [512], replicated, may hold values from -3 to 3
- query_weight: bfloat16 [512, 512], replicated, may hold values from -0.25 to 0.25
- query_bias: bfloat16 [512], replicated, may hold values from -3 to 3
- key_weight: bfloat16 [512, 512], replicated, may hold values from -0.25 to 0.25
- value_weight: bfloat16 [512, 512], replicated, may hold values from -0.25 to 0.25
- value_bias: bfloat16 [512], replicated, may hold values from -3 to 3
- out_weight: bfloat16 [512, 512], replicated, may hold values from -2 to 2
- out_bias: bfloat16 [512], replicated, may hold values from -3 to 3
Outputs:
- block_out: bfloat16 [64, 16, 16, 512], P(('grp', 'row'))
- input_grad: bfloat16 [64, 16, 16, 512], P('grp', 'row')
- norm1_gain_grad: float32 [512], replicated
- norm1_bias_grad: float32 [512], replicated
- conv1_kernel_grad: float32 [3, 3, 512, 512], replicated
- conv1_bias_grad: float32 [512], replicated
- norm2_gain_grad: float32 [512], replicated
- norm2_bias_grad: float32 [512], replicated
- conv2_kernel_grad: float32 [3, 3, 512, 512], replicated
- conv2_bias_grad: float32 [512], replicated
- norm3_gain_grad: float32 [512], replicated
- norm3_bias_grad: float32 [512], replicated
- query_weight_grad: float32 [512, 512], replicated
- query_bias_grad: float32 [512], replicated
- key_weight_grad: float32 [512, 512], replicated
- value_weight_grad: float32 [512, 512], replicated
- value_bias_grad: float32 [512], replicated
- out_weight_grad: float32 [512, 512], replicated
- out_bias_grad: float32 [512], replicated
- new_codebook: float32 [1024, 256], P(('grp', 'row'))
- usage: int32 [1024], replicated
- perplexity: float32 [], replicated
Inputs may be any that keep to these rules, and one draw needn't show every extreme that they name: `code_ids`: a code index. `dead_flags`: exactly 256 entries are 1, the others 0. `replace_ids`: a row of latents.
All inputs are finite; a program needn't handle non-finite values.
Results may differ from a plain program's by a relative error of at most 0.014.
The roundings to bfloat16 on the way count: a program that leaves them out, or rounds other values in their place, can miss the bound.
Values may be sent and summed in bfloat16 or wider, within the bound.
No kernel may reach another device: no remote copies, remote signals or barrier semaphores. Data moves between devices by JAX's collectives and lax.ppermute only.
A program may use at most 128 MiB of HBM per device.

v0:
```python
import jax
import jax.numpy as jnp
from jax import lax
from jax.sharding import PartitionSpec as P

G = 32


epsilon = 1e-06


def group_norm(source, scaling, offsets):
    images, height, across, channels = source.shape
    grouped = source.reshape(images, height * across, G, channels // G)
    middle = jnp.mean(grouped, axis=(1, 3), keepdims=True)
    centered = grouped - middle
    spread = jnp.mean(centered * centered, axis=(1, 3), keepdims=True)
    normed = (centered * lax.rsqrt(spread + epsilon)).reshape(images, height, across, channels)
    return normed * scaling + offsets


def norm_swish(source, scaling, offsets):
    return jax.nn.silu(group_norm(source, scaling, offsets))


def padded(source):
    return jnp.pad(source, ((0, 0), (1, 1), (1, 1), (0, 0)))


def conv_taps(source, kernel):
    images, height, across, channels = source.shape
    border = padded(source)
    summed = jnp.zeros((images, height, across, kernel.shape[3]), jnp.float32)
    for tap_row in range(3):
        for tap_col in range(3):
            window = border[:, tap_row : tap_row + height, tap_col : tap_col + across, :]
            summed = summed + lax.dot_general(
                window,
                kernel[tap_row, tap_col],
                (((3,), (0,)), ((), ())),
                preferred_element_type=jnp.float32,
            )
    return summed


def kernel_grad(source, upstream):
    images, height, across, channels = source.shape
    border = padded(source)
    pieces = []
    for tap_row in range(3):
        for tap_col in range(3):
            window = border[:, tap_row : tap_row + height, tap_col : tap_col + across, :]
            pieces.append(
                lax.dot_general(
                    window,
                    upstream,
                    (((0, 1, 2), (0, 1, 2)), ((), ())),
                    preferred_element_type=jnp.float32,
                )
            )
    return jnp.stack(pieces).reshape(3, 3, channels, upstream.shape[3])


def flip_kernel(kernel):
    return jnp.transpose(kernel[::-1, ::-1], (0, 1, 3, 2))


def local(
    image_rows,
    grad_out,
    code_ids,
    dead_flags,
    replace_ids,
    latents,
    codebook,
    norm1_gain,
    norm1_bias,
    conv1_kernel,
    conv1_bias,
    norm2_gain,
    norm2_bias,
    conv2_kernel,
    conv2_bias,
    norm3_gain,
    norm3_bias,
    query_weight,
    query_bias,
    key_weight,
    value_weight,
    value_bias,
    out_weight,
    out_bias,
):
    (
        first_gain,
        first_offset,
        first_bias,
        second_gain,
        second_offset,
        second_bias,
        third_gain,
        third_offset,
        query_offset,
        value_offset,
        out_offset,
    ) = [
        vector.astype(jnp.float32)
        for vector in (
            norm1_gain,
            norm1_bias,
            conv1_bias,
            norm2_gain,
            norm2_bias,
            conv2_bias,
            norm3_gain,
            norm3_bias,
            query_bias,
            value_bias,
            out_bias,
        )
    ]
    regrouped = lax.all_to_all(image_rows, "row", split_axis=0, concat_axis=1, tiled=True)
    images, height, across, channels = regrouped.shape
    positions = height * across
    pixels = images * positions
    key_scale = channels ** (-0.5)
    contract_rows = (((0,), (0,)), ((), ()))
    contract_cols = (((1,), (1,)), ((), ()))
    source = regrouped.astype(jnp.float32)
    first_active = norm_swish(source, first_gain, first_offset).astype(jnp.bfloat16)
    first_filtered = conv_taps(first_active, conv1_kernel) + first_bias
    second_active = norm_swish(first_filtered, second_gain, second_offset).astype(jnp.bfloat16)
    residual = source + (conv_taps(second_active, conv2_kernel) + second_bias)
    normed = (
        group_norm(residual, third_gain, third_offset)
        .astype(jnp.bfloat16)
        .reshape(pixels, channels)
    )
    queries = (
        (jnp.dot(normed, query_weight, preferred_element_type=jnp.float32) + query_offset)
        .astype(jnp.bfloat16)
        .reshape(images, positions, channels)
    )
    key_rows = (
        jnp.dot(normed, key_weight, preferred_element_type=jnp.float32)
        .astype(jnp.bfloat16)
        .reshape(images, positions, channels)
    )
    values = (
        (jnp.dot(normed, value_weight, preferred_element_type=jnp.float32) + value_offset)
        .astype(jnp.bfloat16)
        .reshape(images, positions, channels)
    )
    scores = (
        jnp.einsum("bnd,bmd->bnm", queries, key_rows, preferred_element_type=jnp.float32)
        * key_scale
    )
    peak_score = jnp.max(scores, axis=2, keepdims=True)
    lifted = jnp.exp(scores - peak_score)
    summed = jnp.sum(lifted, axis=2, keepdims=True)
    log_total = peak_score + jnp.log(summed)
    attention_low = (lifted / summed).astype(jnp.bfloat16)
    blended = (
        jnp.einsum("bnm,bmd->bnd", attention_low, values, preferred_element_type=jnp.float32)
        .astype(jnp.bfloat16)
        .reshape(pixels, channels)
    )
    projected = jnp.dot(blended, out_weight, preferred_element_type=jnp.float32) + out_offset
    block_out = (residual + projected.reshape(images, height, across, channels)).astype(
        jnp.bfloat16
    )
    upstream = grad_out.reshape(pixels, channels)
    out_bias_grad = jnp.sum(upstream.astype(jnp.float32), axis=0)
    out_weight_grad = lax.dot_general(
        blended, upstream, contract_rows, preferred_element_type=jnp.float32
    )
    grad_blended = (
        lax.dot_general(upstream, out_weight, contract_cols, preferred_element_type=jnp.float32)
        .astype(jnp.bfloat16)
        .reshape(images, positions, channels)
    )
    rescored = (
        jnp.einsum("bnd,bmd->bnm", queries, key_rows, preferred_element_type=jnp.float32)
        * key_scale
    )
    attention = jnp.exp(rescored - log_total)
    grad_values = (
        jnp.einsum(
            "bnm,bnd->bmd",
            attention.astype(jnp.bfloat16),
            grad_blended,
            preferred_element_type=jnp.float32,
        )
        .astype(jnp.bfloat16)
        .reshape(pixels, channels)
    )
    grad_attention = jnp.einsum(
        "bnd,bmd->bnm", grad_blended, values, preferred_element_type=jnp.float32
    )
    grad_scores = (
        attention * (grad_attention - jnp.sum(attention * grad_attention, axis=2, keepdims=True))
    ).astype(jnp.bfloat16)
    grad_queries = (
        (
            jnp.einsum("bnm,bmd->bnd", grad_scores, key_rows, preferred_element_type=jnp.float32)
            * key_scale
        )
        .astype(jnp.bfloat16)
        .reshape(pixels, channels)
    )
    grad_keys = (
        (
            jnp.einsum("bnm,bnd->bmd", grad_scores, queries, preferred_element_type=jnp.float32)
            * key_scale
        )
        .astype(jnp.bfloat16)
        .reshape(pixels, channels)
    )
    query_bias_grad = jnp.sum(grad_queries.astype(jnp.float32), axis=0)
    value_bias_grad = jnp.sum(grad_values.astype(jnp.float32), axis=0)
    query_weight_grad = lax.dot_general(
        normed, grad_queries, contract_rows, preferred_element_type=jnp.float32
    )
    key_weight_grad = lax.dot_general(
        normed, grad_keys, contract_rows, preferred_element_type=jnp.float32
    )
    value_weight_grad = lax.dot_general(
        normed, grad_values, contract_rows, preferred_element_type=jnp.float32
    )
    grad_normed = lax.dot_general(
        grad_queries, query_weight, contract_cols, preferred_element_type=jnp.float32
    )
    grad_normed = grad_normed + lax.dot_general(
        grad_keys, key_weight, contract_cols, preferred_element_type=jnp.float32
    )
    grad_normed = grad_normed + lax.dot_general(
        grad_values, value_weight, contract_cols, preferred_element_type=jnp.float32
    )
    skipped, third_pull = jax.vjp(group_norm, residual, third_gain, third_offset)
    grad_residual, third_gain_grad, third_offset_grad = third_pull(
        grad_normed.reshape(images, height, across, channels)
    )
    grad_residual = grad_residual + grad_out.astype(jnp.float32)
    grad_second_out = grad_residual.astype(jnp.bfloat16)
    second_bias_grad = jnp.sum(grad_second_out.astype(jnp.float32), axis=(0, 1, 2))
    conv2_kernel_grad = kernel_grad(second_active, grad_second_out)
    grad_second = conv_taps(grad_second_out, flip_kernel(conv2_kernel))
    skipped, second_pull = jax.vjp(norm_swish, first_filtered, second_gain, second_offset)
    grad_first_filtered, second_gain_grad, second_offset_grad = second_pull(grad_second)
    grad_first_out = grad_first_filtered.astype(jnp.bfloat16)
    first_bias_grad = jnp.sum(grad_first_out.astype(jnp.float32), axis=(0, 1, 2))
    conv1_kernel_grad = kernel_grad(first_active, grad_first_out)
    grad_first = conv_taps(grad_first_out, flip_kernel(conv1_kernel))
    skipped, first_pull = jax.vjp(norm_swish, source, first_gain, first_offset)
    grad_source, first_gain_grad, first_offset_grad = first_pull(grad_first)
    input_local = (grad_residual + grad_source).astype(jnp.bfloat16)
    input_grad = lax.all_to_all(input_local, "row", split_axis=1, concat_axis=0, tiled=True)
    code_range = jnp.arange(dead_flags.shape[0], dtype=jnp.int32)
    counts = jnp.sum((code_ids[:, None] == code_range[None, :]).astype(jnp.float32), axis=0)
    (
        first_gain_grad,
        first_offset_grad,
        conv1_kernel_grad,
        first_bias_grad,
        second_gain_grad,
        second_offset_grad,
        conv2_kernel_grad,
        second_bias_grad,
        counts,
        third_gain_grad,
        third_offset_grad,
        query_weight_grad,
        query_bias_grad,
        key_weight_grad,
        value_weight_grad,
        value_bias_grad,
        out_weight_grad,
        out_bias_grad,
    ) = lax.psum(
        (
            first_gain_grad,
            first_offset_grad,
            conv1_kernel_grad,
            first_bias_grad,
            second_gain_grad,
            second_offset_grad,
            conv2_kernel_grad,
            second_bias_grad,
            counts,
            third_gain_grad,
            third_offset_grad,
            query_weight_grad,
            query_bias_grad,
            key_weight_grad,
            value_weight_grad,
            value_bias_grad,
            out_weight_grad,
            out_bias_grad,
        ),
        ("grp", "row"),
    )
    shares = counts / jnp.sum(counts)
    perplexity = jnp.exp(-jnp.sum(shares * jnp.log(shares + 1e-10)))
    usage = counts.astype(jnp.int32)
    local_pixels = latents.shape[0]
    book_rows = codebook.shape[0]
    device_index = lax.axis_index(("grp", "row"))
    pixel_offset = device_index * local_pixels
    pixel_range = jnp.arange(local_pixels, dtype=jnp.int32)
    own_flags = lax.dynamic_slice_in_dim(dead_flags, device_index * book_rows, book_rows)
    wanted = replace_ids - pixel_offset
    chosen = (wanted[:, None] == pixel_range[None, :]).astype(jnp.bfloat16)
    fetched = lax.psum_scatter(
        jnp.dot(chosen, latents, preferred_element_type=jnp.float32),
        ("grp", "row"),
        scatter_dimension=0,
        tiled=True,
    )
    new_codebook = jnp.where(own_flags[:, None] == 1, fetched, codebook)
    return (
        block_out,
        input_grad,
        first_gain_grad,
        first_offset_grad,
        conv1_kernel_grad,
        first_bias_grad,
        second_gain_grad,
        second_offset_grad,
        conv2_kernel_grad,
        second_bias_grad,
        third_gain_grad,
        third_offset_grad,
        query_weight_grad,
        query_bias_grad,
        key_weight_grad,
        value_weight_grad,
        value_bias_grad,
        out_weight_grad,
        out_bias_grad,
        new_codebook,
        usage,
        perplexity,
    )


def solution(mesh):
    in_specs = (
        P("grp", "row", None, None),
        P(("grp", "row"), None, None, None),
        P(("grp", "row")),
        P(),
        P(),
        P(("grp", "row"), None),
        P(("grp", "row"), None),
        P(),
        P(),
        P(),
        P(),
        P(),
        P(),
        P(),
        P(),
        P(),
        P(),
        P(),
        P(),
        P(),
        P(),
        P(),
        P(),
        P(),
    )
    out_specs = (
        P(("grp", "row"), None, None, None),
        P("grp", "row", None, None),
        P(),
        P(),
        P(),
        P(),
        P(),
        P(),
        P(),
        P(),
        P(),
        P(),
        P(),
        P(),
        P(),
        P(),
        P(),
        P(),
        P(),
        P(("grp", "row"), None),
        P(),
        P(),
    )
    return jax.shard_map(local, mesh=mesh, in_specs=in_specs, out_specs=out_specs, check_vma=False)
```

profile of v0, /device:TPU:0, one launch (start us, length us, event | category | flops | bytes accessed | tf_op | source)
XLA Modules:
  0.0 556.5 jit_solution(8809578873958543179)
XLA Ops:
  7.2 3.6 all-to-all-start
  11.6 2.4 fusion
  32.0 1.7 fusion.43
  40.6 5.0 reshape.298
  49.2 1.7 convolution_convert_fusion.1
  55.4 6.6 %copy.106 = bf16[3,3,512,512]{2,3,1,0:T(8,128)(2,1)} copy(bf16[3,3,512,512]{3,2,1,0:T(8,128)(2,1)} %param.37) | data formatting | bytes 9437184 | tf_op args[13]
  62.0 2.3 convolution_convert_fusion.2
  64.3 2.6 fusion.139
  68.5 6.1 %copy.103 = f32[2,256,32,16]{1,0,3,2:T(2,128)} copy(f32[2,256,32,16]{3,2,1,0:T(8,128)} %reshape.298) | data formatting | bytes 2097152 | tf_op jit(solution)/shard_map/reshape | solution.py:14
  74.6 2.6 fusion.141
  77.2 2.0 convolution_add_fusion.17
  82.3 2.5 copy.100
  84.8 2.9 reshape.297
  87.9 2.9 fusion.27
  91.3 2.8 reverse_bitcast_fusion.1
  99.6 1.9 fusion.133
  101.8 1.9 multiply_reduce_fusion.1
  104.1 1.9 convert_reduce_fusion.5
  113.6 3.3 copy-done.13
  122.4 3.7 copy-done.12
  126.2 6.9 %copy.107 = bf16[3,3,512,512]{2,3,1,0:T(8,128)(2,1)} copy(bf16[3,3,512,512]{3,2,1,0:T(8,128)(2,1)} %param.33) | data formatting | bytes 9437184 | tf_op args[9]
  133.1 2.6 reverse_bitcast_fusion
  139.4 1.9 fusion.134
  141.7 1.6 multiply_reduce_fusion.2
  143.7 1.6 convolution_add_fusion.18
  145.3 3.1 add_convert_fusion
  149.3 3.5 all-to-all-start.1
  155.6 44.6 %all-reduce.4 = (f32[512]{0:T(512)}, f32[512]{0:T(512)}, f32[512]{0:T(512)}, f32[512]{0:T(512)}, f32[512]{0:T(512)}, /*index=5*/f32[512]{0:T(512)}, f32[512]{0:T...) all-reduce(f32[512]{0:T(512)S(1)} %get-tuple-element.24, ...), channel_id=1, replica_groups=mesh['grp'=16,'row'=2] {'grp','row'}, use_global_device_ids=true, to_apply=%region_27.28 | all-reduce | flops 6656 | bytes 53248 | tf_op jit(solution)/shard_map/psum | solution.py:279
  200.8 1.8 multiply_reduce_fusion.10
  205.6 325.8 %all-reduce.8.cloned.1.call-done = (f32[3,3,512,512]{3,2,1,0:T(8,128)}, f32[3,3,512,512]{3,2,1,0:T(8,128)}, f32[512,512]{1,0:T(8,128)}, f32[512,512]{1,0:T(8,128...) async-done(((f32[3,3,512,512]{3,2,1,0:T(8,128)}, f32[3,3,512,512]{3,2,1,0:T(8,128)}, f32[512,512]{1,0:T(8,128)}, f32[512,512]{1,0:T(8,128)}, f32[512,512]{1,0:T(8,128)}, ...) | async-done | bytes 23068688 | tf_op jit(solution)/shard_map/psum | solution.py:279
  531.4 8.8 %copy.191 = f32[3,3,512,512]{3,2,1,0:T(8,128)} copy(f32[3,3,512,512]{3,2,1,0:T(8,128)} %get-tuple-element.78) | data formatting | bytes 18874368
  540.2 4.1 copy.192
  (260 shorter events, 72.3 us)
Async XLA Ops:
  7.2 43.7 %copy-start = (bf16[512,512]{1,0:T(8,128)(2,1)S(1)}, bf16[512,512]{1,0:T(8,128)(2,1)}, u32[]{:S(2)}) copy-start(bf16[512,512]{1,0:T(8,128)(2,1)} %param.44) | copy-start | bytes 1572868
  7.2 8.3 %copy-start.31 = (bf16[512]{0:T(512)(128)(2,1)S(1)}, bf16[512]{0:T(512)(128)(2,1)}, u32[]{:S(2)}) copy-start(bf16[512]{0:T(512)(128)(2,1)} %param.32) | copy-start | bytes 3076
  7.2 9.3 %copy-start.32 = (bf16[512]{0:T(512)(128)(2,1)S(1)}, bf16[512]{0:T(512)(128)(2,1)}, u32[]{:S(2)}) copy-start(bf16[512]{0:T(512)(128)(2,1)} %param.35) | copy-start | bytes 3076
  7.2 9.3 %copy-start.33 = (bf16[512]{0:T(512)(128)(2,1)S(1)}, bf16[512]{0:T(512)(128)(2,1)}, u32[]{:S(2)}) copy-start(bf16[512]{0:T(512)(128)(2,1)} %param.34) | copy-start | bytes 3076
  7.2 7.6 %all-to-all-start = ((bf16[4,8,16,512]{3,2,1,0:T(8,128)(2,1)}), bf16[4,8,16,512]{3,2,1,0:T(8,128)(2,1)S(1)}, u32[]{:S(2)}, u32[]{:S(2)}) async-start(bf16[4,8,16,512]{3,2,1,0:T(8,128)(2,1)} %param.24), calls=%async_computation | async-start | bytes 1048576 | tf_op jit(solution)/shard_map/all_to_all | solution.py:122
  10.9 193.2 %reduce-scatter.2.cloned.1.call-start = ((), (), s32[]{:S(2)}) async-start(), calls=%async_computation.3 | async-start | bytes 1081344 | tf_op jit(solution)/shard_map/reduce_scatter | solution.py:313
  14.1 517.3 %all-reduce.8.cloned.1.call-start = ((), (), s32[]{:S(2)}) async-start(), calls=%async_computation.4 | async-start | bytes 46137344 | tf_op jit(solution)/shard_map/psum | solution.py:279
  14.9 4.9 copy-start.2
  26.2 4.9 copy-start.34
  26.3 5.4 copy-start.35
  30.8 6.0 %copy-start.5 = (f32[2,16,16,512]{3,2,1,0:T(8,128)}, f32[2,16,16,512]{3,2,1,0:T(8,128)S(1)}, u32[]{:S(2)}) copy-start(f32[2,16,16,512]{3,2,1,0:T(8,128)S(1)} %get-tuple-element.60) | copy-start | bytes 3145732
  31.7 6.6 %slice-start = ((s8[4718592]{0:T(1024)(128)(4,1)}), s8[4194304]{0:T(1024)(128)(4,1)S(1)}, s32[]{:S(2)}) async-start(s8[4718592]{0:T(1024)(128)(4,1)} %bitcast.513), calls=%async_computation.5 | async-start | bytes 8388608
  33.7 4.6 slice-start.1
  40.6 5.9 %copy-start.29 = (bf16[512]{0:T(512)(128)(2,1)S(1)}, bf16[512]{0:T(512)(128)(2,1)}, u32[]{:S(2)}) copy-start(bf16[512]{0:T(512)(128)(2,1)} %param.39) | copy-start | bytes 3076
  40.6 5.9 %copy-start.36 = (bf16[512]{0:T(512)(128)(2,1)S(1)}, bf16[512]{0:T(512)(128)(2,1)}, u32[]{:S(2)}) copy-start(bf16[512]{0:T(512)(128)(2,1)} %param.40) | copy-start | bytes 3076
  40.6 5.9 %copy-start.37 = (bf16[512]{0:T(512)(128)(2,1)S(1)}, bf16[512]{0:T(512)(128)(2,1)}, u32[]{:S(2)}) copy-start(bf16[512]{0:T(512)(128)(2,1)} %param.42) | copy-start | bytes 3076
  40.6 6.1 %copy-start.19 = (bf16[512,512]{1,0:T(8,128)(2,1)S(1)}, bf16[512,512]{1,0:T(8,128)(2,1)}, u32[]{:S(2)}) copy-start(bf16[512,512]{1,0:T(8,128)(2,1)} %param.43) | copy-start | bytes 1572868
  46.7 4.9 copy-start.8
  62.0 5.0 copy-start.9
  62.0 5.0 copy-start.17
  68.5 6.1 %copy-start.10 = (bf16[2,16,16,512]{3,2,1,0:T(8,128)(2,1)S(1)}, bf16[2,16,16,512]{3,2,1,0:T(8,128)(2,1)}, u32[]{:S(2)}) copy-start(bf16[2,16,16,512]{3,2,1,0:T(8,128)(2,1)} %copy-done.8) | copy-start | bytes 1572868
  74.6 4.6 copy-start.18
  122.4 3.7 copy-start.12
  139.4 4.3 copy-start.39
  139.4 5.9 %copy-start.16 = (bf16[2,16,16,512]{3,2,1,0:T(8,128)(2,1)S(1)}, bf16[2,16,16,512]{3,2,1,0:T(8,128)(2,1)}, u32[]{:S(2)}) copy-start(bf16[2,16,16,512]{3,2,1,0:T(8,128)(2,1)} %param.25) | copy-start | bytes 1572868
  145.3 10.0 %copy-start.30 = (s32[512]{0:T(512)S(1)}, s32[512]{0:T(512)}, u32[]{:S(2)}) copy-start(s32[512]{0:T(512)} %param.26) | copy-start | bytes 6148
  145.3 58.8 %copy-start.26 = (f32[32,256]{1,0:T(8,128)S(1)}, f32[32,256]{1,0:T(8,128)}, u32[]{:S(2)}) copy-start(f32[32,256]{1,0:T(8,128)} %param.30) | copy-start | bytes 98308
  149.3 5.2 all-to-all-start.1
  531.4 8.8 %copy-start.11 = (f32[3,3,512,512]{3,2,1,0:T(8,128)S(1)}, f32[3,3,512,512]{3,2,1,0:T(8,128)}, u32[]{:S(2)}) copy-start(f32[3,3,512,512]{3,2,1,0:T(8,128)} %get-tuple-element.82) | copy-start | bytes 28311556
  540.2 4.1 copy-start.24
  540.2 5.0 copy-start.23
  540.2 8.0 %copy-start.1 = (bf16[512,512]{1,0:T(8,128)(2,1)S(1)}, bf16[512,512]{1,0:T(8,128)(2,1)}, u32[]{:S(2)}) copy-start(bf16[512,512]{1,0:T(8,128)(2,1)} %param.44) | copy-start | bytes 1572868
  (17 other events, 38.5 us)
Sparse Core Ops, SparseCore 0:
  14.2 137.6 reduce-scatter.1
  160.6 370.7 all-reduce.7
where the time goes:
time: 565 us; the launch traced here: 557 us
  waiting for transfers between devices  326 us (58%)
  matrix products  69.9 us (12%)
  local copies, waits for them, and re-layouts  68.6 us (12%)
  blocking collectives  44.6 us (8%)
  other arithmetic  22.6 us (4%)
  between operations  17.4 us (3%)
  starting transfers between devices  7.2 us (1%)
    psum x1, waiting for transfers between devices, local(): lax.psum((first_gain_grad, first_offset_grad, conv1_kernel_grad, first_bi...  326 us
    psum x1, blocking collectives, local(): lax.psum((first_gain_grad, first_offset_grad, conv1_kernel_grad, first_bi...  44.6 us
    unnamed x98, local copies, waits for them, and re-layouts  41.5 us
    dot_general x36, matrix products, conv_taps(): lax.dot_general(window, kernel[tap_row, tap_col], (((3,), (0,)), ((), ())...  32.7 us
  transfers between devices with their start and end apart: 4, of which 2 were waited for; matrix products, arithmetic and copies ran while one was open for 24% of the time, Pallas kernels for 0%

commit v1 on v0

v1 whole, which is shorter than its diff:
```python
import functools

import jax
import jax.numpy as jnp
from jax import lax
from jax.experimental import pallas as pl
from jax.experimental.pallas import tpu as pltpu
from jax.sharding import PartitionSpec as P

EPS = 1e-06
GROUP = 16
DEAD = 256
AXES = ("grp", "row")
F32 = jnp.float32
BF = jnp.bfloat16
NN = (((1,), (0,)), ((), ()))
NT = (((1,), (1,)), ((), ()))
TN = (((0,), (0,)), ((), ()))
VMEM = pl.BlockSpec(memory_space=pltpu.VMEM)
SMEM = pl.BlockSpec(memory_space=pltpu.SMEM)
HBM = pl.BlockSpec(memory_space=pl.ANY)
shape_of = jax.ShapeDtypeStruct


def mm(a, b, dims=NN):
    return lax.dot_general(a, b, dims, preferred_element_type=F32)


def colsum(v):
    return jnp.sum(v, axis=0, keepdims=True)


def group_sum(v):
    lanes = v.shape[1]
    lane = lax.broadcasted_iota(jnp.int32, v.shape, 1)
    step = 1
    while step < GROUP:
        below = pltpu.roll(v, step, 1)
        above = pltpu.roll(v, lanes - step, 1)
        v = v + jnp.where((lane & step) != 0, below, above)
        step *= 2
    return v


def normalized(v):
    count = v.shape[0] * GROUP
    middle = group_sum(colsum(v)) / count
    centered = v - middle
    spread = group_sum(colsum(centered * centered)) / count
    scale = lax.rsqrt(spread + EPS)
    return centered * scale, scale


def norm_back(n, scale, gain, dy):
    count = n.shape[0] * GROUP
    bias_grad = colsum(dy)
    gain_grad = colsum(dy * n)
    mean_d = group_sum(bias_grad * gain) / count
    mean_dn = group_sum(gain_grad * gain) / count
    return scale * (dy * gain - mean_d - n * mean_dn), gain_grad, bias_grad


def sigmoid(y):
    return 1.0 / (1.0 + jnp.exp(-y))


def shifted(v, side):
    px = v.shape[0]
    col = lax.broadcasted_iota(jnp.int32, v.shape, 0) % side
    left = jnp.where(col == 0, 0.0, pltpu.roll(v, 1, 0))
    right = jnp.where(col == side - 1, 0.0, pltpu.roll(v, px - 1, 0))
    return left, v, right


def put_shifts(s_ref, image, v, side):
    px, ch = v.shape
    for j, t in enumerate(shifted(v, side)):
        s_ref[image, side : px + side, j * ch : (j + 1) * ch] = t.astype(BF)


def clear_edges(s_ref, side):
    images, rows, width = s_ref.shape
    zero = jnp.zeros((side, width), BF)
    for i in range(images):
        s_ref[i, 0:side, :] = zero
        s_ref[i, rows - side : rows, :] = zero


def conv(s_ref, w_ref, image, px, side, ch):
    acc = None
    for dh in range(3):
        part = mm(
            s_ref[image, dh * side : dh * side + px, :],
            w_ref[dh * 3 * ch : (dh + 1) * 3 * ch, :],
        )
        acc = part if acc is None else acc + part
    return acc


def conv_back(s_ref, w_ref, image, px, side, ch):
    acc = None
    for dh in range(3):
        for dw in range(3):
            tap = dh * 3 + dw
            first = (2 - dh) * side
            part = mm(
                s_ref[image, first : first + px, (2 - dw) * ch : (3 - dw) * ch],
                w_ref[tap * ch : (tap + 1) * ch, :],
                NT,
            )
            acc = part if acc is None else acc + part
    return acc


def gather_rows(dst_ref, mine_ref, other_ref, core):
    images, part, ch = other_ref.shape
    for i in range(images):
        dst_ref[i, pl.ds(pl.multiple_of(core * part, part), part), :] = mine_ref[core * images + i]
        dst_ref[i, pl.ds(pl.multiple_of((1 - core) * part, part), part), :] = other_ref[i]


def split_cols(v, core):
    half = v.shape[1] // 2
    low, high = v[:, :half], v[:, half:]
    return jnp.where(core == 0, low, high), jnp.where(core == 0, high, low)


def forward_body(
    place_ref, mine_ref, other_ref, gy_ref, vec_ref, w1_hbm, w2_hbm, wq_hbm, wk_hbm, wv_hbm, wo_hbm,
    out_ref, act1_ref, act2_ref, conv1_ref, dres_ref, dkeep_ref, dsend_ref, stat_ref, gkeep_ref, gsend_ref,
    s_ref, x_ref, w1, w2, wq, wk, wv, wo, normed, q, k, v, mixed, sems, *, side,
):
    images, px, ch = x_ref.shape
    core = place_ref[0]
    me = place_ref[1]
    pairs = ((w1_hbm, w1), (w2_hbm, w2), (wq_hbm, wq), (wk_hbm, wk), (wv_hbm, wv), (wo_hbm, wo))
    copies = [pltpu.make_async_copy(a, b, sems.at[i]) for i, (a, b) in enumerate(pairs)]
    for c in copies:
        c.start()

    def row(i):
        return vec_ref[i : i + 1, :]

    clear_edges(s_ref, side)
    gather_rows(x_ref, mine_ref, other_ref, core)

    def first(i, carry):
        n, _ = normalized(x_ref[i].astype(F32))
        y = n * row(0) + row(1)
        a = y * sigmoid(y)
        act1_ref[i] = a.astype(BF)
        put_shifts(s_ref, i, a, side)
        return carry

    lax.fori_loop(0, images, first, 0)
    copies[0].wait()

    def second(i, carry):
        conv1_ref[i] = conv(s_ref, w1, i, px, side, ch) + row(2)
        return carry

    lax.fori_loop(0, images, second, 0)

    def third(i, carry):
        n, _ = normalized(conv1_ref[i])
        y = n * row(3) + row(4)
        a = y * sigmoid(y)
        act2_ref[i] = a.astype(BF)
        put_shifts(s_ref, i, a, side)
        return carry

    lax.fori_loop(0, images, third, 0)
    copies[1].wait()

    def fourth(i, carry):
        res = x_ref[i].astype(F32) + (conv(s_ref, w2, i, px, side, ch) + row(5))
        dres_ref[i] = res
        n, _ = normalized(res)
        normed[i] = (n * row(6) + row(7)).astype(BF)
        return carry

    lax.fori_loop(0, images, fourth, 0)
    for c in copies[2:]:
        c.wait()
    scale = ch ** -0.5
    stat_ref[...] = jnp.zeros(stat_ref.shape, F32)

    def attend(i, carry):
        nb = normed[i]
        qi = (mm(nb, wq[...]) + row(8)).astype(BF)
        ki = mm(nb, wk[...]).astype(BF)
        vi = (mm(nb, wv[...]) + row(9)).astype(BF)
        scores = mm(qi, ki, NT) * scale
        peak = jnp.max(scores, axis=1, keepdims=True)
        lifted = jnp.exp(scores - peak)
        probs = lifted / jnp.sum(lifted, axis=1, keepdims=True)
        pb = probs.astype(BF)
        mi = mm(pb, vi).astype(BF)
        mixed[i] = mi
        res = dres_ref[i]
        out_ref[i] = (res + (mm(mi, wo[...]) + row(10))).astype(BF)
        gy = gy_ref[i]
        gyf = gy.astype(F32)
        dm = mm(gy, wo[...], NT).astype(BF)
        dv = mm(pb, dm, TN).astype(BF)
        dp = mm(dm, vi, NT)
        ds = (probs * (dp - jnp.sum(probs * dp, axis=1, keepdims=True))).astype(BF)
        dq = (mm(ds, ki) * scale).astype(BF)
        dk = (mm(ds, qi, TN) * scale).astype(BF)
        q[i] = dq
        k[i] = dk
        v[i] = dv
        dn = mm(dq, wq[...], NT) + mm(dk, wk[...], NT) + mm(dv, wv[...], NT)
        n, r = normalized(res)
        dx, gain_grad, bias_grad = norm_back(n, r, row(6), dn)
        dres = gyf + dx
        dres_ref[i] = dres
        db = dres.astype(BF)
        dkeep_ref[i], dsend_ref[i] = split_cols(db, core)
        stat_ref[0:1, :] += colsum(db.astype(F32))
        stat_ref[1:2, :] += gain_grad
        stat_ref[2:3, :] += bias_grad
        stat_ref[3:4, :] += colsum(dq.astype(F32))
        stat_ref[4:5, :] += colsum(dv.astype(F32))
        stat_ref[5:6, :] += colsum(gyf)
        return carry

    lax.fori_loop(0, images, attend, 0)
    owners, _, rows, _ = gkeep_ref.shape

    def flat(ref):
        return ref[...].reshape(images * px, ch)

    for j, (lhs, rhs) in enumerate(((normed, q), (normed, k), (normed, v), (mixed, gy_ref))):
        keep, send = split_cols(mm(flat(lhs), flat(rhs), TN).astype(BF), core)
        for o in range(owners):
            gkeep_ref[o ^ me, j] = keep[o * rows : (o + 1) * rows]
            gsend_ref[o ^ me, j] = send[o * rows : (o + 1) * rows]


def run_forward(place, mine, other, gy, vec, w1, w2, wq, wk, wv, wo, owners, side):
    images, px, ch = gy.shape
    half = ch // 2
    rows = ch // owners
    whole = (images, px, ch)
    return pl.pallas_call(
        functools.partial(forward_body, side=side),
        name="forward_attention",
        in_specs=[SMEM] + [VMEM] * 4 + [HBM] * 6,
        out_specs=[VMEM] * 10,
        out_shape=[
            shape_of(whole, BF), shape_of(whole, BF), shape_of(whole, BF),
            shape_of(whole, F32), shape_of(whole, F32),
            shape_of((images, px, half), BF), shape_of((images, px, half), BF),
            shape_of((8, ch), F32),
            shape_of((owners, 4, rows, half), BF), shape_of((owners, 4, rows, half), BF),
        ],
        scratch_shapes=[
            pltpu.VMEM((images, px + 2 * side, 3 * ch), BF),
            pltpu.VMEM(whole, BF),
            pltpu.VMEM((9 * ch, ch), BF), pltpu.VMEM((9 * ch, ch), BF),
        ]
        + [pltpu.VMEM((ch, ch), BF)] * 4
        + [pltpu.VMEM(whole, BF)] * 5
        + [pltpu.SemaphoreType.DMA((6,))],
        compiler_params=pltpu.CompilerParams(vmem_limit_bytes=52 << 20),
    )(place, mine, other, gy, vec, w1, w2, wq, wk, wv, wo)


def back2_body(
    place_ref, dres_ref, conv1_ref, vec_ref, w2_hbm,
    dkeep_ref, dsend_ref, dfull_ref, stat_ref, s_ref, w2, sem, *, side,
):
    images, px, ch = dres_ref.shape
    core = place_ref[0]
    copy = pltpu.make_async_copy(w2_hbm, w2, sem)
    copy.start()
    clear_edges(s_ref, side)
    stat_ref[...] = jnp.zeros(stat_ref.shape, F32)

    def row(i):
        return vec_ref[i : i + 1, :]

    def shifts(i, carry):
        put_shifts(s_ref, i, dres_ref[i], side)
        return carry

    lax.fori_loop(0, images, shifts, 0)
    copy.wait()

    def body(i, carry):
        da = conv_back(s_ref, w2, i, px, side, ch)
        n, r = normalized(conv1_ref[i])
        y = n * row(3) + row(4)
        sig = sigmoid(y)
        dy = da * (sig * (1.0 + y * (1.0 - sig)))
        dx, gain_grad, bias_grad = norm_back(n, r, row(3), dy)
        db = dx.astype(BF)
        dfull_ref[i] = db
        dkeep_ref[i], dsend_ref[i] = split_cols(db, core)
        stat_ref[0:1, :] += gain_grad
        stat_ref[1:2, :] += bias_grad
        stat_ref[2:3, :] += colsum(db.astype(F32))
        return carry

    lax.fori_loop(0, images, body, 0)


def run_back2(place, dres, conv1, vec, w2, side):
    images, px, ch = dres.shape
    half = (images, px, ch // 2)
    return pl.pallas_call(
        functools.partial(back2_body, side=side),
        name="conv2_back",
        in_specs=[SMEM, VMEM, VMEM, VMEM, HBM],
        out_specs=[VMEM] * 4,
        out_shape=[shape_of(half, BF), shape_of(half, BF), shape_of((images, px, ch), BF), shape_of((8, ch), F32)],
        scratch_shapes=[
            pltpu.VMEM((images, px + 2 * side, 3 * ch), BF),
            pltpu.VMEM((9 * ch, ch), BF),
            pltpu.SemaphoreType.DMA(()),
        ],
        compiler_params=pltpu.CompilerParams(vmem_limit_bytes=40 << 20),
    )(place, dres, conv1, vec, w2)


def back1_body(
    place_ref, dfull_ref, mine_ref, other_ref, dres_ref, vec_ref, w1_hbm,
    keep_ref, send_ref, stat_ref, s_ref, x_ref, w1, sem, *, side,
):
    images, px, ch = dres_ref.shape
    part = px // 2
    core = place_ref[0]
    copy = pltpu.make_async_copy(w1_hbm, w1, sem)
    copy.start()
    clear_edges(s_ref, side)
    stat_ref[...] = jnp.zeros(stat_ref.shape, F32)
    gather_rows(x_ref, mine_ref, other_ref, core)

    def row(i):
        return vec_ref[i : i + 1, :]

    def shifts(i, carry):
        put_shifts(s_ref, i, dfull_ref[i].astype(F32), side)
        return carry

    lax.fori_loop(0, images, shifts, 0)
    copy.wait()

    def body(i, carry):
        da = conv_back(s_ref, w1, i, px, side, ch)
        n, r = normalized(x_ref[i].astype(F32))
        y = n * row(0) + row(1)
        sig = sigmoid(y)
        dy = da * (sig * (1.0 + y * (1.0 - sig)))
        dx, gain_grad, bias_grad = norm_back(n, r, row(0), dy)
        stat_ref[0:1, :] += gain_grad
        stat_ref[1:2, :] += bias_grad
        total = (dres_ref[i] + dx).astype(BF)
        low, high = total[:part], total[part:]
        keep_ref[i] = jnp.where(core == 0, low, high)
        send_ref[i] = jnp.where(core == 0, high, low)
        return carry

    lax.fori_loop(0, images, body, 0)


def run_back1(place, dfull, mine, other, dres, vec, w1, side):
    images, px, ch = dres.shape
    part = (images, px // 2, ch)
    return pl.pallas_call(
        functools.partial(back1_body, side=side),
        name="conv1_back",
        in_specs=[SMEM] + [VMEM] * 5 + [HBM],
        out_specs=[VMEM] * 3,
        out_shape=[shape_of(part, BF), shape_of(part, BF), shape_of((8, ch), F32)],
        scratch_shapes=[
            pltpu.VMEM((images, px + 2 * side, 3 * ch), BF),
            pltpu.VMEM((images, px, ch), BF),
            pltpu.VMEM((9 * ch, ch), BF),
            pltpu.SemaphoreType.DMA(()),
        ],
        compiler_params=pltpu.CompilerParams(vmem_limit_bytes=40 << 20),
    )(place, dfull, mine, other, dres, vec, w1)


def kernel_grad_body(place_ref, a0_ref, a1_ref, d0_ref, d1_ref, low_ref, high_ref, s_ref, d_ref, *, side):
    images, px, ch = a0_ref.shape
    half = d0_ref.shape[2]
    quarter = half // 2
    me = place_ref[1]
    owners, _, rows, _ = low_ref.shape
    zero = jnp.zeros((side, half), BF)
    for n in range(2 * images):
        d_ref[n, 0:side, :] = zero
        d_ref[n, px + side :, :] = zero
    for n, (a, d) in enumerate(((a0_ref, d0_ref), (a1_ref, d1_ref))):

        def fill(i, carry, a=a, d=d, n=n):
            at = n * images + i
            d_ref[at, side : px + side, :] = d[i]
            for j, t in enumerate(shifted(a[i].astype(F32), side)):
                s_ref[j * ch : (j + 1) * ch, pl.ds(pl.multiple_of(at * px, px), px)] = t.astype(BF).T
            return carry

        lax.fori_loop(0, images, fill, 0)
    for dh in range(3):
        start = (2 - dh) * side
        d = jnp.concatenate([d_ref[n, start : start + px, :] for n in range(2 * images)], axis=0)
        g = mm(s_ref[...], d).astype(BF)
        for o in range(owners):
            low_ref[o ^ me, dh] = g[o * rows : (o + 1) * rows, :quarter]
            high_ref[o ^ me, dh] = g[o * rows : (o + 1) * rows, quarter:]


def run_kernel_grad(place, a0, a1, d0, d1, owners, side, name):
    images, px, ch = a0.shape
    half = d0.shape[2]
    out = shape_of((owners, 3, 3 * ch // owners, half // 2), BF)
    return pl.pallas_call(
        functools.partial(kernel_grad_body, side=side),
        name=name,
        in_specs=[SMEM] + [VMEM] * 4,
        out_specs=[VMEM] * 2,
        out_shape=[out, out],
        scratch_shapes=[
            pltpu.VMEM((3 * ch, 2 * images * px), BF),
            pltpu.VMEM((2 * images, px + 2 * side, half), BF),
        ],
        compiler_params=pltpu.CompilerParams(vmem_limit_bytes=40 << 20),
    )(place, a0, a1, d0, d1)


def codes_body(place_ref, ids_ref, dead_ref, replace_ref, latents_ref, counts_ref, slots_ref, keep_ref, send_ref):
    core = place_ref[0]
    me = place_ref[1]
    offset = place_ref[2]
    codes = dead_ref.shape[1]
    pixels, width = latents_ref.shape
    one = jnp.ones((), BF)
    none = jnp.zeros((), BF)
    code = lax.broadcasted_iota(jnp.int32, (codes, pixels), 0)
    hit = jnp.where(code == ids_ref[...], one, none)
    counts_ref[...] = mm(jnp.ones((8, pixels), BF), hit, NT)
    dead = dead_ref[...]
    ahead = lax.broadcasted_iota(jnp.int32, (codes, codes), 0) <= lax.broadcasted_iota(jnp.int32, (codes, codes), 1)
    rank = mm(jnp.broadcast_to(dead.astype(F32), (8, codes)).astype(BF), jnp.where(ahead, one, none))[0:1]
    rank = jnp.where(dead == 1, rank.astype(jnp.int32) - 1, -1)
    owners, count, _ = keep_ref.shape
    at = lax.broadcasted_iota(jnp.int32, (DEAD, codes), 0)
    chip_at = (at % (owners * count)) // count
    at = ((at // (owners * count)) ^ core) * (owners * count) + (chip_at ^ me) * count + at % count
    slot = at == rank
    slots_ref[...] = jnp.where(slot, one, none)
    wanted = jnp.sum(jnp.where(slot, replace_ref[...], 0), axis=1, keepdims=True) - offset
    pixel = lax.broadcasted_iota(jnp.int32, (DEAD, pixels), 1)
    rows = mm(jnp.where(pixel == wanted, one, none), latents_ref[...]).astype(BF)
    for j in range(owners):
        keep_ref[j] = rows[j * count : (j + 1) * count]
        send_ref[j] = rows[DEAD // 2 + j * count : DEAD // 2 + (j + 1) * count]


def run_codes(place, ids, dead, replace, latents, owners):
    codes = dead.shape[1]
    width = latents.shape[1]
    rows = shape_of((owners, DEAD // (2 * owners), width), BF)
    return pl.pallas_call(
        codes_body,
        name="codes",
        in_specs=[SMEM] + [VMEM] * 4,
        out_specs=[VMEM] * 4,
        out_shape=[shape_of((8, codes), F32), shape_of((DEAD, codes), BF), rows, rows],
        compiler_params=pltpu.CompilerParams(vmem_limit_bytes=40 << 20),
    )(place, ids, dead, replace, latents)


def codebook_body(place_ref, mine_low, mine_high, other_low, other_high, slots_ref, book_ref, out_ref, rows_ref):
    device = place_ref[3]
    owners, count, quarter = mine_low.shape
    entries, width = book_ref.shape
    rows_ref[:, width:] = jnp.ones((DEAD, 128), F32)
    for side, (low, high) in enumerate(((mine_low, mine_high), (other_low, other_high))):
        for j in range(owners):
            start = (side * owners + j) * count
            at = slice(start, start + count)
            rows_ref[at, :quarter] = low[j].astype(F32)
            rows_ref[at, quarter:width] = high[j].astype(F32)
    whole = mm(slots_ref[...], rows_ref[...].astype(BF), TN)
    rows_out = whole.shape[0]
    pick = lax.broadcasted_iota(jnp.int32, (entries, rows_out), 1) - device * entries
    pick = jnp.where(pick == lax.broadcasted_iota(jnp.int32, (entries, rows_out), 0), 1.0, 0.0).astype(BF)
    own = mm(pick, whole.astype(BF))
    out_ref[...] = jnp.where(own[:, width : width + 1] > 0.5, own[:, :width], book_ref[...])


def run_codebook(place, mine, other, slots, book):
    entries, width = book.shape
    return pl.pallas_call(
        codebook_body,
        name="codebook",
        in_specs=[SMEM] + [VMEM] * 6,
        out_specs=VMEM,
        out_shape=shape_of(book.shape, F32),
        scratch_shapes=[pltpu.VMEM((DEAD, width + 128), F32)],
        compiler_params=pltpu.CompilerParams(vmem_limit_bytes=40 << 20),
    )(place, *mine, *other, slots, book)


def spread_body(place_ref, mine_low, mine_high, other_low, other_high, *outs):
    core = place_ref[0]
    count = len(outs)
    mine = jnp.concatenate([mine_low[0], mine_high[0]], axis=1).astype(F32)
    other = jnp.concatenate([other_low[0], other_high[0]], axis=1).astype(F32)
    both = jnp.concatenate([jnp.where(core == 0, mine, other), jnp.where(core == 0, other, mine)], axis=1)
    if count == 1:
        outs[0][...] = both.reshape(outs[0].shape)
    else:
        rows = both.shape[0] // count
        for i, out in enumerate(outs):
            out[0] = both[i * rows : (i + 1) * rows]


def run_spread(place, mine, other, outs, name):
    owners, rows, quarter = mine[0].shape
    block = pl.BlockSpec((1, rows, quarter), lambda j, p: (j, 0, 0))
    if len(outs[0]) == 4:
        pieces, _, each, ch = outs[0]
        specs = [pl.BlockSpec((pieces, 1, each, ch), lambda j, p: (0, j ^ p[1], 0, 0))]
    else:
        specs = [pl.BlockSpec((1,) + s[1:], lambda j, p: (j ^ p[1], 0, 0)) for s in outs]
    return pl.pallas_call(
        spread_body,
        name=name,
        grid_spec=pltpu.PrefetchScalarGridSpec(
            num_scalar_prefetch=1, grid=(owners,), in_specs=[block] * 4, out_specs=specs
        ),
        out_shape=[shape_of(s, F32) for s in outs],
        compiler_params=pltpu.CompilerParams(vmem_limit_bytes=32 << 20),
    )(place, *mine, *other)


def vectors_body(sums_ref, *outs):
    *vectors, usage_ref, perplexity_ref = outs
    for i, out in enumerate(vectors):
        out[...] = sums_ref[i : i + 1, :]
    codes = usage_ref.shape[1]
    width = sums_ref.shape[1]
    first = len(vectors)
    counts = jnp.concatenate([sums_ref[first + i : first + i + 1, :] for i in range(codes // width)], axis=1)
    usage_ref[...] = counts.astype(jnp.int32)
    share = counts / jnp.sum(counts, axis=1, keepdims=True)
    entropy = jnp.sum(share * jnp.log(share + 1e-10), axis=1, keepdims=True)
    perplexity_ref[...] = jnp.exp(-entropy)


def run_vectors(sums, vectors, codes):
    ch = sums.shape[1]
    return pl.pallas_call(
        vectors_body,
        name="vectors",
        in_specs=[VMEM],
        out_specs=[VMEM] * (vectors + 2),
        out_shape=[shape_of((1, ch), F32)] * vectors + [shape_of((1, codes), jnp.int32), shape_of((1, 1), F32)],
    )(sums)


class Links:
    def __init__(self, chips):
        self.chips = chips
        bits = chips.bit_length() - 1
        low = max(1, bits // 2 - 1) if bits > 1 else bits
        if bits % 3 == 0:
            sizes = [bits // 3] * 3
        elif bits == 4:
            sizes = [1, 1, 2]
        else:
            sizes = [low, bits - 2 * low, low]
        self.dims = []
        shift = 0
        for size in sizes:
            self.dims.append((shift, 1 << size))
            shift += size
        self.lead = tuple(n for _, n in reversed(self.dims))

    def axis(self, dim):
        return len(self.dims) - 1 - dim

    def send(self, value, key):
        pairs = [(g * 2 + c, (g ^ key) * 2 + c) for g in range(self.chips) for c in range(2)]
        return lax.ppermute(value, AXES, pairs)

    def partner(self, value):
        pairs = [(g * 2 + c, g * 2 + 1 - c) for g in range(self.chips) for c in range(2)]
        return lax.ppermute(value, AXES, pairs)

    def reduce(self, value, dim):
        shift, n = self.dims[dim]
        ax = self.axis(dim)
        got = [self.send(lax.index_in_dim(value, k, ax), k << shift) for k in range(1, n)]
        total = lax.index_in_dim(value, 0, ax).astype(F32)
        for g in got:
            total = total + g.astype(F32)
        return total.astype(BF)

    def gather(self, value, dim):
        shift, n = self.dims[dim]
        return jnp.concatenate([value] + [self.send(value, k << shift) for k in range(1, n)], axis=self.axis(dim))

    def all_reduce(self, low, high):
        shape = low.shape
        rows = shape[1]
        last = range(2, len(self.dims))
        low = low.reshape(self.lead + shape[1:])
        high = high.reshape(self.lead + shape[1:])
        low = self.reduce(low, 0)
        high = self.reduce(high, 1)
        low = self.reduce(low, 1)
        high = self.reduce(high, 0)
        both = jnp.concatenate([low, high], axis=-2)
        for dim in last:
            both = self.reduce(both, dim)
        for dim in reversed(last):
            both = self.gather(both, dim)
        low, high = both[..., :rows, :], both[..., rows:, :]
        low = self.gather(low, 1)
        high = self.gather(high, 0)
        low = self.gather(low, 0)
        high = self.gather(high, 1)
        return low.reshape(shape), high.reshape(shape)

    def small_all_reduce(self, value):
        value = value + self.partner(value)
        key = 1
        while key < self.chips:
            value = value + self.send(value, key)
            key *= 2
        return value


def local(
    image_rows, grad_out, code_ids, dead_flags, replace_ids, latents, codebook,
    norm1_gain, norm1_bias, conv1_kernel, conv1_bias, norm2_gain, norm2_bias, conv2_kernel, conv2_bias,
    norm3_gain, norm3_bias, query_weight, query_bias, key_weight, value_weight, value_bias, out_weight, out_bias,
    *, chips,
):
    links = Links(chips)
    owners = chips
    all_images, part_rows, side, ch = image_rows.shape
    images = all_images // 2
    px = grad_out.shape[1] * side
    part = part_rows * side
    core = lax.axis_index("row").astype(jnp.int32)
    chip = lax.axis_index("grp").astype(jnp.int32)
    device = chip * 2 + core
    place = jnp.stack([core, chip, device * latents.shape[0], device])
    mine = image_rows.reshape(all_images, part, ch)
    other = links.partner(lax.dynamic_slice_in_dim(mine, (1 - core) * images, images))
    vec = jnp.stack([
        norm1_gain, norm1_bias, conv1_bias, norm2_gain, norm2_bias, conv2_bias,
        norm3_gain, norm3_bias, query_bias, value_bias, out_bias,
    ]).astype(F32)
    w1 = conv1_kernel.reshape(9 * ch, ch)
    w2 = conv2_kernel.reshape(9 * ch, ch)
    codes = dead_flags.shape[0]
    counts, slots, ckeep, csend = run_codes(
        place, code_ids.reshape(1, -1), dead_flags.reshape(1, -1), replace_ids.reshape(1, -1), latents, owners
    )
    gy = grad_out.reshape(images, px, ch)
    out, act1, act2, filtered, dres, dkeep2, dsend2, stat_a, gkeep, gsend = run_forward(
        place, mine, other, gy, vec, w1, w2, query_weight, key_weight, value_weight, out_weight, owners, side
    )
    dother2 = links.partner(dsend2)
    act2_other = links.partner(act2)
    act1_other = links.partner(act1)
    got = links.partner(jnp.concatenate([gsend.reshape(owners, -1, ch // 2), csend], axis=1))
    kept = jnp.concatenate([gkeep.reshape(owners, -1, ch // 2), ckeep], axis=1)
    attn = (kept.astype(F32) + got.astype(F32)).astype(BF)
    quarter = ch // 4
    attn_rows = 4 * (ch // owners)
    dkeep1, dsend1, dfull1, stat_b = run_back2(place, dres, filtered, vec, w2, side)
    dother1 = links.partner(dsend1)
    low2, high2 = run_kernel_grad(place, act2, act2_other, dkeep2, dother2, owners, side, "conv2_grad")
    conv_rows = low2.shape[1] * low2.shape[2]
    low2 = low2.reshape(owners, conv_rows, quarter)
    high2 = high2.reshape(owners, conv_rows, quarter)
    low_a, high_a = links.all_reduce(
        jnp.concatenate([attn[:, :, :quarter], low2], axis=1), jnp.concatenate([attn[:, :, quarter:], high2], axis=1)
    )
    low1, high1 = run_kernel_grad(place, act1, act1_other, dkeep1, dother1, owners, side, "conv1_grad")
    low_b, high_b = links.all_reduce(
        low1.reshape(owners, conv_rows, quarter), high1.reshape(owners, conv_rows, quarter)
    )
    in_keep, in_send, stat_c = run_back1(place, dfull1, mine, other, dres, vec, w1, side)
    in_got = links.partner(in_send)
    ordered = jnp.where(core == 0, jnp.concatenate([in_keep, in_got]), jnp.concatenate([in_got, in_keep]))
    input_grad = ordered.reshape(image_rows.shape)
    vectors = jnp.concatenate([stat_c[:2], stat_b[2:3], stat_b[:2], stat_a[:6], counts[:1].reshape(-1, ch)])
    vectors = links.small_all_reduce(vectors)
    *vec_grads, usage, perplexity = run_vectors(vectors, 11, codes)
    (g1, b1, cb1, g2, b2, cb2, g3, b3, qb, vb, ob) = [v.reshape(ch) for v in vec_grads]
    low_ao, high_ao = links.partner(low_a), links.partner(high_a)
    each = ch // owners
    ends = (attn_rows, attn_rows + DEAD // (2 * owners))
    groups = (low_a, high_a, low_ao, high_ao)
    a_parts = [t[:, : ends[0]] for t in groups]
    c_parts = [t[:, ends[0] : ends[1]] for t in groups]
    w_parts = [t[:, ends[1] :] for t in groups]
    qg, kg, vg, og = run_spread(place, a_parts[:2], a_parts[2:], [(owners, each, ch)] * 4, "attention_spread")
    conv_shape = (3, owners, 3 * each, ch)
    (grad2,) = run_spread(place, w_parts[:2], w_parts[2:], [conv_shape], "conv2_spread")
    new_codebook = run_codebook(place, c_parts[:2], c_parts[2:], slots, codebook)
    (grad1,) = run_spread(
        place, (low_b, high_b), (links.partner(low_b), links.partner(high_b)), [conv_shape], "conv1_spread"
    )
    kernel_shape = (3, 3, ch, ch)
    qg, kg, vg, og = [t.reshape(ch, ch) for t in (qg, kg, vg, og)]
    return (
        out.reshape(grad_out.shape), input_grad,
        g1, b1, grad1.reshape(kernel_shape), cb1, g2, b2, grad2.reshape(kernel_shape), cb2, g3, b3,
        qg, qb, kg, vg, vb, og, ob,
        new_codebook, usage.reshape(codes), perplexity.reshape(()),
    )


def solution(mesh):
    both = ("grp", "row")
    in_specs = (
        P("grp", "row", None, None), P(both, None, None, None), P(both), P(), P(), P(both, None), P(both, None),
    ) + (P(),) * 17
    out_specs = (P(both, None, None, None), P("grp", "row", None, None)) + (P(),) * 17 + (P(both, None), P(), P())
    body = functools.partial(local, chips=mesh.shape["grp"])
    return jax.shard_map(body, mesh=mesh, in_specs=in_specs, out_specs=out_specs, check_vma=False)
```

time: 565 us -> 293 us (0.52); the launches traced: 557 us -> 291 us
  waiting for transfers between devices: 326 us -> 122 us
  Pallas kernels: 0 us -> 72.7 us
  matrix products: 69.9 us -> 0 us
  starting transfers between devices: 7.2 us -> 53 us
  blocking collectives: 44.6 us -> 0 us
  local copies, waits for them, and re-layouts: 68.6 us -> 32.6 us
  between operations: 17.4 us -> 1.19 us
  other arithmetic: 22.6 us -> 9.41 us
    psum x1 -> x0, waiting for transfers between devices: 326 us -> none  [local(): lax.psum((first_gain_grad, first_offset_grad, conv1_kernel_grad, first_bi...]
    ppermute x0 -> x44, waiting for transfers between devices: none -> 122 us  [the longest x32 121 us: send(): return lax.ppermute(value, AXES, pairs)]
    pallas_call x0 -> x11, Pallas kernels: none -> 72.7 us  [the longest x3 25.3 us: run_spread(): pl.pallas_call(spread_body, name=name, grid_spec=pltpu.PrefetchScalarGrid...]
    dot_general x73 -> x0, matrix products: 69.9 us -> none  [the longest x36 32.7 us: conv_taps(): lax.dot_general(window, kernel[tap_row, tap_col], (((3,), (0,)), ((), ())...]
    ppermute x0 -> x44, starting transfers between devices: none -> 53 us  [the longest x32 50.1 us: send(): return lax.ppermute(value, AXES, pairs)]
    psum x1 -> x0, blocking collectives: 44.6 us -> none  [local(): lax.psum((first_gain_grad, first_offset_grad, conv1_kernel_grad, first_bi...]
    unnamed x98 -> x40, local copies, waits for them, and re-layouts: 41.5 us -> 10.7 us
    reduce_sum x25 -> x0, other arithmetic: 14.3 us -> none  [the longest x3 4.85 us: group_norm(): return normed * scaling + offsets]
  transfers between devices with their start and end apart: 4 -> 44, of which waited for: 2 -> 19; matrix products, arithmetic and copies ran while one was open for 24% -> 8% of each run, Pallas kernels for 0% -> 12%
where the time goes in v1:
time: 293 us; the launch traced here: 291 us
  waiting for transfers between devices  122 us (42%)
  Pallas kernels  72.7 us (25%)
  starting transfers between devices  53 us (18%)
  local copies, waits for them, and re-layouts  32.6 us (11%)
  other arithmetic  9.41 us (3%)
    ppermute x32, waiting for transfers between devices, send(): return lax.ppermute(value, AXES, pairs)  121 us
    ppermute x32, starting transfers between devices, send(): return lax.ppermute(value, AXES, pairs)  50.1 us
    pallas_call x3, Pallas kernels, run_spread(): pl.pallas_call(spread_body, name=name, grid_spec=pltpu.PrefetchScalarGrid...  25.3 us
    pallas_call x1, Pallas kernels, run_forward(): pl.pallas_call(functools.partial(forward_body, side=side), name='forward_...  23.1 us
    unnamed x40, local copies, waits for them, and re-layouts  10.7 us
    pallas_call x2, Pallas kernels, run_kernel_grad(): pl.pallas_call(functools.partial(kernel_grad_body, side=side), name=name,...  8.9 us
    another operation x12, local copies, waits for them, and re-layouts, local(): jnp.stack([norm1_gain, norm1_bias, conv1_bias, norm2_gain, norm2_bias, co...  7.56 us
  transfers between devices with their start and end apart: 44, of which 19 were waited for; matrix products, arithmetic and copies ran while one was open for 8% of the time, Pallas kernels for 12%

profile of v1, /device:TPU:0, one launch (start us, length us, event | category | flops | bytes accessed | tf_op | source)
XLA Modules:
  0.0 291.0 jit_solution(11842213233395839552)
XLA Ops:
  15.4 23.1 %forward_attention.1 = (bf16[2,256,512]{2,1,0:T(8,128)(2,1)}, bf16[2,256,512]{2,1,0:T(8,128)(2,1)S(1)}, bf16[2,256,512]{2,1,0:T(8,128)(2,1)S(1)}, f32[2,256,512]...) custom-call(s32[4]{0:T(128)S(1)} %pad_add_fusion.place_ref, ...), custom_call_target="tpu_custom_call" | custom-call | tf_op jit(solution)/shard_map/forward_attention/pallas_call | solution.py:246
  41.2 5.1 %conv2_back.1 = (bf16[2,256,256]{2,1,0:T(8,128)(2,1)S(1)}, bf16[2,256,256]{2,1,0:T(8,128)(2,1)S(1)}, bf16[2,256,512]{2,1,0:T(8,128)(2,1)S(1)}, f32[8,512]{1,0:T(8,128)S(1)}) custom-call(s32[4]{0:T(128)S(1)} %pad_add_fusion.place_ref, f32[2,256,512]{2,1,0:T(8,128)S(1)} %copy-done.1, f32[2,256,512]{2,1,0:T(8,128)S(1)} %copy-done.5, ...), custom_call_target="tpu_custom_call" | custom-call | tf_op jit(solution)/shard_map/conv2_back/pallas_call | solution.py:312
  46.4 4.5 %conv2_grad.1 = (bf16[16,3,96,128]{3,2,1,0:T(8,128)(2,1)S(1)}, bf16[16,3,96,128]{3,2,1,0:T(8,128)(2,1)S(1)}) custom-call(s32[4]{0:T(128)S(1)} %pad_add_fusion.place_ref, bf16[2,256,512]{2,1,0:T(8,128)(2,1)S(1)} %get-tuple-element.88.a0_ref, bf16[2,256,512]{2,1,0:T(8,128)(2,1)S(1)} %collective-permute-done.26.a1_ref, ...), custom_call_target="tpu_custom_call" | custom-call | tf_op jit(solution)/shard_map/conv2_grad/pallas_call | solution.py:420
  51.6 3.0 %collective-permute-start.28 = (bf16[4,2,1,424,128]{4,3,2,1,0:T(8,128)(2,1)S(1)}, bf16[4,2,1,424,128]{4,3,2,1,0:T(8,128)(2,1)S(1)}, u32[]{:S(2)}, u32[]{:S(2)}) collective-permute-start(bf16[4,2,1,424,128]{4,3,2,1,0:T(8,128)(2,1)S(1)} %pad_maximum_fusion.6), channel_id=1, source_target_pairs={{0,2},{1,3},{2,0},{3,1},{4,6},{5,7},{6,4},{7,5},{8,10},{9,11},{10,... | collective-permute-start | bytes 2605064 | tf_op jit(solution)/shard_map/ppermute | solution.py:590
  54.6 4.4 %conv1_grad.1 = (bf16[16,3,96,128]{3,2,1,0:T(8,128)(2,1)S(1)}, bf16[16,3,96,128]{3,2,1,0:T(8,128)(2,1)S(1)}) custom-call(s32[4]{0:T(128)S(1)} %pad_add_fusion.place_ref, bf16[2,256,512]{2,1,0:T(8,128)(2,1)S(1)} %get-tuple-element.76.a0_ref, bf16[2,256,512]{2,1,0:T(8,128)(2,1)S(1)} %collective-permute-done.7.a1_ref, ...), custom_call_target="tpu_custom_call" | custom-call | tf_op jit(solution)/shard_map/conv1_grad/pallas_call | solution.py:420
  59.1 2.1 collective-permute-start.30
  61.4 25.4 %collective-permute-done.9 = bf16[4,2,1,288,128]{4,3,2,1,0:T(8,128)(2,1)S(1)} collective-permute-done((bf16[4,2,1,288,128]{4,3,2,1,0:T(8,128)(2,1)S(1)}, bf16[4,2,1,288,128]{4,3,2,1,0:T(8,128)(2,1)S(1)}, u32[]{:S(2)}, u32[]{:S(2)}) %collective-permute-start.9) | collective-permute-done | bytes 589856 | tf_op jit(solution)/shard_map/ppermute | solution.py:590
  91.5 2.6 collective-permute-done.11
  94.2 2.1 collective-permute-start.12
  96.3 12.2 %collective-permute-done.29 = bf16[4,1,1,424,128]{4,3,2,1,0:T(8,128)(2,1)S(1)} collective-permute-done((bf16[4,1,1,424,128]{4,3,2,1,0:T(8,128)(2,1)S(1)}, bf16[4,1,1,424,128]{4,3,2,1,0:T(8,128)(2,1)S(1)}, u32[]{:S(2)}, u32[]{:S(2)}) %collective-permute-start.29) | collective-permute-done | bytes 434208 | tf_op jit(solution)/shard_map/ppermute | solution.py:590
  110.7 2.5 collective-permute-start.34
  113.3 3.1 %collective-permute-done.32 = bf16[1,1,1,848,128]{4,3,2,1,0:T(8,128)(2,1)S(1)} collective-permute-done((bf16[1,1,1,848,128]{4,3,2,1,0:T(8,128)(2,1)S(1)}, bf16[1,1,1,848,128]{4,3,2,1,0:T(8,128)(2,1)S(1)}, u32[]{:S(2)}, u32[]{:S(2)}) %collective-permute-start.32) | collective-permute-done | bytes 217120 | tf_op jit(solution)/shard_map/ppermute | solution.py:590
  116.5 7.5 %collective-permute-done.34 = bf16[1,1,1,848,128]{4,3,2,1,0:T(8,128)(2,1)S(1)} collective-permute-done((bf16[1,1,1,848,128]{4,3,2,1,0:T(8,128)(2,1)S(1)}, bf16[1,1,1,848,128]{4,3,2,1,0:T(8,128)(2,1)S(1)}, u32[]{:S(2)}, u32[]{:S(2)}) %collective-permute-start.34) | collective-permute-done | bytes 217120 | tf_op jit(solution)/shard_map/ppermute | solution.py:590
  123.9 7.1 %collective-permute-done.33 = bf16[1,1,1,848,128]{4,3,2,1,0:T(8,128)(2,1)S(1)} collective-permute-done((bf16[1,1,1,848,128]{4,3,2,1,0:T(8,128)(2,1)S(1)}, bf16[1,1,1,848,128]{4,3,2,1,0:T(8,128)(2,1)S(1)}, u32[]{:S(2)}, u32[]{:S(2)}) %collective-permute-start.33) | collective-permute-done | bytes 217120 | tf_op jit(solution)/shard_map/ppermute | solution.py:590
  131.2 3.7 %collective-permute-start.37 = (bf16[1,1,1,848,128]{4,3,2,1,0:T(8,128)(2,1)S(1)}, bf16[1,1,1,848,128]{4,3,2,1,0:T(8,128)(2,1)S(1)}, u32[]{:S(2)}, u32[]{:S(2)}) collective-permute-start(bf16[1,1,1,848,128]{4,3,2,1,0:T(8,128)(2,1)S(1)} %add_convert_fusion.9), channel_id=1, source_target_pairs={{0,24},{1,25},{2,26},{3,27},{4,28},{5,29},{6,30},{7,31},{8,16},{9,... | collective-permute-start | bytes 651272 | tf_op jit(solution)/shard_map/ppermute | solution.py:590
  137.1 2.4 collective-permute-start.15
  141.3 7.8 %collective-permute-start.14 = (bf16[1,1,1,576,128]{4,3,2,1,0:T(8,128)(2,1)S(1)}, bf16[1,1,1,576,128]{4,3,2,1,0:T(8,128)(2,1)S(1)}, u32[]{:S(2)}, u32[]{:S(2)}) collective-permute-start(bf16[1,1,1,576,128]{4,3,2,1,0:T(8,128)(2,1)S(1)} %get-tuple-element.117), channel_id=1, source_target_pairs={{0,16},{1,17},{2,18},{3,19},{4,20},{5,21},{6,22},{7,23},{8,24},{9,... | collective-permute-start | bytes 442376 | tf_op jit(solution)/shard_map/ppermute | solution.py:590
  149.1 9.0 %collective-permute-done.36 = bf16[1,1,1,848,128]{4,3,2,1,0:T(8,128)(2,1)S(1)} collective-permute-done((bf16[1,1,1,848,128]{4,3,2,1,0:T(8,128)(2,1)S(1)}, bf16[1,1,1,848,128]{4,3,2,1,0:T(8,128)(2,1)S(1)}, u32[]{:S(2)}, u32[]{:S(2)}) %collective-permute-start.36) | collective-permute-done | bytes 217120 | tf_op jit(solution)/shard_map/ppermute | solution.py:590
  163.2 2.6 collective-permute-start.18
  167.7 3.9 %collective-permute-done.18 = bf16[1,1,1,576,128]{4,3,2,1,0:T(8,128)(2,1)S(1)} collective-permute-done((bf16[1,1,1,576,128]{4,3,2,1,0:T(8,128)(2,1)S(1)}, bf16[1,1,1,576,128]{4,3,2,1,0:T(8,128)(2,1)S(1)}, u32[]{:S(2)}, u32[]{:S(2)}) %collective-permute-start.18) | collective-permute-done | bytes 147488 | tf_op jit(solution)/shard_map/ppermute | solution.py:590
  171.6 4.7 %collective-permute-done.17 = bf16[1,1,1,576,128]{4,3,2,1,0:T(8,128)(2,1)S(1)} collective-permute-done((bf16[1,1,1,576,128]{4,3,2,1,0:T(8,128)(2,1)S(1)}, bf16[1,1,1,576,128]{4,3,2,1,0:T(8,128)(2,1)S(1)}, u32[]{:S(2)}, u32[]{:S(2)}) %collective-permute-start.17) | collective-permute-done | bytes 147488 | tf_op jit(solution)/shard_map/ppermute | solution.py:590
  180.8 22.8 %collective-permute-done.19 = bf16[4,1,1,288,128]{4,3,2,1,0:T(8,128)(2,1)S(1)} collective-permute-done((bf16[4,1,1,288,128]{4,3,2,1,0:T(8,128)(2,1)S(1)}, bf16[4,1,1,288,128]{4,3,2,1,0:T(8,128)(2,1)S(1)}, u32[]{:S(2)}, u32[]{:S(2)}) %collective-permute-start.19) | collective-permute-done | bytes 294944 | tf_op jit(solution)/shard_map/ppermute | solution.py:590
  209.1 6.8 %collective-permute-done.20 = bf16[4,2,1,288,128]{4,3,2,1,0:T(8,128)(2,1)S(1)} collective-permute-done((bf16[4,2,1,288,128]{4,3,2,1,0:T(8,128)(2,1)S(1)}, bf16[4,2,1,288,128]{4,3,2,1,0:T(8,128)(2,1)S(1)}, u32[]{:S(2)}, u32[]{:S(2)}) %collective-permute-start.20) | collective-permute-done | bytes 589856 | tf_op jit(solution)/shard_map/ppermute | solution.py:590
  216.9 2.3 copy-done
  222.3 5.3 %conv1_back.1 = (bf16[2,128,512]{2,1,0:T(8,128)(2,1)S(1)}, bf16[2,128,512]{2,1,0:T(8,128)(2,1)S(1)}, f32[8,512]{1,0:T(8,128)S(1)}) custom-call(s32[4]{0:T(128)S(1)} %pad_add_fusion.place_ref, bf16[2,256,512]{2,1,0:T(8,128)(2,1)S(1)} %copy-done.7, bf16[4,128,512]{2,1,0:T(8,128)(2,1)S(1)} %bitcast.62, bf16[2,128,512]{2,1,0:T(8,128)(2,1)S(1)} %copy-done.4, ...), custom_call_target="tpu_custom_call" | custom-call | tf_op jit(solution)/shard_map/conv1_back/pallas_call | solution.py:371
  231.7 2.6 collective-permute-done.3
  235.8 2.4 collective-permute-done.4
  238.2 3.9 %collective-permute-done.5 = f32[13,512]{1,0:T(8,128)S(1)} collective-permute-done((f32[13,512]{1,0:T(8,128)S(1)}, f32[13,512]{1,0:T(8,128)S(1)}, u32[]{:S(2)}, u32[]{:S(2)}) %collective-permute-start.5) | collective-permute-done | bytes 26656 | tf_op jit(solution)/shard_map/ppermute | solution.py:590
  243.5 3.4 %collective-permute-done.6 = f32[13,512]{1,0:T(8,128)S(1)} collective-permute-done((f32[13,512]{1,0:T(8,128)S(1)}, f32[13,512]{1,0:T(8,128)S(1)}, u32[]{:S(2)}, u32[]{:S(2)}) %collective-permute-start.6) | collective-permute-done | bytes 26656 | tf_op jit(solution)/shard_map/ppermute | solution.py:590
  251.0 11.3 %conv1_spread.1 = f32[3,16,96,512]{3,2,1,0:T(8,128)} custom-call(s32[4]{0:T(128)S(1)} %pad_add_fusion.place_ref, bf16[16,288,128]{2,1,0:T(8,128)(2,1)S(1)} %bitcast.57, bf16[16,288,128]{2,1,0:T(8,128)(2,1)S(1)} %bitcast.59, bf16[16,288,128]{2,1,0:T(8,128)(2,1)} %collective-permute-done.23.other_low, bf16[16,288,128]{2,1,0:T(8,128)(2,1)} %collective-permute-done.24.other_high), custom_call_target="tpu_custom_call" | custom-call | tf_op jit(solution)/shard_map/conv1_spread/pallas_call | solution.py:531
  270.9 6.4 %attention_spread.1 = (f32[16,32,512]{2,1,0:T(8,128)}, f32[16,32,512]{2,1,0:T(8,128)}, f32[16,32,512]{2,1,0:T(8,128)}, f32[16,32,512]{2,1,0:T(8,128)}) custom-call(s32[4]{0:T(128)S(1)} %pad_add_fusion.place_ref, bf16[16,128,128]{2,1,0:T(8,128)(2,1)S(1)} %slice.226.mine_low, bf16[16,128,128]{2,1,0:T(8,128)(2,1)S(1)} %slice.227.mine_high, ...), custom_call_target="tpu_custom_call" | custom-call | tf_op jit(solution)/shard_map/attention_spread/pallas_call | solution.py:531
  280.0 7.6 %conv2_spread.1 = f32[3,16,96,512]{3,2,1,0:T(8,128)} custom-call(s32[4]{0:T(128)S(1)} %pad_add_fusion.place_ref, bf16[16,288,128]{2,1,0:T(8,128)(2,1)S(1)} %slice.221.mine_low, bf16[16,288,128]{2,1,0:T(8,128)(2,1)S(1)} %slice.223.mine_high, bf16[16,288,128]{2,1,0:T(8,128)(2,1)S(1)} %slice.224.other_low, bf16[16,288,128]{2,1,0:T(8,128)(2,1)S(1)} %slice.225.other_high), custom_call_target="tpu_custom_call" | custom-call | tf_op jit(solution)/shard_map/conv2_spread/pallas_call | solution.py:531
  (182 shorter events, 76.3 us)
Async XLA Ops:
  1.6 13.8 %collective-permute-start = (bf16[2,128,512]{2,1,0:T(8,128)(2,1)S(1)}, bf16[2,128,512]{2,1,0:T(8,128)(2,1)S(1)}, u32[]{:S(2)}, u32[]{:S(2)}) collective-permute-start(bf16[2,128,512]{2,1,0:T(8,128)(2,1)S(1)} %constant_dynamic-slice_fusion), channel_id=1, source_target_pairs={{0,1},{1,0},{2,3},{3,2},{4,5},{5,4},{6,7},{7,6},{8,9},{9,8},{10,11... | collective-permute-start | bytes 786440 | tf_op jit(solution)/shard_map/ppermute | solution.py:594
  40.1 10.9 %collective-permute-start.25 = (bf16[16,136,256]{2,1,0:T(8,128)(2,1)S(1)}, bf16[16,136,256]{2,1,0:T(8,128)(2,1)S(1)}, u32[]{:S(2)}, u32[]{:S(2)}) collective-permute-start(bf16[16,136,256]{2,1,0:T(8,128)(2,1)S(1)} %pad_maximum_fusion.4), channel_id=1, source_target_pairs={{0,1},{1,0},{2,3},{3,2},{4,5},{5,4},{6,7},{7,6},{8,9},{9,8},{10,11... | collective-permute-start | bytes 3342344 | tf_op jit(solution)/shard_map/ppermute | solution.py:594
  40.7 13.9 %collective-permute-start.7 = (bf16[2,256,512]{2,1,0:T(8,128)(2,1)S(1)}, bf16[2,256,512]{2,1,0:T(8,128)(2,1)S(1)}, u32[]{:S(2)}, u32[]{:S(2)}) collective-permute-start(bf16[2,256,512]{2,1,0:T(8,128)(2,1)S(1)} %get-tuple-element.76.a0_ref), channel_id=1, source_target_pairs={{0,1},{1,0},{2,3},{3,2},{4,5},{5,4},{6,7},{7,6},{8,9},{9,8},{10,11... | collective-permute-start | bytes 1572872 | tf_op jit(solution)/shard_map/ppermute | solution.py:594
  51.6 37.2 %collective-permute-start.28 = (bf16[4,2,1,424,128]{4,3,2,1,0:T(8,128)(2,1)S(1)}, bf16[4,2,1,424,128]{4,3,2,1,0:T(8,128)(2,1)S(1)}, u32[]{:S(2)}, u32[]{:S(2)}) collective-permute-start(bf16[4,2,1,424,128]{4,3,2,1,0:T(8,128)(2,1)S(1)} %pad_maximum_fusion.6), channel_id=1, source_target_pairs={{0,2},{1,3},{2,0},{3,1},{4,6},{5,7},{6,4},{7,5},{8,10},{9,11},{10,... | collective-permute-start | bytes 2605064 | tf_op jit(solution)/shard_map/ppermute | solution.py:590
  59.0 27.8 %collective-permute-start.9 = (bf16[4,2,1,288,128]{4,3,2,1,0:T(8,128)(2,1)S(1)}, bf16[4,2,1,288,128]{4,3,2,1,0:T(8,128)(2,1)S(1)}, u32[]{:S(2)}, u32[]{:S(2)}) collective-permute-start(bf16[4,2,1,288,128]{4,3,2,1,0:T(8,128)(2,1)S(1)} %slice.189), channel_id=1, source_target_pairs={{0,2},{1,3},{2,0},{3,1},{4,6},{5,7},{6,4},{7,5},{8,10},{9,11},{10,... | collective-permute-start | bytes 1769480 | tf_op jit(solution)/shard_map/ppermute | solution.py:590
  59.1 30.2 %collective-permute-start.30 = (bf16[4,1,2,424,128]{4,3,2,1,0:T(8,128)(2,1)S(1)}, bf16[4,1,2,424,128]{4,3,2,1,0:T(8,128)(2,1)S(1)}, u32[]{:S(2)}, u32[]{:S(2)}) collective-permute-start(bf16[4,1,2,424,128]{4,3,2,1,0:T(8,128)(2,1)S(1)} %pad_maximum_fusion.5), channel_id=1, source_target_pairs={{0,4},{1,5},{2,6},{3,7},{4,0},{5,1},{6,2},{7,3},{8,12},{9,13},{10,... | collective-permute-start | bytes 2605064 | tf_op jit(solution)/shard_map/ppermute | solution.py:590
  61.3 32.8 %collective-permute-start.11 = (bf16[4,1,2,288,128]{4,3,2,1,0:T(8,128)(2,1)S(1)}, bf16[4,1,2,288,128]{4,3,2,1,0:T(8,128)(2,1)S(1)}, u32[]{:S(2)}, u32[]{:S(2)}) collective-permute-start(bf16[4,1,2,288,128]{4,3,2,1,0:T(8,128)(2,1)S(1)} %slice.193), channel_id=1, source_target_pairs={{0,4},{1,5},{2,6},{3,7},{4,0},{5,1},{6,2},{7,3},{8,12},{9,13},{10,... | collective-permute-start | bytes 1769480 | tf_op jit(solution)/shard_map/ppermute | solution.py:590
  86.9 26.3 %collective-permute-start.10 = (bf16[4,1,1,288,128]{4,3,2,1,0:T(8,128)(2,1)S(1)}, bf16[4,1,1,288,128]{4,3,2,1,0:T(8,128)(2,1)S(1)}, u32[]{:S(2)}, u32[]{:S(2)}) collective-permute-start(bf16[4,1,1,288,128]{4,3,2,1,0:T(8,128)(2,1)S(1)} %slice.191), channel_id=1, source_target_pairs={{0,4},{1,5},{2,6},{3,7},{4,0},{5,1},{6,2},{7,3},{8,12},{9,13},{10,... | collective-permute-start | bytes 884744 | tf_op jit(solution)/shard_map/ppermute | solution.py:590
  89.1 19.4 %collective-permute-start.29 = (bf16[4,1,1,424,128]{4,3,2,1,0:T(8,128)(2,1)S(1)}, bf16[4,1,1,424,128]{4,3,2,1,0:T(8,128)(2,1)S(1)}, u32[]{:S(2)}, u32[]{:S(2)}) collective-permute-start(bf16[4,1,1,424,128]{4,3,2,1,0:T(8,128)(2,1)S(1)} %slice.208), channel_id=1, source_target_pairs={{0,4},{1,5},{2,6},{3,7},{4,0},{5,1},{6,2},{7,3},{8,12},{9,13},{10,... | collective-permute-start | bytes 1302536 | tf_op jit(solution)/shard_map/ppermute | solution.py:590
  89.6 19.0 %collective-permute-start.31 = (bf16[4,1,1,424,128]{4,3,2,1,0:T(8,128)(2,1)S(1)}, bf16[4,1,1,424,128]{4,3,2,1,0:T(8,128)(2,1)S(1)}, u32[]{:S(2)}, u32[]{:S(2)}) collective-permute-start(bf16[4,1,1,424,128]{4,3,2,1,0:T(8,128)(2,1)S(1)} %slice.213), channel_id=1, source_target_pairs={{0,2},{1,3},{2,0},{3,1},{4,6},{5,7},{6,4},{7,5},{8,10},{9,11},{10,... | collective-permute-start | bytes 1302536 | tf_op jit(solution)/shard_map/ppermute | solution.py:590
  94.2 41.4 %collective-permute-start.12 = (bf16[4,1,1,288,128]{4,3,2,1,0:T(8,128)(2,1)S(1)}, bf16[4,1,1,288,128]{4,3,2,1,0:T(8,128)(2,1)S(1)}, u32[]{:S(2)}, u32[]{:S(2)}) collective-permute-start(bf16[4,1,1,288,128]{4,3,2,1,0:T(8,128)(2,1)S(1)} %slice.195), channel_id=1, source_target_pairs={{0,2},{1,3},{2,0},{3,1},{4,6},{5,7},{6,4},{7,5},{8,10},{9,11},{10,... | collective-permute-start | bytes 884744 | tf_op jit(solution)/shard_map/ppermute | solution.py:590
  110.7 13.3 %collective-permute-start.34 = (bf16[1,1,1,848,128]{4,3,2,1,0:T(8,128)(2,1)S(1)}, bf16[1,1,1,848,128]{4,3,2,1,0:T(8,128)(2,1)S(1)}, u32[]{:S(2)}, u32[]{:S(2)}) collective-permute-start(bf16[1,1,1,848,128]{4,3,2,1,0:T(8,128)(2,1)S(1)} %get-tuple-element.111), channel_id=1, source_target_pairs={{0,24},{1,25},{2,26},{3,27},{4,28},{5,29},{6,30},{7,31},{8,16},{9,... | collective-permute-start | bytes 651272 | tf_op jit(solution)/shard_map/ppermute | solution.py:590
  113.1 17.9 %collective-permute-start.33 = (bf16[1,1,1,848,128]{4,3,2,1,0:T(8,128)(2,1)S(1)}, bf16[1,1,1,848,128]{4,3,2,1,0:T(8,128)(2,1)S(1)}, u32[]{:S(2)}, u32[]{:S(2)}) collective-permute-start(bf16[1,1,1,848,128]{4,3,2,1,0:T(8,128)(2,1)S(1)} %get-tuple-element.112), channel_id=1, source_target_pairs={{0,16},{1,17},{2,18},{3,19},{4,20},{5,21},{6,22},{7,23},{8,24},{9,... | collective-permute-start | bytes 651272 | tf_op jit(solution)/shard_map/ppermute | solution.py:590
  134.9 23.3 %collective-permute-start.36 = (bf16[1,1,1,848,128]{4,3,2,1,0:T(8,128)(2,1)S(1)}, bf16[1,1,1,848,128]{4,3,2,1,0:T(8,128)(2,1)S(1)}, u32[]{:S(2)}, u32[]{:S(2)}) collective-permute-start(bf16[1,1,1,848,128]{4,3,2,1,0:T(8,128)(2,1)S(1)} %add_convert_fusion.9), channel_id=1, source_target_pairs={{0,16},{1,17},{2,18},{3,19},{4,20},{5,21},{6,22},{7,23},{8,24},{9,... | collective-permute-start | bytes 651272 | tf_op jit(solution)/shard_map/ppermute | solution.py:590
  134.9 23.3 %collective-permute-start.35 = (bf16[1,1,1,848,128]{4,3,2,1,0:T(8,128)(2,1)S(1)}, bf16[1,1,1,848,128]{4,3,2,1,0:T(8,128)(2,1)S(1)}, u32[]{:S(2)}, u32[]{:S(2)}) collective-permute-start(bf16[1,1,1,848,128]{4,3,2,1,0:T(8,128)(2,1)S(1)} %add_convert_fusion.9), channel_id=1, source_target_pairs={{0,8},{1,9},{2,10},{3,11},{4,12},{5,13},{6,14},{7,15},{8,0},{9,1},... | collective-permute-start | bytes 651272 | tf_op jit(solution)/shard_map/ppermute | solution.py:590
  135.7 25.7 %collective-permute-start.13 = (bf16[1,1,1,576,128]{4,3,2,1,0:T(8,128)(2,1)S(1)}, bf16[1,1,1,576,128]{4,3,2,1,0:T(8,128)(2,1)S(1)}, u32[]{:S(2)}, u32[]{:S(2)}) collective-permute-start(bf16[1,1,1,576,128]{4,3,2,1,0:T(8,128)(2,1)S(1)} %get-tuple-element.115), channel_id=1, source_target_pairs={{0,8},{1,9},{2,10},{3,11},{4,12},{5,13},{6,14},{7,15},{8,0},{9,1},... | collective-permute-start | bytes 442376 | tf_op jit(solution)/shard_map/ppermute | solution.py:590
  137.1 24.3 %collective-permute-start.15 = (bf16[1,1,1,576,128]{4,3,2,1,0:T(8,128)(2,1)S(1)}, bf16[1,1,1,576,128]{4,3,2,1,0:T(8,128)(2,1)S(1)}, u32[]{:S(2)}, u32[]{:S(2)}) collective-permute-start(bf16[1,1,1,576,128]{4,3,2,1,0:T(8,128)(2,1)S(1)} %get-tuple-element.116), channel_id=1, source_target_pairs={{0,24},{1,25},{2,26},{3,27},{4,28},{5,29},{6,30},{7,31},{8,16},{9,... | collective-permute-start | bytes 442376 | tf_op jit(solution)/shard_map/ppermute | solution.py:590
  141.3 21.9 %collective-permute-start.14 = (bf16[1,1,1,576,128]{4,3,2,1,0:T(8,128)(2,1)S(1)}, bf16[1,1,1,576,128]{4,3,2,1,0:T(8,128)(2,1)S(1)}, u32[]{:S(2)}, u32[]{:S(2)}) collective-permute-start(bf16[1,1,1,576,128]{4,3,2,1,0:T(8,128)(2,1)S(1)} %get-tuple-element.117), channel_id=1, source_target_pairs={{0,16},{1,17},{2,18},{3,19},{4,20},{5,21},{6,22},{7,23},{8,24},{9,... | collective-permute-start | bytes 442376 | tf_op jit(solution)/shard_map/ppermute | solution.py:590
  158.3 19.6 %collective-permute-start.40 = (bf16[4,1,1,424,128]{4,3,2,1,0:T(8,128)(2,1)S(1)}, bf16[4,1,1,424,128]{4,3,2,1,0:T(8,128)(2,1)S(1)}, u32[]{:S(2)}, u32[]{:S(2)}) collective-permute-start(bf16[4,1,1,424,128]{4,3,2,1,0:T(8,128)(2,1)S(1)} %get-tuple-element.108), channel_id=1, source_target_pairs={{0,2},{1,3},{2,0},{3,1},{4,6},{5,7},{6,4},{7,5},{8,10},{9,11},{10,... | collective-permute-start | bytes 1302536 | tf_op jit(solution)/shard_map/ppermute | solution.py:590
  159.9 16.5 %collective-permute-start.38 = (bf16[4,1,1,424,128]{4,3,2,1,0:T(8,128)(2,1)S(1)}, bf16[4,1,1,424,128]{4,3,2,1,0:T(8,128)(2,1)S(1)}, u32[]{:S(2)}, u32[]{:S(2)}) collective-permute-start(bf16[4,1,1,424,128]{4,3,2,1,0:T(8,128)(2,1)S(1)} %get-tuple-element.109), channel_id=1, source_target_pairs={{0,4},{1,5},{2,6},{3,7},{4,0},{5,1},{6,2},{7,3},{8,12},{9,13},{10,... | collective-permute-start | bytes 1302536 | tf_op jit(solution)/shard_map/ppermute | solution.py:590
  165.9 10.4 %collective-permute-start.17 = (bf16[1,1,1,576,128]{4,3,2,1,0:T(8,128)(2,1)S(1)}, bf16[1,1,1,576,128]{4,3,2,1,0:T(8,128)(2,1)S(1)}, u32[]{:S(2)}, u32[]{:S(2)}) collective-permute-start(bf16[1,1,1,576,128]{4,3,2,1,0:T(8,128)(2,1)S(1)} %add_convert_fusion.10), channel_id=1, source_target_pairs={{0,16},{1,17},{2,18},{3,19},{4,20},{5,21},{6,22},{7,23},{8,24},{9,... | collective-permute-start | bytes 442376 | tf_op jit(solution)/shard_map/ppermute | solution.py:590
  165.9 10.4 %collective-permute-start.16 = (bf16[1,1,1,576,128]{4,3,2,1,0:T(8,128)(2,1)S(1)}, bf16[1,1,1,576,128]{4,3,2,1,0:T(8,128)(2,1)S(1)}, u32[]{:S(2)}, u32[]{:S(2)}) collective-permute-start(bf16[1,1,1,576,128]{4,3,2,1,0:T(8,128)(2,1)S(1)} %add_convert_fusion.10), channel_id=1, source_target_pairs={{0,8},{1,9},{2,10},{3,11},{4,12},{5,13},{6,14},{7,15},{8,0},{9,1},... | collective-permute-start | bytes 442376 | tf_op jit(solution)/shard_map/ppermute | solution.py:590
  176.4 29.4 %collective-permute-start.39 = (bf16[4,2,1,424,128]{4,3,2,1,0:T(8,128)(2,1)S(1)}, bf16[4,2,1,424,128]{4,3,2,1,0:T(8,128)(2,1)S(1)}, u32[]{:S(2)}, u32[]{:S(2)}) collective-permute-start(bf16[4,2,1,424,128]{4,3,2,1,0:T(8,128)(2,1)S(1)} %pad_maximum_fusion.8), channel_id=1, source_target_pairs={{0,2},{1,3},{2,0},{3,1},{4,6},{5,7},{6,4},{7,5},{8,10},{9,11},{10,... | collective-permute-start | bytes 2605064 | tf_op jit(solution)/shard_map/ppermute | solution.py:590
  178.1 29.2 %collective-permute-start.41 = (bf16[4,1,2,424,128]{4,3,2,1,0:T(8,128)(2,1)S(1)}, bf16[4,1,2,424,128]{4,3,2,1,0:T(8,128)(2,1)S(1)}, u32[]{:S(2)}, u32[]{:S(2)}) collective-permute-start(bf16[4,1,2,424,128]{4,3,2,1,0:T(8,128)(2,1)S(1)} %pad_maximum_fusion.9), channel_id=1, source_target_pairs={{0,4},{1,5},{2,6},{3,7},{4,0},{5,1},{6,2},{7,3},{8,12},{9,13},{10,... | collective-permute-start | bytes 2605064 | tf_op jit(solution)/shard_map/ppermute | solution.py:590
  179.7 23.9 %collective-permute-start.19 = (bf16[4,1,1,288,128]{4,3,2,1,0:T(8,128)(2,1)S(1)}, bf16[4,1,1,288,128]{4,3,2,1,0:T(8,128)(2,1)S(1)}, u32[]{:S(2)}, u32[]{:S(2)}) collective-permute-start(bf16[4,1,1,288,128]{4,3,2,1,0:T(8,128)(2,1)S(1)} %get-tuple-element.114), channel_id=1, source_target_pairs={{0,4},{1,5},{2,6},{3,7},{4,0},{5,1},{6,2},{7,3},{8,12},{9,13},{10,... | collective-permute-start | bytes 884744 | tf_op jit(solution)/shard_map/ppermute | solution.py:590
  180.3 24.0 %collective-permute-start.21 = (bf16[4,1,1,288,128]{4,3,2,1,0:T(8,128)(2,1)S(1)}, bf16[4,1,1,288,128]{4,3,2,1,0:T(8,128)(2,1)S(1)}, u32[]{:S(2)}, u32[]{:S(2)}) collective-permute-start(bf16[4,1,1,288,128]{4,3,2,1,0:T(8,128)(2,1)S(1)} %get-tuple-element.113), channel_id=1, source_target_pairs={{0,2},{1,3},{2,0},{3,1},{4,6},{5,7},{6,4},{7,5},{8,10},{9,11},{10,... | collective-permute-start | bytes 884744 | tf_op jit(solution)/shard_map/ppermute | solution.py:590
  203.6 12.3 %collective-permute-start.20 = (bf16[4,2,1,288,128]{4,3,2,1,0:T(8,128)(2,1)S(1)}, bf16[4,2,1,288,128]{4,3,2,1,0:T(8,128)(2,1)S(1)}, u32[]{:S(2)}, u32[]{:S(2)}) collective-permute-start(bf16[4,2,1,288,128]{4,3,2,1,0:T(8,128)(2,1)S(1)} %pad_maximum_fusion.11), channel_id=1, source_target_pairs={{0,2},{1,3},{2,0},{3,1},{4,6},{5,7},{6,4},{7,5},{8,10},{9,11},{10,... | collective-permute-start | bytes 1769480 | tf_op jit(solution)/shard_map/ppermute | solution.py:590
  204.3 12.0 %collective-permute-start.22 = (bf16[4,1,2,288,128]{4,3,2,1,0:T(8,128)(2,1)S(1)}, bf16[4,1,2,288,128]{4,3,2,1,0:T(8,128)(2,1)S(1)}, u32[]{:S(2)}, u32[]{:S(2)}) collective-permute-start(bf16[4,1,2,288,128]{4,3,2,1,0:T(8,128)(2,1)S(1)} %pad_maximum_fusion.12), channel_id=1, source_target_pairs={{0,4},{1,5},{2,6},{3,7},{4,0},{5,1},{6,2},{7,3},{8,12},{9,13},{10,... | collective-permute-start | bytes 1769480 | tf_op jit(solution)/shard_map/ppermute | solution.py:590
  207.2 61.5 %collective-permute-start.42 = (bf16[16,424,128]{2,1,0:T(8,128)(2,1)}, bf16[16,424,128]{2,1,0:T(8,128)(2,1)}, u32[]{:S(2)}, u32[]{:S(2)}) collective-permute-start(bf16[16,424,128]{2,1,0:T(8,128)(2,1)} %bitcast.30), channel_id=1, source_target_pairs={{0,1},{1,0},{2,3},{3,2},{4,5},{5,4},{6,7},{7,6},{8,9},{9,8},{10,11... | collective-permute-start | bytes 5210120 | tf_op jit(solution)/shard_map/ppermute | solution.py:594
  208.6 61.2 %collective-permute-start.43 = (bf16[16,424,128]{2,1,0:T(8,128)(2,1)}, bf16[16,424,128]{2,1,0:T(8,128)(2,1)}, u32[]{:S(2)}, u32[]{:S(2)}) collective-permute-start(bf16[16,424,128]{2,1,0:T(8,128)(2,1)} %bitcast.31), channel_id=1, source_target_pairs={{0,1},{1,0},{2,3},{3,2},{4,5},{5,4},{6,7},{7,6},{8,9},{9,8},{10,11... | collective-permute-start | bytes 5210120 | tf_op jit(solution)/shard_map/ppermute | solution.py:594
  216.1 34.9 %collective-permute-start.23 = (bf16[16,288,128]{2,1,0:T(8,128)(2,1)S(1)}, bf16[16,288,128]{2,1,0:T(8,128)(2,1)}, u32[]{:S(2)}, u32[]{:S(2)}) collective-permute-start(bf16[16,288,128]{2,1,0:T(8,128)(2,1)S(1)} %bitcast.56), channel_id=1, source_target_pairs={{0,1},{1,0},{2,3},{3,2},{4,5},{5,4},{6,7},{7,6},{8,9},{9,8},{10,11... | collective-permute-start | bytes 3538952 | tf_op jit(solution)/shard_map/ppermute | solution.py:594
  216.5 34.5 %collective-permute-start.24 = (bf16[16,288,128]{2,1,0:T(8,128)(2,1)S(1)}, bf16[16,288,128]{2,1,0:T(8,128)(2,1)}, u32[]{:S(2)}, u32[]{:S(2)}) collective-permute-start(bf16[16,288,128]{2,1,0:T(8,128)(2,1)S(1)} %bitcast.58), channel_id=1, source_target_pairs={{0,1},{1,0},{2,3},{3,2},{4,5},{5,4},{6,7},{7,6},{8,9},{9,8},{10,11... | collective-permute-start | bytes 3538952 | tf_op jit(solution)/shard_map/ppermute | solution.py:594
  (32 other events, 184.8 us)

commit v2 on v1

v2 whole, which is shorter than its diff:
```python
import functools

import jax
import jax.numpy as jnp
from jax import lax
from jax.experimental import pallas as pl
from jax.experimental.pallas import tpu as pltpu
from jax.sharding import PartitionSpec as P

EPS = 1e-06
GROUP = 16
LANES = 128
DEAD = 256
AXES = ("grp", "row")
F32 = jnp.float32
BF = jnp.bfloat16
NN = (((1,), (0,)), ((), ()))
NT = (((1,), (1,)), ((), ()))
TN = (((0,), (0,)), ((), ()))
VMEM = pl.BlockSpec(memory_space=pltpu.VMEM)
SMEM = pl.BlockSpec(memory_space=pltpu.SMEM)
HBM = pl.BlockSpec(memory_space=pltpu.HBM)
shape_of = jax.ShapeDtypeStruct


def took(us):
    return pl.CostEstimate(flops=int(us * 1.15e9), bytes_accessed=1 << 20, transcendentals=0)


def hbm(value):
    return pltpu.with_memory_space_constraint(value, pltpu.HBM)


def mm(a, b, dims=NN):
    return lax.dot_general(a, b, dims, preferred_element_type=F32)


def colsum(v):
    return jnp.sum(v, axis=0, keepdims=True)


def group_sums(rows):
    chunks = rows[0].shape[1] // LANES
    v = jnp.concatenate([r[:, c * LANES : (c + 1) * LANES] for r in rows for c in range(chunks)], axis=0)
    lane = lax.broadcasted_iota(jnp.int32, v.shape, 1)
    step = 1
    while step < GROUP:
        below = pltpu.roll(v, step, 1)
        above = pltpu.roll(v, LANES - step, 1)
        v = v + jnp.where((lane & step) != 0, below, above)
        step *= 2
    return [
        jnp.concatenate([v[k * chunks + c : k * chunks + c + 1] for c in range(chunks)], axis=1)
        for k in range(len(rows))
    ]


def normalized(images):
    count = images[0].shape[0] * GROUP
    middles = group_sums([colsum(v) for v in images])
    centered = [v - m / count for v, m in zip(images, middles)]
    spreads = group_sums([colsum(c * c) for c in centered])
    scales = [lax.rsqrt(v / count + EPS) for v in spreads]
    return [(c * r, r) for c, r in zip(centered, scales)]


def norm_back(images, gain):
    count = images[0][0].shape[0] * GROUP
    bias_grads = [colsum(dy) for _, _, dy in images]
    gain_grads = [colsum(dy * n) for n, _, dy in images]
    sums = group_sums([g * gain for g in bias_grads] + [g * gain for g in gain_grads])
    total = len(images)
    dxs = [
        r * (dy * gain - sums[i] / count - n * (sums[total + i] / count)) for i, (n, r, dy) in enumerate(images)
    ]
    return dxs, sum(gain_grads), sum(bias_grads)


def sigmoid(y):
    return 1.0 / (1.0 + jnp.exp(-y))


def shifted(v, side):
    px = v.shape[0]
    col = lax.broadcasted_iota(jnp.int32, v.shape, 0) % side
    left = jnp.where(col == 0, 0.0, pltpu.roll(v, 1, 0))
    right = jnp.where(col == side - 1, 0.0, pltpu.roll(v, px - 1, 0))
    return left, v, right


def put_shifts(s_ref, image, v, side):
    px, ch = v.shape
    for j, t in enumerate(shifted(v, side)):
        s_ref[image, side : px + side, j * ch : (j + 1) * ch] = t.astype(BF)


def clear_edges(s_ref, side):
    images, rows, width = s_ref.shape
    zero = jnp.zeros((side, width), BF)
    for i in range(images):
        s_ref[i, 0:side, :] = zero
        s_ref[i, rows - side : rows, :] = zero


def window(s_ref, first, px, cols):
    return jnp.concatenate([s_ref[i, first : first + px, cols] for i in range(s_ref.shape[0])], axis=0)


def conv(s_ref, w_ref, px, side, ch):
    acc = None
    for dh in range(3):
        part = mm(window(s_ref, dh * side, px, slice(None)), w_ref[dh * 3 * ch : (dh + 1) * 3 * ch, :])
        acc = part if acc is None else acc + part
    return acc


def conv_back(s_ref, w_ref, px, side, ch):
    acc = None
    for dh in range(3):
        for dw in range(3):
            tap = dh * 3 + dw
            cols = slice((2 - dw) * ch, (3 - dw) * ch)
            part = mm(window(s_ref, (2 - dh) * side, px, cols), w_ref[tap * ch : (tap + 1) * ch, :], NT)
            acc = part if acc is None else acc + part
    return acc


def split_cols(v, bit):
    half = v.shape[1] // 2
    low, high = v[:, :half], v[:, half:]
    return jnp.where(bit == 0, low, high), jnp.where(bit == 0, high, low)


def start_copies(pairs, sems):
    copies = [pltpu.make_async_copy(a, b, sems.at[i]) for i, (a, b) in enumerate(pairs)]
    for c in copies:
        c.start()
    return copies


def entry_body(
    place_ref, mine_hbm, other_ref, vec_ref, w1, gy_hbm, w2_hbm, wq_hbm, wk_hbm, wv_hbm, wo_hbm,
    own_ref, chip_ref, near_ref, far_ref, norm2_ref, scale2_ref, x_ref, gy_ref, w2, wq, wk, wv, wo, s_ref, sems, *, side,
):
    images, px, ch = x_ref.shape
    part = px // 2
    core = place_ref[0]
    bit, other_bit = place_ref[6], place_ref[7]
    here = pl.multiple_of(core * part, part)
    there = pl.multiple_of((1 - core) * part, part)
    copies = start_copies(
        [(mine_hbm.at[core * images + i], x_ref.at[i, pl.ds(here, part)]) for i in range(images)]
        + [(w2_hbm, w2), (gy_hbm, gy_ref), (wq_hbm, wq), (wk_hbm, wk), (wv_hbm, wv), (wo_hbm, wo)],
        sems,
    )

    def row(i):
        return vec_ref[i : i + 1, :]

    def give(which, a):
        for i in range(images):
            low = a[i].astype(BF)
            own_ref[which, i], near_ref[which, i] = split_cols(low, bit)
            chip_ref[which, i], far_ref[which, i] = split_cols(low, other_bit)

    clear_edges(s_ref, side)
    for i in range(images):
        x_ref[i, pl.ds(there, part), :] = other_ref[i]
    for c in copies[:images]:
        c.wait()
    active = []
    for i, (n, _) in enumerate(normalized([x_ref[i].astype(F32) for i in range(images)])):
        y = n * row(0) + row(1)
        active.append(y * sigmoid(y))
        put_shifts(s_ref, i, active[i], side)
    give(0, active)
    filtered = conv(s_ref, w1, px, side, ch) + row(2)
    active = []
    for i, (n, r) in enumerate(normalized([filtered[i * px : (i + 1) * px] for i in range(images)])):
        norm2_ref[i] = n
        scale2_ref[i : i + 1, :] = r
        y = n * row(3) + row(4)
        active.append(y * sigmoid(y))
    give(1, active)
    for c in copies[images:]:
        c.wait()


def run_entry(place, mine, other, vec, w1, gy, w2, weights, side):
    images, part, ch = other.shape
    px = 2 * part
    acts = shape_of((2, images, px, ch // 2), BF)
    whole = (images, px, ch)
    return pl.pallas_call(
        functools.partial(entry_body, side=side),
        name="entry",
        in_specs=[SMEM, HBM] + [VMEM] * 3 + [HBM] * 6,
        out_specs=[VMEM] * 13,
        out_shape=[acts] * 4
        + [shape_of(whole, F32), shape_of((images, ch), F32), shape_of(whole, BF), shape_of(whole, BF), shape_of(w2.shape, BF)]
        + [shape_of((ch, ch), BF)] * 4,
        scratch_shapes=[
            pltpu.VMEM((images, px + 2 * side, 3 * ch), BF),
            pltpu.SemaphoreType.DMA((images + 6,)),
        ],
        cost_estimate=took(8.5),
        compiler_params=pltpu.CompilerParams(vmem_limit_bytes=12 << 20),
    )(place, hbm(mine), other, vec, w1, *[hbm(v) for v in (gy, w2, *weights)])


def attention_body(
    place_ref, x_ref, own_ref, near_ref, gy_ref, ckeep_ref, csend_ref, vec_ref, w2, wq, wk, wv, wo,
    out_ref, dres_ref, dkeep_ref, dsend_ref, stat_ref, gkeep_ref, gsend_ref,
    s_ref, norm_ref, normed, q, k, v, mixed, *, side,
):
    images, px, ch = x_ref.shape
    core = place_ref[0]
    bit = place_ref[6]

    def row(i):
        return vec_ref[i : i + 1, :]

    every = range(images)
    clear_edges(s_ref, side)
    for i in every:
        mine, other = own_ref[1, i], near_ref[1, i]
        a = jnp.concatenate([jnp.where(bit == 0, mine, other), jnp.where(bit == 0, other, mine)], axis=1)
        put_shifts(s_ref, i, a.astype(F32), side)

    def flat(ref):
        return ref[...].reshape(images * px, ch)

    def spans(v):
        return [v[i * px : (i + 1) * px] for i in every]

    dm = mm(flat(gy_ref), wo[...], NT).astype(BF)
    branch = conv(s_ref, w2, px, side, ch) + row(5)
    res = [x_ref[i].astype(F32) + b for i, b in zip(every, spans(branch))]
    scales = []
    for i, (n, r) in enumerate(normalized(res)):
        dres_ref[i] = res[i]
        norm_ref[i] = n
        scales.append(r)
        normed[i] = (n * row(6) + row(7)).astype(BF)
    nb = flat(normed)
    queries = (mm(nb, wq[...]) + row(8)).astype(BF)
    keys = mm(nb, wk[...]).astype(BF)
    values = (mm(nb, wv[...]) + row(9)).astype(BF)
    scale = ch ** -0.5
    for i, qi, ki, vi, di in zip(every, spans(queries), spans(keys), spans(values), spans(dm)):
        scores = mm(qi, ki, NT) * scale
        dp = mm(di, vi, NT)
        peak = jnp.max(scores, axis=1, keepdims=True)
        lifted = jnp.exp(scores - peak)
        probs = lifted / jnp.sum(lifted, axis=1, keepdims=True)
        pb = probs.astype(BF)
        mixed[i] = mm(pb, vi).astype(BF)
        v[i] = mm(pb, di, TN).astype(BF)
        ds = (probs * (dp - jnp.sum(probs * dp, axis=1, keepdims=True))).astype(BF)
        q[i] = (mm(ds, ki) * scale).astype(BF)
        k[i] = (mm(ds, qi, TN) * scale).astype(BF)
    dn = mm(flat(q), wq[...], NT) + mm(flat(k), wk[...], NT) + mm(flat(v), wv[...], NT)
    projected = mm(flat(mixed), wo[...]) + row(10)
    for i, p in zip(every, spans(projected)):
        out_ref[i] = (dres_ref[i] + p).astype(BF)
    dxs, gain_grad, bias_grad = norm_back(
        [(norm_ref[i], r, d) for i, r, d in zip(every, scales, spans(dn))], row(6)
    )
    total = jnp.zeros((1, ch), F32)
    for i, dx in zip(every, dxs):
        dres = gy_ref[i].astype(F32) + dx
        dres_ref[i] = dres
        db = dres.astype(BF)
        dkeep_ref[i], dsend_ref[i] = split_cols(db, core)
        total = total + colsum(db.astype(F32))
    stat_ref[...] = jnp.zeros(stat_ref.shape, F32)
    stat_ref[0:1, :] = total
    stat_ref[1:2, :] = gain_grad
    stat_ref[2:3, :] = bias_grad
    stat_ref[3:4, :] = colsum(flat(q).astype(F32))
    stat_ref[4:5, :] = colsum(flat(v).astype(F32))
    stat_ref[5:6, :] = colsum(flat(gy_ref).astype(F32))
    owners = gkeep_ref.shape[0]
    rows = ch // owners
    mine_at, other_at = place_ref[4], place_ref[5]
    for j, (lhs, rhs) in enumerate(((normed, q), (normed, k), (normed, v), (mixed, gy_ref))):
        keep, send = split_cols(mm(flat(lhs), flat(rhs), TN).astype(BF), core)
        for o in range(owners):
            gkeep_ref[o ^ mine_at, j * rows : (j + 1) * rows] = keep[o * rows : (o + 1) * rows]
            gsend_ref[o ^ other_at, j * rows : (j + 1) * rows] = send[o * rows : (o + 1) * rows]
    for o in range(owners):
        gkeep_ref[o, 4 * rows :] = ckeep_ref[o]
        gsend_ref[o, 4 * rows :] = csend_ref[o]


def run_attention(place, x, own, near, gy, ckeep, csend, vec, weights, side):
    images, px, ch = gy.shape
    half = ch // 2
    owners, count, _ = ckeep.shape
    rows = 4 * (ch // owners) + count
    whole = (images, px, ch)
    return pl.pallas_call(
        functools.partial(attention_body, side=side),
        name="attention",
        in_specs=[SMEM] + [VMEM] * 12,
        out_specs=[VMEM] * 7,
        out_shape=[
            shape_of(whole, BF), shape_of(whole, F32),
            shape_of((images, px, half), BF), shape_of((images, px, half), BF),
            shape_of((8, ch), F32),
            shape_of((owners, rows, half), BF), shape_of((owners, rows, half), BF),
        ],
        scratch_shapes=[pltpu.VMEM((images, px + 2 * side, 3 * ch), BF), pltpu.VMEM(whole, F32)]
        + [pltpu.VMEM(whole, BF)] * 5,
        cost_estimate=took(13.5),
        compiler_params=pltpu.CompilerParams(vmem_limit_bytes=20 << 20),
    )(place, x, own, near, gy, ckeep, csend, vec, *weights)


def swish_back(da, ns, gain, bias):
    dys = []
    for d, n in zip(da, ns):
        y = n * gain + bias
        sig = sigmoid(y)
        dys.append(d * (sig * (1.0 + y * (1.0 - sig))))
    return dys


def back2_body(
    place_ref, dres_ref, norm2_ref, scale2_ref, vec_ref, w2,
    dkeep_ref, dsend_ref, dfull_ref, stat_ref, s_ref, *, side,
):
    images, px, ch = dres_ref.shape
    every = range(images)
    core = place_ref[0]
    clear_edges(s_ref, side)

    def row(i):
        return vec_ref[i : i + 1, :]

    for i in every:
        put_shifts(s_ref, i, dres_ref[i], side)
    da = conv_back(s_ref, w2, px, side, ch)
    ns = [norm2_ref[i] for i in every]
    dys = swish_back([da[i * px : (i + 1) * px] for i in every], ns, row(3), row(4))
    dxs, gain_grad, bias_grad = norm_back(
        [(n, scale2_ref[i : i + 1, :], dy) for i, n, dy in zip(every, ns, dys)], row(3)
    )
    total = jnp.zeros((1, ch), F32)
    for i, dx in zip(every, dxs):
        db = dx.astype(BF)
        dfull_ref[i] = db
        dkeep_ref[i], dsend_ref[i] = split_cols(db, core)
        total = total + colsum(db.astype(F32))
    stat_ref[...] = jnp.zeros(stat_ref.shape, F32)
    stat_ref[0:1, :] = gain_grad
    stat_ref[1:2, :] = bias_grad
    stat_ref[2:3, :] = total


def run_back2(place, dres, norm2, scale2, vec, w2, side):
    images, px, ch = dres.shape
    half = (images, px, ch // 2)
    return pl.pallas_call(
        functools.partial(back2_body, side=side),
        name="conv2_back",
        in_specs=[SMEM] + [VMEM] * 5,
        out_specs=[VMEM] * 4,
        out_shape=[shape_of(half, BF), shape_of(half, BF), shape_of((images, px, ch), BF), shape_of((8, ch), F32)],
        scratch_shapes=[pltpu.VMEM((images, px + 2 * side, 3 * ch), BF)],
        cost_estimate=took(5),
        compiler_params=pltpu.CompilerParams(vmem_limit_bytes=12 << 20),
    )(place, dres, norm2, scale2, vec, w2)


def back1_body(
    place_ref, dfull_ref, x_ref, dres_ref, vec_ref, w1,
    out_hbm, send_ref, stat_ref, s_ref, keep_ref, sem, *, side,
):
    images, px, ch = dres_ref.shape
    part = px // 2
    core = place_ref[0]
    every = range(images)
    clear_edges(s_ref, side)

    def row(i):
        return vec_ref[i : i + 1, :]

    for i in every:
        put_shifts(s_ref, i, dfull_ref[i].astype(F32), side)
    da = conv_back(s_ref, w1, px, side, ch)
    norms = normalized([x_ref[i].astype(F32) for i in every])
    ns = [n for n, _ in norms]
    dys = swish_back([da[i * px : (i + 1) * px] for i in every], ns, row(0), row(1))
    dxs, gain_grad, bias_grad = norm_back([(n, r, dy) for (n, r), dy in zip(norms, dys)], row(0))
    for i, dx in zip(every, dxs):
        total = (dres_ref[i] + dx).astype(BF)
        low, high = total[:part], total[part:]
        keep_ref[i] = jnp.where(core == 0, low, high)
        send_ref[i] = jnp.where(core == 0, high, low)
    stat_ref[...] = jnp.zeros(stat_ref.shape, F32)
    stat_ref[0:1, :] = gain_grad
    stat_ref[1:2, :] = bias_grad
    copy = pltpu.make_async_copy(keep_ref, out_hbm.at[pl.ds(core * images, images)], sem)
    copy.start()
    copy.wait()


def run_back1(place, dfull, x, dres, vec, w1, side):
    images, px, ch = dres.shape
    part = (images, px // 2, ch)
    return pl.pallas_call(
        functools.partial(back1_body, side=side),
        name="conv1_back",
        in_specs=[SMEM] + [VMEM] * 5,
        out_specs=[HBM, VMEM, VMEM],
        out_shape=[shape_of((2 * images, px // 2, ch), BF), shape_of(part, BF), shape_of((8, ch), F32)],
        scratch_shapes=[
            pltpu.VMEM((images, px + 2 * side, 3 * ch), BF),
            pltpu.VMEM(part, BF),
            pltpu.SemaphoreType.DMA(()),
        ],
        cost_estimate=took(5.4),
        compiler_params=pltpu.CompilerParams(vmem_limit_bytes=12 << 20),
    )(place, dfull, x, dres, vec, w1)


def place_rows_body(place_ref, got_ref, into_hbm, out_hbm, token_ref, sem):
    images = got_ref.shape[0]
    token_ref[...] = jnp.zeros(token_ref.shape, F32)
    copy = pltpu.make_async_copy(got_ref, out_hbm.at[pl.ds((1 - place_ref[0]) * images, images)], sem)
    copy.start()
    copy.wait()


def run_place_rows(place, got, into):
    return pl.pallas_call(
        place_rows_body,
        name="place_rows",
        in_specs=[SMEM, VMEM, HBM],
        out_specs=[HBM, VMEM],
        out_shape=[shape_of(into.shape, BF), shape_of((8, 128), F32)],
        scratch_shapes=[pltpu.SemaphoreType.DMA(())],
        input_output_aliases={2: 0},
        cost_estimate=took(1),
        compiler_params=pltpu.CompilerParams(vmem_limit_bytes=4 << 20),
    )(place, got, into)


def kernel_grad_body(place_ref, *refs, side, which):
    acts, grads = refs[:4], refs[4:8]
    out_ref, s_ref, d_ref = refs[-3:]
    _, images, px, part = acts[0].shape
    half = grads[0].shape[2]
    bits = place_ref[8]
    first, second, _, _ = out_ref.shape
    owners = first * second
    rows = part // owners
    zero = jnp.zeros((side, half), BF)
    for n in range(4 * images):
        d_ref[n, 0:side, :] = zero
        d_ref[n, px + side :, :] = zero
    for n, (a, d) in enumerate(zip(acts, grads)):

        def fill(i, carry, a=a, d=d, n=n):
            at = n * images + i
            d_ref[at, side : px + side, :] = d[i]
            for j, t in enumerate(shifted(a[which, i].astype(F32), side)):
                s_ref[j * part : (j + 1) * part, pl.ds(pl.multiple_of(at * px, px), px)] = t.astype(BF).T
            return carry

        lax.fori_loop(0, images, fill, 0)
    for dh in range(3):
        start = (2 - dh) * side
        d = jnp.concatenate([d_ref[n, start : start + px, :] for n in range(4 * images)], axis=0)
        g = mm(s_ref[...], d).astype(BF)
        for o in range(owners):
            at = o ^ bits
            for dw in range(3):
                tap = dh * 3 + dw
                begin = dw * part + o * rows
                out_ref[at // second, at % second, tap * rows : (tap + 1) * rows, :] = g[begin : begin + rows]


def run_kernel_grad(place, which, acts, grads, lead, side, name):
    _, images, px, part = acts[0].shape
    half = grads[0].shape[2]
    rows = 9 * (part // (lead[0] * lead[1]))
    return pl.pallas_call(
        functools.partial(kernel_grad_body, side=side, which=which),
        name=name,
        in_specs=[SMEM] + [VMEM] * 8,
        out_specs=VMEM,
        out_shape=shape_of((lead[0], lead[1], rows, half), BF),
        scratch_shapes=[
            pltpu.VMEM((3 * part, 4 * images * px), BF),
            pltpu.VMEM((4 * images, px + 2 * side, half), BF),
        ],
        cost_estimate=took(4.8),
        compiler_params=pltpu.CompilerParams(vmem_limit_bytes=14 << 20),
    )(place, *acts, *grads)


def prepare_body(place_ref, ids_hbm, dead_hbm, replace_hbm, latents_hbm, w1_hbm, *refs):
    count_vectors = (len(refs) - 12) // 2
    vectors = refs[:count_vectors]
    counts_ref, slots_ref, keep_ref, send_ref, vec_ref, w1_ref = refs[count_vectors : count_vectors + 6]
    lines = refs[count_vectors + 6 : 2 * count_vectors + 6]
    ids_ref, dead_ref, replace_ref, latents_ref, sems, _ = refs[2 * count_vectors + 6 :]
    copies = start_copies(
        (
            (ids_hbm, ids_ref), (dead_hbm, dead_ref), (replace_hbm, replace_ref), (latents_hbm, latents_ref),
            *zip(vectors, lines), (w1_hbm, w1_ref),
        ),
        sems,
    )
    core = place_ref[0]
    offset = place_ref[2]
    for c in copies[:2]:
        c.wait()
    codes = dead_ref.shape[1]
    pixels, width = latents_ref.shape
    one = jnp.ones((), BF)
    none = jnp.zeros((), BF)
    code = lax.broadcasted_iota(jnp.int32, (codes, pixels), 0)
    hit = jnp.where(code == ids_ref[...], one, none)
    counts_ref[...] = mm(jnp.ones((8, pixels), BF), hit, NT)
    dead = dead_ref[...]
    ahead = lax.broadcasted_iota(jnp.int32, (codes, codes), 0) <= lax.broadcasted_iota(jnp.int32, (codes, codes), 1)
    rank = mm(jnp.broadcast_to(dead.astype(F32), (8, codes)).astype(BF), jnp.where(ahead, one, none))[0:1]
    rank = jnp.where(dead == 1, rank.astype(jnp.int32) - 1, -1)
    owners, count, _ = keep_ref.shape
    at = lax.broadcasted_iota(jnp.int32, (DEAD, codes), 0)
    beyond = at // (owners * count)
    owner = ((at % (owners * count)) // count) ^ jnp.where(beyond == 0, place_ref[4], place_ref[5])
    at = (beyond ^ core) * (owners * count) + owner * count + at % count
    slot = at == rank
    slots_ref[...] = jnp.where(slot, one, none)
    for c in copies[2:4]:
        c.wait()
    wanted = jnp.sum(jnp.where(slot, replace_ref[...], 0), axis=1, keepdims=True) - offset
    pixel = lax.broadcasted_iota(jnp.int32, (DEAD, pixels), 1)
    rows = mm(jnp.where(pixel == wanted, one, none), latents_ref[...]).astype(BF)
    for j in range(owners):
        keep_ref[j] = rows[j * count : (j + 1) * count]
        send_ref[j] = rows[DEAD // 2 + j * count : DEAD // 2 + (j + 1) * count]
    for c in copies[4:]:
        c.wait()
    for i, line in enumerate(lines):
        vec_ref[i : i + 1, :] = line[...].astype(F32).reshape(1, -1)


def run_prepare(place, ids, dead, replace, latents, w1, vectors, owners):
    codes = dead.shape[1]
    pixels, width = latents.shape
    ch = w1.shape[1]
    rows = shape_of((owners, DEAD // (2 * owners), width), BF)
    return pl.pallas_call(
        prepare_body,
        name="prepare",
        in_specs=[SMEM] + [HBM] * (5 + len(vectors)),
        out_specs=[VMEM] * 6,
        out_shape=[
            shape_of((8, codes), F32), shape_of((DEAD, codes), BF), rows, rows,
            shape_of((16, ch), F32), shape_of(w1.shape, BF),
        ],
        scratch_shapes=[pltpu.VMEM((ch,), BF)] * len(vectors)
        + [
            pltpu.VMEM((1, pixels), jnp.int32), pltpu.VMEM((1, codes), jnp.int32), pltpu.VMEM((1, codes), jnp.int32),
            pltpu.VMEM((pixels, width), BF), pltpu.SemaphoreType.DMA((5 + len(vectors),)), pltpu.SMEM((1,), jnp.int32),
        ],
        cost_estimate=took(2.2),
        compiler_params=pltpu.CompilerParams(vmem_limit_bytes=16 << 20),
    )(place, *[hbm(v) for v in (ids, dead, replace, latents, w1, *vectors)])


def spread_all(place_ref, pieces, buf, sem, taps_out, outs, start=0):
    core = place_ref[0]
    ats = (place_ref[4], place_ref[5])
    copies = []
    step = 0
    for piece, beyond, far in pieces:
        owners = piece.shape[0]
        _, groups, rows, cols = buf.shape
        high = core ^ beyond
        for j in range(owners):
            buf[step] = piece[j, start : start + groups * rows, :].astype(F32).reshape(groups, rows, cols)
            at = pl.ds(pl.multiple_of(((j + far * owners) ^ ats[beyond]) * rows, rows), rows)
            to = pl.ds(pl.multiple_of(high * cols, cols), cols)
            if taps_out is None:
                new = [pltpu.make_async_copy(buf.at[step, g], out.at[at, to], sem) for g, out in enumerate(outs)]
            else:
                new = [pltpu.make_async_copy(buf.at[step], taps_out.at[:, at, to], sem)]
            for c in new:
                c.start()
            copies += new
            step += 1
    for c in copies:
        c.wait()


def attention_finish_body(place_ref, mine0, other0, mine1, other1, slots_ref, book_ref, *refs):
    *outs, out_ref, rows_ref, buf, sem = refs
    device = place_ref[3]
    pieces = ((mine0, 0, 0), (other0, 1, 0), (mine1, 0, 1), (other1, 1, 1))
    entries, width = book_ref.shape
    owners, total, _ = mine0.shape
    count = DEAD // (4 * owners)
    start = total - count
    rows_ref[:, width:] = jnp.ones((DEAD, 128), F32)
    for n, piece in enumerate((mine0, mine1, other0, other1)):
        for j in range(owners):
            at = (n * owners + j) * count
            rows_ref[at : at + count, :width] = piece[j, start:, :].astype(F32)
    whole = mm(slots_ref[...], rows_ref[...].astype(BF), TN)
    codes = whole.shape[0]
    pick = lax.broadcasted_iota(jnp.int32, (entries, codes), 1) - device * entries
    pick = jnp.where(pick == lax.broadcasted_iota(jnp.int32, (entries, codes), 0), 1.0, 0.0).astype(BF)
    own = mm(pick, whole.astype(BF))
    out_ref[...] = jnp.where(own[:, width : width + 1] > 0.5, own[:, :width], book_ref[...])
    spread_all(place_ref, pieces, buf, sem, None, outs, start - buf.shape[1] * buf.shape[2])


def run_attention_finish(place, pieces, slots, book, ch):
    owners, total, half = pieces[0].shape
    rows = ch // (2 * owners)
    width = book.shape[1]
    return pl.pallas_call(
        attention_finish_body,
        name="attention_finish",
        in_specs=[SMEM] + [VMEM] * 6,
        out_specs=[HBM] * 4 + [VMEM],
        out_shape=[shape_of((ch, ch), F32)] * 4 + [shape_of(book.shape, F32)],
        scratch_shapes=[
            pltpu.VMEM((DEAD, width + 128), F32),
            pltpu.VMEM((4 * owners, 4, rows, half), F32),
            pltpu.SemaphoreType.DMA(()),
        ],
        cost_estimate=took(3),
        compiler_params=pltpu.CompilerParams(vmem_limit_bytes=12 << 20),
    )(place, *pieces, slots, book)


def conv_finish_body(place_ref, mine, other, *refs, far):
    out_ref, buf, sem = refs[-3:]
    spread_all(place_ref, ((mine, 0, far), (other, 1, far)), buf, sem, out_ref, ())


def run_conv_finish(place, mine, other, into, ch, name):
    owners, total, half = mine.shape
    rows = ch // (2 * owners)
    given = [] if into is None else [into]
    return pl.pallas_call(
        functools.partial(conv_finish_body, far=len(given)),
        name=name,
        in_specs=[SMEM] + [VMEM] * 2 + [HBM] * len(given),
        out_specs=HBM,
        out_shape=shape_of((9, ch, ch), F32),
        scratch_shapes=[pltpu.VMEM((2 * owners, 9, rows, half), F32), pltpu.SemaphoreType.DMA(())],
        input_output_aliases={3: 0} if given else {},
        cost_estimate=took(3.5),
        compiler_params=pltpu.CompilerParams(vmem_limit_bytes=12 << 20),
    )(place, mine, other, *given)


def together(*values):
    return lax.optimization_barrier(values)


def vectors_body(sums_ref, *outs):
    *vectors, usage_ref, perplexity_ref = outs
    for i, out in enumerate(vectors):
        out[...] = sums_ref[i : i + 1, :]
    codes = usage_ref.shape[1]
    width = sums_ref.shape[1]
    first = len(vectors)
    counts = jnp.concatenate([sums_ref[first + i : first + i + 1, :] for i in range(codes // width)], axis=1)
    usage_ref[...] = counts.astype(jnp.int32)
    share = counts / jnp.sum(counts, axis=1, keepdims=True)
    entropy = jnp.sum(share * jnp.log(share + 1e-10), axis=1, keepdims=True)
    perplexity_ref[...] = jnp.exp(-entropy)


def run_vectors(sums, vectors, codes):
    ch = sums.shape[1]
    return pl.pallas_call(
        vectors_body,
        name="vectors",
        in_specs=[VMEM],
        out_specs=[VMEM] * (vectors + 2),
        cost_estimate=took(1.4),
        out_shape=[shape_of((1, ch), F32)] * vectors + [shape_of((1, codes), jnp.int32), shape_of((1, 1), F32)],
    )(sums)


class Links:
    def __init__(self, chips):
        self.chips = chips
        bits = chips.bit_length() - 1
        self.low = 1 if bits < 6 else 2
        sizes = [self.low - 1, self.low, bits - 2 * self.low]
        shifts = [1, self.low, 2 * self.low]
        self.dims = [(shift, size) for shift, size in zip(shifts, sizes) if size > 0]
        self.rest = bits - 1

    def swapped(self, index):
        mask = (1 << self.low) - 1
        first, second = index & mask, (index >> self.low) & mask
        return ((index >> (2 * self.low)) << (2 * self.low)) | (first << self.low) | second

    def flat(self, index):
        total = index & 1
        for shift, size in self.dims:
            total = (total << size) | ((index >> shift) & ((1 << size) - 1))
        return total

    def key(self, key, core):
        return self.swapped(key) if core else key

    def send(self, value, key):
        pairs = [(g * 2 + c, (g ^ self.key(key, c)) * 2 + c) for g in range(self.chips) for c in range(2)]
        return lax.ppermute(value, AXES, pairs)

    def partner(self, value):
        pairs = [(g * 2 + c, g * 2 + 1 - c) for g in range(self.chips) for c in range(2)]
        return lax.ppermute(value, AXES, pairs)

    def far(self, value):
        pairs = [(g * 2 + c, (g ^ self.key(1, 1 - c)) * 2 + 1 - c) for g in range(self.chips) for c in range(2)]
        return lax.ppermute(value, AXES, pairs)

    def reduce(self, value, dim, keep=None):
        shift, size = self.dims[dim]
        got = [self.send(value[k], k << shift) for k in range(1, 1 << size)]
        total = (value if keep is None else keep)[0].astype(F32)
        for g in got:
            total = total + g.astype(F32)
        return total.astype(BF)

    def gather(self, value, dim):
        shift, size = self.dims[dim]
        return jnp.stack([value] + [self.send(value, k << shift) for k in range(1, 1 << size)])

    def lead(self):
        return tuple(1 << size for _, size in self.dims)

    def small_steps(self):
        steps = [lambda value: value + self.partner(value)]
        for bit in range(self.chips.bit_length() - 1):
            steps.append(lambda value, key=1 << bit: value + self.send(value, key))
        return steps


def local(
    image_rows, grad_out, code_ids, dead_flags, replace_ids, latents, codebook,
    norm1_gain, norm1_bias, conv1_kernel, conv1_bias, norm2_gain, norm2_bias, conv2_kernel, conv2_bias,
    norm3_gain, norm3_bias, query_weight, query_bias, key_weight, value_weight, value_bias, out_weight, out_bias,
    *, chips,
):
    links = Links(chips)
    owners = chips
    all_images, part_rows, side, ch = image_rows.shape
    images = all_images // 2
    px = grad_out.shape[1] * side
    part = part_rows * side
    core = lax.axis_index("row").astype(jnp.int32)
    chip = lax.axis_index("grp").astype(jnp.int32)
    device = chip * 2 + core
    as_first, as_second = links.flat(chip), links.flat(links.swapped(chip))
    mine_at = jnp.where(core == 0, as_first, as_second)
    other_at = jnp.where(core == 0, as_second, as_first)
    low = owners // 2
    place = jnp.stack([
        core, chip, device * latents.shape[0], device, mine_at, other_at,
        mine_at // low, other_at // low, mine_at % low,
    ])
    mine = image_rows.reshape(all_images, part, ch)
    other = links.partner(lax.dynamic_slice_in_dim(mine, (1 - core) * images, images))
    vectors = [
        norm1_gain, norm1_bias, conv1_bias, norm2_gain, norm2_bias, conv2_bias,
        norm3_gain, norm3_bias, query_bias, value_bias, out_bias,
    ]
    codes = dead_flags.shape[0]
    counts, slots, ckeep, csend, vec, w1 = run_prepare(
        place, code_ids.reshape(1, -1), dead_flags.reshape(1, -1), replace_ids.reshape(1, -1), latents,
        conv1_kernel.reshape(9 * ch, ch), vectors, owners,
    )
    own, to_chip, to_near, to_far, norm2, scale2, x, gy, w2, *weights = run_entry(
        place, mine, other, vec, w1, grad_out.reshape(images, px, ch), conv2_kernel.reshape(9 * ch, ch),
        (query_weight, key_weight, value_weight, out_weight), side,
    )
    acts = [own, links.partner(to_chip), links.send(to_near, 1), links.far(to_far)]
    out, dres, dkeep2, dsend2, stat_a, gkeep, gsend = run_attention(
        place, x, own, to_near, gy, ckeep, csend, vec, [w2] + weights, side
    )
    dres, dkeep2, dsend2, gsend, *acts[1:] = together(dres, dkeep2, dsend2, gsend, *acts[1:])
    grads2 = [dkeep2, links.partner(dsend2), links.send(dkeep2, 1), links.far(dsend2)]
    attn = (gkeep.astype(F32) + links.partner(gsend).astype(F32)).astype(BF)
    attn = attn.reshape((2, low) + attn.shape[1:])
    attn_keep, attn_send, dres = together(attn[0], attn[1], dres)
    attn_got = links.send(attn_send, 1)
    dkeep1, dsend1, dfull1, stat_b = run_back2(place, dres, norm2, scale2, vec, w2, side)
    grads2[0], stat_b = together(grads2[0], stat_b)
    grads1 = [dkeep1, links.partner(dsend1), links.send(dkeep1, 1), links.far(dsend1)]
    lead = links.lead()
    rest = range(1, len(lead))
    split = (lead[0], low // lead[0])

    def reduce(value, dims):
        for dim in dims:
            value = links.reduce(value, dim)
        return value

    def gather(value, dims):
        for dim in reversed(dims):
            value = links.gather(value, dim)
        return value

    def owned(value):
        return value.reshape((low,) + value.shape[-2:])

    sum2 = run_kernel_grad(place, 1, acts, grads2, split, side, "conv2_grad")
    sum2_keep, attn_got, grads1[0] = together(sum2, attn_got, grads1[0])
    sum1 = run_kernel_grad(place, 0, acts, grads1, split, side, "conv1_grad")
    attn = (attn_keep.astype(F32) + attn_got.astype(F32)).astype(BF)
    attn = attn.reshape(lead + attn.shape[1:])
    sum2 = sum2.reshape(lead + sum2.shape[2:])
    sum2_keep = sum2_keep.reshape(sum2.shape)
    sum1 = sum1.reshape(lead + sum1.shape[2:])
    attn = reduce(attn, [0])
    sum2 = links.reduce(sum2, 0, sum2_keep)
    attn, sum2, sum1, dfull1 = together(attn, sum2, sum1, dfull1)
    conv_rows = sum2.shape[-2]
    sum2 = reduce(jnp.concatenate([sum2, attn], axis=-2), rest)
    sum1 = reduce(sum1, [0])
    rows_out, in_send, stat_c = run_back1(place, dfull1, x, dres, vec, w1, side)
    sum2, sum1, in_send, stat_c = together(sum2, sum1, in_send, stat_c)
    vectors = jnp.concatenate([stat_c[:2], stat_b[2:3], stat_b[:2], stat_a[:6], counts[:1].reshape(-1, ch)])
    steps = links.small_steps()
    sum2 = gather(sum2, rest)
    in_got = links.partner(in_send)
    vectors = steps[0](vectors)
    sum2, sum1, in_got, vectors = together(sum2, sum1, in_got, vectors)
    sum2 = owned(gather(sum2, [0]))
    sum1 = reduce(sum1, rest)
    vectors = steps[1](vectors)
    input_grad, _ = run_place_rows(place, in_got, rows_out)
    sum2, sum1, vectors, input_grad = together(sum2, sum1, vectors, input_grad)
    far2 = links.send(sum2, 1)
    other2 = links.partner(sum2)
    sum1 = gather(sum1, rest)
    vectors = steps[2](vectors)
    grad2 = run_conv_finish(place, sum2, other2, None, ch, "conv2_finish")
    far2, sum1, vectors, grad2 = together(far2, sum1, vectors, grad2)
    sum1 = owned(gather(sum1, [0]))
    other_far2 = links.partner(far2)
    vectors = steps[3](vectors)
    sum1, vectors, other_far2 = together(sum1, vectors, other_far2)
    far1 = links.send(sum1, 1)
    other1 = links.partner(sum1)
    for step in steps[4:]:
        vectors = step(vectors)
    qg, kg, vg, og, new_codebook = run_attention_finish(
        place, (sum2, other2, far2, other_far2), slots, codebook, ch
    )
    grad2 = run_conv_finish(place, far2, other_far2, grad2, ch, "conv2_finish")
    grad1 = run_conv_finish(place, sum1, other1, None, ch, "conv1_finish")
    *vec_grads, usage, perplexity = run_vectors(vectors, 11, codes)
    (g1, b1, cb1, g2, b2, cb2, g3, b3, qb, vb, ob) = [v.reshape(ch) for v in vec_grads]
    far1, grad2, grad1, perplexity, new_codebook = together(far1, grad2, grad1, perplexity, new_codebook)
    grad1 = run_conv_finish(place, far1, links.partner(far1), grad1, ch, "conv1_finish")
    input_grad = input_grad.reshape(image_rows.shape)
    kernel_shape = (3, 3, ch, ch)
    return (
        out.reshape(grad_out.shape), input_grad,
        g1, b1, grad1.reshape(kernel_shape), cb1, g2, b2, grad2.reshape(kernel_shape), cb2, g3, b3,
        qg, qb, kg, vg, vb, og, ob,
        new_codebook, usage.reshape(codes), perplexity.reshape(()),
    )


def solution(mesh):
    both = ("grp", "row")
    in_specs = (
        P("grp", "row", None, None), P(both, None, None, None), P(both), P(), P(), P(both, None), P(both, None),
    ) + (P(),) * 17
    out_specs = (P(both, None, None, None), P("grp", "row", None, None)) + (P(),) * 17 + (P(both, None), P(), P())
    body = functools.partial(local, chips=mesh.shape["grp"])
    return jax.shard_map(body, mesh=mesh, in_specs=in_specs, out_specs=out_specs, check_vma=False)
```

time: 293 us -> 175 us (0.60)
  waiting for transfers between devices: 122 us -> 74 us
  local copies, waits for them, and re-layouts: 32.6 us -> 1.77 us
  Pallas kernels: 72.7 us -> 56.7 us
  starting transfers between devices: 53 us -> 38.7 us
  other arithmetic: 9.41 us -> 2.23 us
    ppermute x32 -> x27, waiting for transfers between devices: 121 us -> 70.3 us  [send(): return lax.ppermute(value, AXES, pairs)]
    ppermute x32 -> x27, starting transfers between devices: 50.1 us -> 31.1 us  [send(): return lax.ppermute(value, AXES, pairs)]
    pallas_call x8 -> x11, Pallas kernels: 60.9 us -> 46 us  [the longest x4 10.9 us: run_conv_finish(): pl.pallas_call(functools.partial(conv_finish_body, far=len(given)), name=...]
    slice x21 -> x2, local copies, waits for them, and re-layouts: 13.3 us -> 0.09 us  [the longest x1 0.07 us: local(): attn_keep, attn_send, dres = together(attn[0], attn[1], dres)]
    unnamed x40 -> x7, local copies, waits for them, and re-layouts: 10.7 us -> 0.06 us
    another operation x12 -> x1, local copies, waits for them, and re-layouts: 7.56 us -> 0.08 us  [local(): jnp.stack([core, chip, device * latents.shape[0], device, mine_at, other_...]
    ppermute x0 -> x3, starting transfers between devices: none -> 5.3 us  [far(): return lax.ppermute(value, AXES, pairs)]
    concatenate x15 -> x0, other arithmetic: 5.09 us -> none  [the longest x10 3.45 us: gather(): jnp.concatenate([value] + [self.send(value, k << shift) for k in range(1,...]
  transfers between devices with their start and end apart: 44 -> 41, of which waited for: 19 -> 19; matrix products, arithmetic and copies ran while one was open for 8% -> 1% of each run, Pallas kernels for 12% -> 27%
where the time goes in v2:
time: 175 us
  waiting for transfers between devices  74 us (42%)
  Pallas kernels  56.7 us (32%)
  starting transfers between devices  38.7 us (22%)
  other arithmetic  2.23 us (1%)
  local copies, waits for them, and re-layouts  1.77 us (1%)
    ppermute x27, waiting for transfers between devices, send(): return lax.ppermute(value, AXES, pairs)  70.3 us
    ppermute x27, starting transfers between devices, send(): return lax.ppermute(value, AXES, pairs)  31.1 us
    pallas_call x4, Pallas kernels, run_conv_finish(): pl.pallas_call(functools.partial(conv_finish_body, far=len(given)), name=...  10.9 us
    pallas_call x1, Pallas kernels, run_attention(): pl.pallas_call(functools.partial(attention_body, side=side), name='attent...  10.3 us
    pallas_call x2, Pallas kernels, run_kernel_grad(): pl.pallas_call(functools.partial(kernel_grad_body, side=side, which=which...  9.18 us
    pallas_call x1, Pallas kernels, run_entry(): pl.pallas_call(functools.partial(entry_body, side=side), name='entry', in...  6.76 us
    ppermute x3, starting transfers between devices, far(): return lax.ppermute(value, AXES, pairs)  5.3 us
    pallas_call x1, Pallas kernels, run_back1(): pl.pallas_call(functools.partial(back1_body, side=side), name='conv1_back...  4.89 us
  transfers between devices with their start and end apart: 41, of which 19 were waited for; matrix products, arithmetic and copies ran while one was open for 1% of the time, Pallas kernels for 27%

profile of v2, /device:TPU:0, one launch (start us, length us, event | category | flops | bytes accessed | tf_op | source)
XLA Modules:
  0.0 174.6 jit_solution(18400744981253331738)
XLA Ops:
  2.2 3.3 %prepare.1 = (f32[8,1024]{1,0:T(8,128)S(1)}, bf16[256,1024]{1,0:T(8,128)(2,1)S(1)}, bf16[16,8,256]{2,1,0:T(8,128)(2,1)S(1)}, bf16[16,8,256]{2,1,0:T(8,128)(2,1)S...) custom-call(s32[9]{0:T(128)S(1)} %stack.87.place_ref, s32[1,512]{1,0:T(1,128)} %bitcast.107, ...), custom_call_target="tpu_custom_call" | custom-call | flops 2529999872 | bytes 1048576 | tf_op jit(solution)/shard_map/prepare/pallas_call | solution.py:558
  5.5 6.8 %entry.1 = (bf16[2,2,256,256]{3,2,1,0:T(8,128)(2,1)S(1)}, bf16[2,2,256,256]{3,2,1,0:T(8,128)(2,1)S(1)}, bf16[2,2,256,256]{3,2,1,0:T(8,128)(2,1)S(1)}, bf16[2,2,2...) custom-call(s32[9]{0:T(128)S(1)} %stack.87.place_ref, ...), custom_call_target="tpu_custom_call" | custom-call | flops 9774999552 | bytes 1048576 | tf_op jit(solution)/shard_map/entry/pallas_call | solution.py:194
  12.5 2.6 %collective-permute-start.3 = (bf16[2,2,256,256]{3,2,1,0:T(8,128)(2,1)S(1)}, bf16[2,2,256,256]{3,2,1,0:T(8,128)(2,1)S(1)}, u32[]{:S(2)}, u32[]{:S(2)}) collective-permute-start(bf16[2,2,256,256]{3,2,1,0:T(8,128)(2,1)S(1)} %get-tuple-element.137), channel_id=1, source_target_pairs={{0,5},{1,2},{2,7},{3,0},{4,1},{5,6},{6,3},{7,4},{8,13},{9,10},{10,... | collective-permute-start | bytes 1572872 | tf_op jit(solution)/shard_map/ppermute | solution.py:730
  16.6 10.3 %attention.1 = (bf16[2,256,512]{2,1,0:T(8,128)(2,1)}, f32[2,256,512]{2,1,0:T(8,128)S(1)}, bf16[2,256,256]{2,1,0:T(8,128)(2,1)S(1)}, bf16[2,256,256]{2,1,0:T(8,12...) custom-call(s32[9]{0:T(128)S(1)} %stack.87.place_ref, ...), custom_call_target="tpu_custom_call" | custom-call | flops 15525000192 | bytes 1048576 | tf_op jit(solution)/shard_map/attention/pallas_call | solution.py:302
  28.0 1.7 collective-permute-start.7
  31.7 4.3 %conv2_back.1 = (bf16[2,256,256]{2,1,0:T(8,128)(2,1)S(1)}, bf16[2,256,256]{2,1,0:T(8,128)(2,1)S(1)}, bf16[2,256,512]{2,1,0:T(8,128)(2,1)S(1)}, f32[8,512]{1,0:T(8,128)S(1)}) custom-call(s32[9]{0:T(128)S(1)} %stack.87.place_ref, f32[2,256,512]{2,1,0:T(8,128)S(1)} %get-tuple-element.145.dres_ref, f32[2,256,512]{2,1,0:T(8,128)S(1)} %get-tuple-element.146.norm2_ref, ...), custom_call_target="tpu_custom_call" | custom-call | flops 5750000128 | bytes 1048576 | tf_op jit(solution)/shard_map/conv2_back/pallas_call | solution.py:364
  39.3 4.6 %conv2_grad.1 = bf16[2,4,288,256]{3,2,1,0:T(8,128)(2,1)S(1)} custom-call(s32[9]{0:T(128)S(1)} %stack.87.place_ref, bf16[2,2,256,256]{3,2,1,0:T(8,128)(2,1)S(1)} %get-tuple-element.120.own_ref.refs_0_, bf16[2,2,256,256]{3,2,1,0:T(8,128)(2,1)S(1)} %collective-permute-done.1.refs_1_, bf16[2,2,256,256]{3,2,1,0:T(8,128)(2,1)S(1)} %collective-permute-done.2.refs_2_, ...), custom_call_target="tpu_custom_call" | custom-call | flops 5520000000 | bytes 1048576 | tf_op jit(solution)/shard_map/conv2_grad/pallas_call | solution.py:489
  45.5 9.4 %collective-permute-done.8 = bf16[8,136,256]{2,1,0:T(8,128)(2,1)S(1)} collective-permute-done((bf16[8,136,256]{2,1,0:T(8,128)(2,1)S(1)}, bf16[8,136,256]{2,1,0:T(8,128)(2,1)S(1)}, u32[]{:S(2)}, u32[]{:S(2)}) %collective-permute-start.8) | collective-permute-done | bytes 557088 | tf_op jit(solution)/shard_map/ppermute | solution.py:722
  56.1 4.6 %conv1_grad.1 = bf16[2,4,288,256]{3,2,1,0:T(8,128)(2,1)S(1)} custom-call(s32[9]{0:T(128)S(1)} %stack.87.place_ref, bf16[2,2,256,256]{3,2,1,0:T(8,128)(2,1)S(1)} %get-tuple-element.120.own_ref.refs_0_, bf16[2,2,256,256]{3,2,1,0:T(8,128)(2,1)S(1)} %collective-permute-done.1.refs_1_, bf16[2,2,256,256]{3,2,1,0:T(8,128)(2,1)S(1)} %collective-permute-done.2.refs_2_, ...), custom_call_target="tpu_custom_call" | custom-call | flops 5520000000 | bytes 1048576 | tf_op jit(solution)/shard_map/conv1_grad/pallas_call | solution.py:489
  64.6 2.5 %collective-permute-start.16 = (bf16[424,256]{1,0:T(8,128)(2,1)S(1)}, bf16[424,256]{1,0:T(8,128)(2,1)S(1)}, u32[]{:S(2)}, u32[]{:S(2)}) collective-permute-start(bf16[424,256]{1,0:T(8,128)(2,1)S(1)} %get-tuple-element.215), channel_id=1, source_target_pairs={{0,24},{1,25},{2,26},{3,27},{4,28},{5,29},{6,30},{7,31},{8,16},{9,... | collective-permute-start | bytes 651272 | tf_op jit(solution)/shard_map/ppermute | solution.py:722
  67.2 4.9 %conv1_back.1 = (bf16[4,128,512]{2,1,0:T(8,128)(2,1)}, bf16[2,128,512]{2,1,0:T(8,128)(2,1)S(1)}, f32[8,512]{1,0:T(8,128)S(1)}) custom-call(s32[9]{0:T(128)S(1)} %stack.87.place_ref, bf16[2,256,512]{2,1,0:T(8,128)(2,1)S(1)} %get-tuple-element.161.dfull_ref, bf16[2,256,512]{2,1,0:T(8,128)(2,1)S(1)} %get-tuple-element.119.x_ref, ...), custom_call_target="tpu_custom_call" | custom-call | flops 6209999872 | bytes 1048576 | tf_op jit(solution)/shard_map/conv1_back/pallas_call | solution.py:412
  72.1 5.6 %collective-permute-done.16 = bf16[424,256]{1,0:T(8,128)(2,1)S(1)} collective-permute-done((bf16[424,256]{1,0:T(8,128)(2,1)S(1)}, bf16[424,256]{1,0:T(8,128)(2,1)S(1)}, u32[]{:S(2)}, u32[]{:S(2)}) %collective-permute-start.16) | collective-permute-done | bytes 217120 | tf_op jit(solution)/shard_map/ppermute | solution.py:722
  77.7 7.1 %collective-permute-done.15 = bf16[424,256]{1,0:T(8,128)(2,1)S(1)} collective-permute-done((bf16[424,256]{1,0:T(8,128)(2,1)S(1)}, bf16[424,256]{1,0:T(8,128)(2,1)S(1)}, u32[]{:S(2)}, u32[]{:S(2)}) %collective-permute-start.15) | collective-permute-done | bytes 217120 | tf_op jit(solution)/shard_map/ppermute | solution.py:722
  85.1 3.5 %collective-permute-start.20 = (bf16[424,256]{1,0:T(8,128)(2,1)S(1)}, bf16[424,256]{1,0:T(8,128)(2,1)S(1)}, u32[]{:S(2)}, u32[]{:S(2)}) collective-permute-start(bf16[424,256]{1,0:T(8,128)(2,1)S(1)} %fusion.4), channel_id=1, source_target_pairs={{0,24},{1,25},{2,26},{3,27},{4,28},{5,29},{6,30},{7,31},{8,16},{9,... | collective-permute-start | bytes 651272 | tf_op jit(solution)/shard_map/ppermute | solution.py:722
  91.4 3.8 %collective-permute-done.20 = bf16[424,256]{1,0:T(8,128)(2,1)S(1)} collective-permute-done((bf16[424,256]{1,0:T(8,128)(2,1)S(1)}, bf16[424,256]{1,0:T(8,128)(2,1)S(1)}, u32[]{:S(2)}, u32[]{:S(2)}) %collective-permute-start.20) | collective-permute-done | bytes 217120 | tf_op jit(solution)/shard_map/ppermute | solution.py:722
  95.3 8.7 %collective-permute-done.19 = bf16[424,256]{1,0:T(8,128)(2,1)S(1)} collective-permute-done((bf16[424,256]{1,0:T(8,128)(2,1)S(1)}, bf16[424,256]{1,0:T(8,128)(2,1)S(1)}, u32[]{:S(2)}, u32[]{:S(2)}) %collective-permute-start.19) | collective-permute-done | bytes 217120 | tf_op jit(solution)/shard_map/ppermute | solution.py:722
  105.8 2.2 %collective-permute-start.26 = (bf16[288,256]{1,0:T(8,128)(2,1)S(1)}, bf16[288,256]{1,0:T(8,128)(2,1)S(1)}, u32[]{:S(2)}, u32[]{:S(2)}) collective-permute-start(bf16[288,256]{1,0:T(8,128)(2,1)S(1)} %get-tuple-element.218), channel_id=1, source_target_pairs={{0,24},{1,25},{2,26},{3,27},{4,28},{5,29},{6,30},{7,31},{8,16},{9,... | collective-permute-start | bytes 442376 | tf_op jit(solution)/shard_map/ppermute | solution.py:722
  110.1 1.8 %place_rows.1 = (bf16[4,128,512]{2,1,0:T(8,128)(2,1)}, f32[8,128]{1,0:T(8,128)}) custom-call(s32[9]{0:T(128)S(1)} %stack.87.place_ref, bf16[2,128,512]{2,1,0:T(8,128)(2,1)S(1)} %collective-permute-done.21.got_ref, bf16[4,128,512]{2,1,0:T(8,128)(2,1)} %get-tuple-element.175.into_hbm), custom_call_target="tpu_custom_call", output_to_operand_aliasing={{0}: (2, {})} | custom-call | flops 1150000000 | bytes 1048576 | tf_op jit(solution)/shard_map/place_rows/pallas_call | solution.py:437
  114.0 5.6 %collective-permute-done.25 = bf16[288,256]{1,0:T(8,128)(2,1)S(1)} collective-permute-done((bf16[288,256]{1,0:T(8,128)(2,1)S(1)}, bf16[288,256]{1,0:T(8,128)(2,1)S(1)}, u32[]{:S(2)}, u32[]{:S(2)}) %collective-permute-start.25) | collective-permute-done | bytes 147488 | tf_op jit(solution)/shard_map/ppermute | solution.py:722
  122.0 2.6 %collective-permute-start.31 = (bf16[288,256]{1,0:T(8,128)(2,1)S(1)}, bf16[288,256]{1,0:T(8,128)(2,1)S(1)}, u32[]{:S(2)}, u32[]{:S(2)}) collective-permute-start(bf16[288,256]{1,0:T(8,128)(2,1)S(1)} %fusion.7), channel_id=1, source_target_pairs={{0,24},{1,25},{2,26},{3,27},{4,28},{5,29},{6,30},{7,31},{8,16},{9,... | collective-permute-start | bytes 442376 | tf_op jit(solution)/shard_map/ppermute | solution.py:722
  126.4 4.2 %collective-permute-done.31 = bf16[288,256]{1,0:T(8,128)(2,1)S(1)} collective-permute-done((bf16[288,256]{1,0:T(8,128)(2,1)S(1)}, bf16[288,256]{1,0:T(8,128)(2,1)S(1)}, u32[]{:S(2)}, u32[]{:S(2)}) %collective-permute-start.31) | collective-permute-done | bytes 147488 | tf_op jit(solution)/shard_map/ppermute | solution.py:722
  130.6 5.8 %collective-permute-done.30 = bf16[288,256]{1,0:T(8,128)(2,1)S(1)} collective-permute-done((bf16[288,256]{1,0:T(8,128)(2,1)S(1)}, bf16[288,256]{1,0:T(8,128)(2,1)S(1)}, u32[]{:S(2)}, u32[]{:S(2)}) %collective-permute-start.30) | collective-permute-done | bytes 147488 | tf_op jit(solution)/shard_map/ppermute | solution.py:722
  136.5 2.7 %conv2_finish.2.refs_0_ = f32[9,512,512]{2,1,0:T(8,128)} custom-call(s32[9]{0:T(128)S(1)} %stack.87.place_ref, bf16[8,424,256]{2,1,0:T(8,128)(2,1)S(1)} %bitcast.80, bf16[8,424,256]{2,1,0:T(8,128)(2,1)S(1)} %collective-permute-done.33.other.other0), custom_call_target="tpu_custom_call" | custom-call | flops 4024999936 | bytes 1048576 | tf_op jit(solution)/shard_map/conv2_finish/pallas_call | solution.py:653
  139.2 3.3 %collective-permute-done.28.mine.mine1 = bf16[8,424,256]{2,1,0:T(8,128)(2,1)S(1)} collective-permute-done((bf16[8,424,256]{2,1,0:T(8,128)(2,1)S(1)}, bf16[8,424,256]{2,1,0:T(8,128)(2,1)S(1)}, u32[]{:S(2)}, u32[]{:S(2)}) %collective-permute-start.28) | collective-permute-done | bytes 1736736 | tf_op jit(solution)/shard_map/ppermute | solution.py:722
  143.6 3.9 %collective-permute-done.35 = f32[13,512]{1,0:T(8,128)S(1)} collective-permute-done((f32[13,512]{1,0:T(8,128)S(1)}, f32[13,512]{1,0:T(8,128)S(1)}, u32[]{:S(2)}, u32[]{:S(2)}) %collective-permute-start.35) | collective-permute-done | bytes 26656 | tf_op jit(solution)/shard_map/ppermute | solution.py:722
  147.5 4.9 %collective-permute-done.34 = bf16[4,288,256]{2,1,0:T(8,128)(2,1)S(1)} collective-permute-done((bf16[4,288,256]{2,1,0:T(8,128)(2,1)S(1)}, bf16[4,288,256]{2,1,0:T(8,128)(2,1)S(1)}, u32[]{:S(2)}, u32[]{:S(2)}) %collective-permute-start.34) | collective-permute-done | bytes 589856 | tf_op jit(solution)/shard_map/ppermute | solution.py:722
  153.9 2.7 %conv2_finish.3 = f32[9,512,512]{2,1,0:T(8,128)} custom-call(s32[9]{0:T(128)S(1)} %stack.87.place_ref, bf16[8,424,256]{2,1,0:T(8,128)(2,1)S(1)} %collective-permute-done.28.mine.mine1, bf16[8,424,256]{2,1,0:T(8,128)(2,1)S(1)} %collective-permute-done.36.other.other1, f32[9,512,512]{2,1,0:T(8,128)} %conv2_finish.2.refs_0_), custom_call_target="tpu_custom_call", output_to_operand_aliasing={{}: (3, {})} | custom-call | flops 4024999936 | bytes 1048576 | tf_op jit(solution)/shard_map/conv2_finish/pallas_call | solution.py:653
  156.6 3.7 %attention_finish.1 = (f32[512,512]{1,0:T(8,128)}, f32[512,512]{1,0:T(8,128)}, f32[512,512]{1,0:T(8,128)}, f32[512,512]{1,0:T(8,128)}, f32[32,256]{1,0:T(8,128)}) custom-call(s32[9]{0:T(128)S(1)} %stack.87.place_ref, bf16[8,424,256]{2,1,0:T(8,128)(2,1)S(1)} %bitcast.81, bf16[8,424,256]{2,1,0:T(8,128)(2,1)S(1)} %collective-permute-done.33.other.other0, ...), custom_call_target="tpu_custom_call" | custom-call | flops 3449999872 | bytes 1048576 | tf_op jit(solution)/shard_map/attention_finish/pallas_call | solution.py:628
  162.4 2.7 %conv1_finish.2.refs_0_ = f32[9,512,512]{2,1,0:T(8,128)} custom-call(s32[9]{0:T(128)S(1)} %stack.87.place_ref, bf16[8,288,256]{2,1,0:T(8,128)(2,1)S(1)} %bitcast.84, bf16[8,288,256]{2,1,0:T(8,128)(2,1)S(1)} %collective-permute-done.39.other), custom_call_target="tpu_custom_call" | custom-call | flops 4024999936 | bytes 1048576 | tf_op jit(solution)/shard_map/conv1_finish/pallas_call | solution.py:653
  165.2 3.7 %collective-permute-done.38.mine = bf16[8,288,256]{2,1,0:T(8,128)(2,1)S(1)} collective-permute-done((bf16[8,288,256]{2,1,0:T(8,128)(2,1)S(1)}, bf16[8,288,256]{2,1,0:T(8,128)(2,1)S(1)}, u32[]{:S(2)}, u32[]{:S(2)}) %collective-permute-start.38) | collective-permute-done | bytes 1179680 | tf_op jit(solution)/shard_map/ppermute | solution.py:722
  168.9 2.8 %collective-permute-done.40.other = bf16[8,288,256]{2,1,0:T(8,128)(2,1)S(1)} collective-permute-done((bf16[8,288,256]{2,1,0:T(8,128)(2,1)S(1)}, bf16[8,288,256]{2,1,0:T(8,128)(2,1)S(1)}, u32[]{:S(2)}, u32[]{:S(2)}) %collective-permute-start.40) | collective-permute-done | bytes 1179680 | tf_op jit(solution)/shard_map/ppermute | solution.py:726
  171.7 2.7 %conv1_finish.3 = f32[9,512,512]{2,1,0:T(8,128)} custom-call(s32[9]{0:T(128)S(1)} %stack.87.place_ref, bf16[8,288,256]{2,1,0:T(8,128)(2,1)S(1)} %collective-permute-done.38.mine, bf16[8,288,256]{2,1,0:T(8,128)(2,1)S(1)} %collective-permute-done.40.other, f32[9,512,512]{2,1,0:T(8,128)} %conv1_finish.2.refs_0_), custom_call_target="tpu_custom_call", output_to_operand_aliasing={{}: (3, {})} | custom-call | flops 4024999936 | bytes 1048576 | tf_op jit(solution)/shard_map/conv1_finish/pallas_call | solution.py:653
  (102 shorter events, 34.2 us)
Async XLA Ops:
  12.3 14.6 %collective-permute-start.1 = (bf16[2,2,256,256]{3,2,1,0:T(8,128)(2,1)S(1)}, bf16[2,2,256,256]{3,2,1,0:T(8,128)(2,1)S(1)}, u32[]{:S(2)}, u32[]{:S(2)}) collective-permute-start(bf16[2,2,256,256]{3,2,1,0:T(8,128)(2,1)S(1)} %get-tuple-element.136), channel_id=1, source_target_pairs={{0,1},{1,0},{2,3},{3,2},{4,5},{5,4},{6,7},{7,6},{8,9},{9,8},{10,11... | collective-permute-start | bytes 1572872 | tf_op jit(solution)/shard_map/ppermute | solution.py:726
  12.5 14.5 %collective-permute-start.3 = (bf16[2,2,256,256]{3,2,1,0:T(8,128)(2,1)S(1)}, bf16[2,2,256,256]{3,2,1,0:T(8,128)(2,1)S(1)}, u32[]{:S(2)}, u32[]{:S(2)}) collective-permute-start(bf16[2,2,256,256]{3,2,1,0:T(8,128)(2,1)S(1)} %get-tuple-element.137), channel_id=1, source_target_pairs={{0,5},{1,2},{2,7},{3,0},{4,1},{5,6},{6,3},{7,4},{8,13},{9,10},{10,... | collective-permute-start | bytes 1572872 | tf_op jit(solution)/shard_map/ppermute | solution.py:730
  15.1 12.5 %collective-permute-start.2 = (bf16[2,2,256,256]{3,2,1,0:T(8,128)(2,1)S(1)}, bf16[2,2,256,256]{3,2,1,0:T(8,128)(2,1)S(1)}, u32[]{:S(2)}, u32[]{:S(2)}) collective-permute-start(bf16[2,2,256,256]{3,2,1,0:T(8,128)(2,1)S(1)} %get-tuple-element.121.near_ref), channel_id=1, source_target_pairs={{0,2},{1,5},{2,0},{3,7},{4,6},{5,1},{6,4},{7,3},{8,10},{9,13},{10,... | collective-permute-start | bytes 1572872 | tf_op jit(solution)/shard_map/ppermute | solution.py:722
  28.0 10.4 %collective-permute-start.7 = (bf16[2,256,256]{2,1,0:T(8,128)(2,1)S(1)}, bf16[2,256,256]{2,1,0:T(8,128)(2,1)S(1)}, u32[]{:S(2)}, u32[]{:S(2)}) collective-permute-start(bf16[2,256,256]{2,1,0:T(8,128)(2,1)S(1)} %get-tuple-element.150), channel_id=1, source_target_pairs={{0,5},{1,2},{2,7},{3,0},{4,1},{5,6},{6,3},{7,4},{8,13},{9,10},{10,... | collective-permute-start | bytes 786440 | tf_op jit(solution)/shard_map/ppermute | solution.py:730
  29.8 9.5 %collective-permute-start.5 = (bf16[2,256,256]{2,1,0:T(8,128)(2,1)S(1)}, bf16[2,256,256]{2,1,0:T(8,128)(2,1)S(1)}, u32[]{:S(2)}, u32[]{:S(2)}) collective-permute-start(bf16[2,256,256]{2,1,0:T(8,128)(2,1)S(1)} %get-tuple-element.150), channel_id=1, source_target_pairs={{0,1},{1,0},{2,3},{3,2},{4,5},{5,4},{6,7},{7,6},{8,9},{9,8},{10,11... | collective-permute-start | bytes 786440 | tf_op jit(solution)/shard_map/ppermute | solution.py:726
  29.8 7.4 %collective-permute-start.6 = (bf16[2,256,256]{2,1,0:T(8,128)(2,1)S(1)}, bf16[2,256,256]{2,1,0:T(8,128)(2,1)S(1)}, u32[]{:S(2)}, u32[]{:S(2)}) collective-permute-start(bf16[2,256,256]{2,1,0:T(8,128)(2,1)S(1)} %get-tuple-element.149.refs_4_), channel_id=1, source_target_pairs={{0,2},{1,5},{2,0},{3,7},{4,6},{5,1},{6,4},{7,3},{8,10},{9,13},{10,... | collective-permute-start | bytes 786440 | tf_op jit(solution)/shard_map/ppermute | solution.py:722
  36.0 20.1 %collective-permute-start.13 = (bf16[2,256,256]{2,1,0:T(8,128)(2,1)S(1)}, bf16[2,256,256]{2,1,0:T(8,128)(2,1)S(1)}, u32[]{:S(2)}, u32[]{:S(2)}) collective-permute-start(bf16[2,256,256]{2,1,0:T(8,128)(2,1)S(1)} %get-tuple-element.156), channel_id=1, source_target_pairs={{0,5},{1,2},{2,7},{3,0},{4,1},{5,6},{6,3},{7,4},{8,13},{9,10},{10,... | collective-permute-start | bytes 786440 | tf_op jit(solution)/shard_map/ppermute | solution.py:730
  36.9 19.2 %collective-permute-start.11 = (bf16[2,256,256]{2,1,0:T(8,128)(2,1)S(1)}, bf16[2,256,256]{2,1,0:T(8,128)(2,1)S(1)}, u32[]{:S(2)}, u32[]{:S(2)}) collective-permute-start(bf16[2,256,256]{2,1,0:T(8,128)(2,1)S(1)} %get-tuple-element.156), channel_id=1, source_target_pairs={{0,1},{1,0},{2,3},{3,2},{4,5},{5,4},{6,7},{7,6},{8,9},{9,8},{10,11... | collective-permute-start | bytes 786440 | tf_op jit(solution)/shard_map/ppermute | solution.py:726
  37.3 18.9 %collective-permute-start.12 = (bf16[2,256,256]{2,1,0:T(8,128)(2,1)S(1)}, bf16[2,256,256]{2,1,0:T(8,128)(2,1)S(1)}, u32[]{:S(2)}, u32[]{:S(2)}) collective-permute-start(bf16[2,256,256]{2,1,0:T(8,128)(2,1)S(1)} %get-tuple-element.155.refs_4_), channel_id=1, source_target_pairs={{0,2},{1,5},{2,0},{3,7},{4,6},{5,1},{6,4},{7,3},{8,10},{9,13},{10,... | collective-permute-start | bytes 786440 | tf_op jit(solution)/shard_map/ppermute | solution.py:722
  38.4 16.5 %collective-permute-start.8 = (bf16[8,136,256]{2,1,0:T(8,128)(2,1)S(1)}, bf16[8,136,256]{2,1,0:T(8,128)(2,1)S(1)}, u32[]{:S(2)}, u32[]{:S(2)}) collective-permute-start(bf16[8,136,256]{2,1,0:T(8,128)(2,1)S(1)} %get-tuple-element.151), channel_id=1, source_target_pairs={{0,2},{1,5},{2,0},{3,7},{4,6},{5,1},{6,4},{7,3},{8,10},{9,13},{10,... | collective-permute-start | bytes 1671176 | tf_op jit(solution)/shard_map/ppermute | solution.py:722
  43.9 16.8 %collective-permute-start.10 = (bf16[4,288,256]{2,1,0:T(8,128)(2,1)S(1)}, bf16[4,288,256]{2,1,0:T(8,128)(2,1)S(1)}, u32[]{:S(2)}, u32[]{:S(2)}) collective-permute-start(bf16[4,288,256]{2,1,0:T(8,128)(2,1)S(1)} %slice_bitcast_fusion), channel_id=1, source_target_pairs={{0,4},{1,3},{2,6},{3,1},{4,0},{5,7},{6,2},{7,5},{8,12},{9,11},{10,... | collective-permute-start | bytes 1769480 | tf_op jit(solution)/shard_map/ppermute | solution.py:722
  61.9 23.0 %collective-permute-start.17 = (bf16[4,288,256]{2,1,0:T(8,128)(2,1)S(1)}, bf16[4,288,256]{2,1,0:T(8,128)(2,1)S(1)}, u32[]{:S(2)}, u32[]{:S(2)}) collective-permute-start(bf16[4,288,256]{2,1,0:T(8,128)(2,1)S(1)} %slice_bitcast_fusion.1), channel_id=1, source_target_pairs={{0,4},{1,3},{2,6},{3,1},{4,0},{5,7},{6,2},{7,5},{8,12},{9,11},{10,... | collective-permute-start | bytes 1769480 | tf_op jit(solution)/shard_map/ppermute | solution.py:722
  63.0 9.1 %collective-permute-start.14 = (bf16[424,256]{1,0:T(8,128)(2,1)S(1)}, bf16[424,256]{1,0:T(8,128)(2,1)S(1)}, u32[]{:S(2)}, u32[]{:S(2)}) collective-permute-start(bf16[424,256]{1,0:T(8,128)(2,1)S(1)} %get-tuple-element.214), channel_id=1, source_target_pairs={{0,8},{1,9},{2,10},{3,11},{4,12},{5,13},{6,14},{7,15},{8,0},{9,1},... | collective-permute-start | bytes 651272 | tf_op jit(solution)/shard_map/ppermute | solution.py:722
  64.6 13.1 %collective-permute-start.16 = (bf16[424,256]{1,0:T(8,128)(2,1)S(1)}, bf16[424,256]{1,0:T(8,128)(2,1)S(1)}, u32[]{:S(2)}, u32[]{:S(2)}) collective-permute-start(bf16[424,256]{1,0:T(8,128)(2,1)S(1)} %get-tuple-element.215), channel_id=1, source_target_pairs={{0,24},{1,25},{2,26},{3,27},{4,28},{5,29},{6,30},{7,31},{8,16},{9,... | collective-permute-start | bytes 651272 | tf_op jit(solution)/shard_map/ppermute | solution.py:722
  67.1 17.7 %collective-permute-start.15 = (bf16[424,256]{1,0:T(8,128)(2,1)S(1)}, bf16[424,256]{1,0:T(8,128)(2,1)S(1)}, u32[]{:S(2)}, u32[]{:S(2)}) collective-permute-start(bf16[424,256]{1,0:T(8,128)(2,1)S(1)} %get-tuple-element.216), channel_id=1, source_target_pairs={{0,16},{1,17},{2,18},{3,19},{4,20},{5,21},{6,22},{7,23},{8,24},{9,... | collective-permute-start | bytes 651272 | tf_op jit(solution)/shard_map/ppermute | solution.py:722
  85.1 10.1 %collective-permute-start.20 = (bf16[424,256]{1,0:T(8,128)(2,1)S(1)}, bf16[424,256]{1,0:T(8,128)(2,1)S(1)}, u32[]{:S(2)}, u32[]{:S(2)}) collective-permute-start(bf16[424,256]{1,0:T(8,128)(2,1)S(1)} %fusion.4), channel_id=1, source_target_pairs={{0,24},{1,25},{2,26},{3,27},{4,28},{5,29},{6,30},{7,31},{8,16},{9,... | collective-permute-start | bytes 651272 | tf_op jit(solution)/shard_map/ppermute | solution.py:722
  88.6 15.4 %collective-permute-start.19 = (bf16[424,256]{1,0:T(8,128)(2,1)S(1)}, bf16[424,256]{1,0:T(8,128)(2,1)S(1)}, u32[]{:S(2)}, u32[]{:S(2)}) collective-permute-start(bf16[424,256]{1,0:T(8,128)(2,1)S(1)} %fusion.4), channel_id=1, source_target_pairs={{0,16},{1,17},{2,18},{3,19},{4,20},{5,21},{6,22},{7,23},{8,24},{9,... | collective-permute-start | bytes 651272 | tf_op jit(solution)/shard_map/ppermute | solution.py:722
  88.6 15.4 %collective-permute-start.18 = (bf16[424,256]{1,0:T(8,128)(2,1)S(1)}, bf16[424,256]{1,0:T(8,128)(2,1)S(1)}, u32[]{:S(2)}, u32[]{:S(2)}) collective-permute-start(bf16[424,256]{1,0:T(8,128)(2,1)S(1)} %fusion.4), channel_id=1, source_target_pairs={{0,8},{1,9},{2,10},{3,11},{4,12},{5,13},{6,14},{7,15},{8,0},{9,1},... | collective-permute-start | bytes 651272 | tf_op jit(solution)/shard_map/ppermute | solution.py:722
  89.6 14.5 %collective-permute-start.21 = (bf16[2,128,512]{2,1,0:T(8,128)(2,1)S(1)}, bf16[2,128,512]{2,1,0:T(8,128)(2,1)S(1)}, u32[]{:S(2)}, u32[]{:S(2)}) collective-permute-start(bf16[2,128,512]{2,1,0:T(8,128)(2,1)S(1)} %get-tuple-element.166), channel_id=1, source_target_pairs={{0,1},{1,0},{2,3},{3,2},{4,5},{5,4},{6,7},{7,6},{8,9},{9,8},{10,11... | collective-permute-start | bytes 786440 | tf_op jit(solution)/shard_map/ppermute | solution.py:726
  104.1 15.5 %collective-permute-start.23 = (bf16[4,424,256]{2,1,0:T(8,128)(2,1)S(1)}, bf16[4,424,256]{2,1,0:T(8,128)(2,1)S(1)}, u32[]{:S(2)}, u32[]{:S(2)}) collective-permute-start(bf16[4,424,256]{2,1,0:T(8,128)(2,1)S(1)} %pad_maximum_fusion.2), channel_id=1, source_target_pairs={{0,4},{1,3},{2,6},{3,1},{4,0},{5,7},{6,2},{7,5},{8,12},{9,11},{10,... | collective-permute-start | bytes 2605064 | tf_op jit(solution)/shard_map/ppermute | solution.py:722
  105.8 7.9 %collective-permute-start.24 = (bf16[288,256]{1,0:T(8,128)(2,1)S(1)}, bf16[288,256]{1,0:T(8,128)(2,1)S(1)}, u32[]{:S(2)}, u32[]{:S(2)}) collective-permute-start(bf16[288,256]{1,0:T(8,128)(2,1)S(1)} %get-tuple-element.217), channel_id=1, source_target_pairs={{0,8},{1,9},{2,10},{3,11},{4,12},{5,13},{6,14},{7,15},{8,0},{9,1},... | collective-permute-start | bytes 442376 | tf_op jit(solution)/shard_map/ppermute | solution.py:722
  105.8 8.1 %collective-permute-start.26 = (bf16[288,256]{1,0:T(8,128)(2,1)S(1)}, bf16[288,256]{1,0:T(8,128)(2,1)S(1)}, u32[]{:S(2)}, u32[]{:S(2)}) collective-permute-start(bf16[288,256]{1,0:T(8,128)(2,1)S(1)} %get-tuple-element.218), channel_id=1, source_target_pairs={{0,24},{1,25},{2,26},{3,27},{4,28},{5,29},{6,30},{7,31},{8,16},{9,... | collective-permute-start | bytes 442376 | tf_op jit(solution)/shard_map/ppermute | solution.py:722
  108.0 11.5 %collective-permute-start.25 = (bf16[288,256]{1,0:T(8,128)(2,1)S(1)}, bf16[288,256]{1,0:T(8,128)(2,1)S(1)}, u32[]{:S(2)}, u32[]{:S(2)}) collective-permute-start(bf16[288,256]{1,0:T(8,128)(2,1)S(1)} %get-tuple-element.219), channel_id=1, source_target_pairs={{0,16},{1,17},{2,18},{3,19},{4,20},{5,21},{6,22},{7,23},{8,24},{9,... | collective-permute-start | bytes 442376 | tf_op jit(solution)/shard_map/ppermute | solution.py:722
  119.8 16.6 %collective-permute-start.33 = (bf16[8,424,256]{2,1,0:T(8,128)(2,1)S(1)}, bf16[8,424,256]{2,1,0:T(8,128)(2,1)S(1)}, u32[]{:S(2)}, u32[]{:S(2)}) collective-permute-start(bf16[8,424,256]{2,1,0:T(8,128)(2,1)S(1)} %bitcast.78), channel_id=1, source_target_pairs={{0,1},{1,0},{2,3},{3,2},{4,5},{5,4},{6,7},{7,6},{8,9},{9,8},{10,11... | collective-permute-start | bytes 5210120 | tf_op jit(solution)/shard_map/ppermute | solution.py:726
  119.9 22.6 %collective-permute-start.28 = (bf16[8,424,256]{2,1,0:T(8,128)(2,1)S(1)}, bf16[8,424,256]{2,1,0:T(8,128)(2,1)S(1)}, u32[]{:S(2)}, u32[]{:S(2)}) collective-permute-start(bf16[8,424,256]{2,1,0:T(8,128)(2,1)S(1)} %bitcast.79), channel_id=1, source_target_pairs={{0,2},{1,5},{2,0},{3,7},{4,6},{5,1},{6,4},{7,3},{8,10},{9,13},{10,... | collective-permute-start | bytes 5210120 | tf_op jit(solution)/shard_map/ppermute | solution.py:722
  122.0 8.6 %collective-permute-start.31 = (bf16[288,256]{1,0:T(8,128)(2,1)S(1)}, bf16[288,256]{1,0:T(8,128)(2,1)S(1)}, u32[]{:S(2)}, u32[]{:S(2)}) collective-permute-start(bf16[288,256]{1,0:T(8,128)(2,1)S(1)} %fusion.7), channel_id=1, source_target_pairs={{0,24},{1,25},{2,26},{3,27},{4,28},{5,29},{6,30},{7,31},{8,16},{9,... | collective-permute-start | bytes 442376 | tf_op jit(solution)/shard_map/ppermute | solution.py:722
  124.6 11.7 %collective-permute-start.30 = (bf16[288,256]{1,0:T(8,128)(2,1)S(1)}, bf16[288,256]{1,0:T(8,128)(2,1)S(1)}, u32[]{:S(2)}, u32[]{:S(2)}) collective-permute-start(bf16[288,256]{1,0:T(8,128)(2,1)S(1)} %fusion.7), channel_id=1, source_target_pairs={{0,16},{1,17},{2,18},{3,19},{4,20},{5,21},{6,22},{7,23},{8,24},{9,... | collective-permute-start | bytes 442376 | tf_op jit(solution)/shard_map/ppermute | solution.py:722
  125.5 10.9 %collective-permute-start.29 = (bf16[288,256]{1,0:T(8,128)(2,1)S(1)}, bf16[288,256]{1,0:T(8,128)(2,1)S(1)}, u32[]{:S(2)}, u32[]{:S(2)}) collective-permute-start(bf16[288,256]{1,0:T(8,128)(2,1)S(1)} %fusion.7), channel_id=1, source_target_pairs={{0,8},{1,9},{2,10},{3,11},{4,12},{5,13},{6,14},{7,15},{8,0},{9,1},... | collective-permute-start | bytes 442376 | tf_op jit(solution)/shard_map/ppermute | solution.py:722
  142.5 10.0 %collective-permute-start.36 = (bf16[8,424,256]{2,1,0:T(8,128)(2,1)S(1)}, bf16[8,424,256]{2,1,0:T(8,128)(2,1)S(1)}, u32[]{:S(2)}, u32[]{:S(2)}) collective-permute-start(bf16[8,424,256]{2,1,0:T(8,128)(2,1)S(1)} %collective-permute-done.28.mine.mine1), channel_id=1, source_target_pairs={{0,1},{1,0},{2,3},{3,2},{4,5},{5,4},{6,7},{7,6},{8,9},{9,8},{10,11... | collective-permute-start | bytes 5210120 | tf_op jit(solution)/shard_map/ppermute | solution.py:726
  142.5 9.9 %collective-permute-start.34 = (bf16[4,288,256]{2,1,0:T(8,128)(2,1)S(1)}, bf16[4,288,256]{2,1,0:T(8,128)(2,1)S(1)}, u32[]{:S(2)}, u32[]{:S(2)}) collective-permute-start(bf16[4,288,256]{2,1,0:T(8,128)(2,1)S(1)} %pad_maximum_fusion.3), channel_id=1, source_target_pairs={{0,4},{1,3},{2,6},{3,1},{4,0},{5,7},{6,2},{7,5},{8,12},{9,11},{10,... | collective-permute-start | bytes 1769480 | tf_op jit(solution)/shard_map/ppermute | solution.py:722
  152.5 9.9 %collective-permute-start.39 = (bf16[8,288,256]{2,1,0:T(8,128)(2,1)S(1)}, bf16[8,288,256]{2,1,0:T(8,128)(2,1)S(1)}, u32[]{:S(2)}, u32[]{:S(2)}) collective-permute-start(bf16[8,288,256]{2,1,0:T(8,128)(2,1)S(1)} %bitcast.82), channel_id=1, source_target_pairs={{0,1},{1,0},{2,3},{3,2},{4,5},{5,4},{6,7},{7,6},{8,9},{9,8},{10,11... | collective-permute-start | bytes 3538952 | tf_op jit(solution)/shard_map/ppermute | solution.py:726
  152.6 16.3 %collective-permute-start.38 = (bf16[8,288,256]{2,1,0:T(8,128)(2,1)S(1)}, bf16[8,288,256]{2,1,0:T(8,128)(2,1)S(1)}, u32[]{:S(2)}, u32[]{:S(2)}) collective-permute-start(bf16[8,288,256]{2,1,0:T(8,128)(2,1)S(1)} %bitcast.83), channel_id=1, source_target_pairs={{0,2},{1,5},{2,0},{3,7},{4,6},{5,1},{6,4},{7,3},{8,10},{9,13},{10,... | collective-permute-start | bytes 3538952 | tf_op jit(solution)/shard_map/ppermute | solution.py:722
  (12 other events, 52.6 us)

commit v3 on v2

--- a/solution.py
+++ b/solution.py
@@ -211,7 +211,7 @@
 def attention_body(
     place_ref, x_ref, own_ref, near_ref, gy_ref, ckeep_ref, csend_ref, vec_ref, w2, wq, wk, wv, wo,
     out_ref, dres_ref, dkeep_ref, dsend_ref, stat_ref, gkeep_ref, gsend_ref,
-    s_ref, norm_ref, normed, q, k, v, mixed, *, side,
+    s_ref, norm_ref, normed, qkv, mixed, *, side,
 ):
     images, px, ch = x_ref.shape
     core = place_ref[0]
@@ -255,11 +255,13 @@
         probs = lifted / jnp.sum(lifted, axis=1, keepdims=True)
         pb = probs.astype(BF)
         mixed[i] = mm(pb, vi).astype(BF)
-        v[i] = mm(pb, di, TN).astype(BF)
+        qkv[i, :, 2 * ch :] = mm(pb, di, TN).astype(BF)
         ds = (probs * (dp - jnp.sum(probs * dp, axis=1, keepdims=True))).astype(BF)
-        q[i] = (mm(ds, ki) * scale).astype(BF)
-        k[i] = (mm(ds, qi, TN) * scale).astype(BF)
-    dn = mm(flat(q), wq[...], NT) + mm(flat(k), wk[...], NT) + mm(flat(v), wv[...], NT)
+        qkv[i, :, :ch] = (mm(ds, ki) * scale).astype(BF)
+        qkv[i, :, ch : 2 * ch] = (mm(ds, qi, TN) * scale).astype(BF)
+    cotangents = qkv[...].reshape(images * px, 3 * ch)
+    dq, dk, dv = [cotangents[:, j * ch : (j + 1) * ch] for j in range(3)]
+    dn = mm(dq, wq[...], NT) + mm(dk, wk[...], NT) + mm(dv, wv[...], NT)
     projected = mm(flat(mixed), wo[...]) + row(10)
     for i, p in zip(every, spans(projected)):
         out_ref[i] = (dres_ref[i] + p).astype(BF)
@@ -277,14 +279,16 @@
     stat_ref[0:1, :] = total
     stat_ref[1:2, :] = gain_grad
     stat_ref[2:3, :] = bias_grad
-    stat_ref[3:4, :] = colsum(flat(q).astype(F32))
-    stat_ref[4:5, :] = colsum(flat(v).astype(F32))
+    stat_ref[3:4, :] = colsum(dq.astype(F32))
+    stat_ref[4:5, :] = colsum(dv.astype(F32))
     stat_ref[5:6, :] = colsum(flat(gy_ref).astype(F32))
     owners = gkeep_ref.shape[0]
     rows = ch // owners
     mine_at, other_at = place_ref[4], place_ref[5]
-    for j, (lhs, rhs) in enumerate(((normed, q), (normed, k), (normed, v), (mixed, gy_ref))):
-        keep, send = split_cols(mm(flat(lhs), flat(rhs), TN).astype(BF), core)
+    whole = mm(flat(normed), cotangents, TN)
+    grads = [whole[:, j * ch : (j + 1) * ch] for j in range(3)] + [mm(flat(mixed), flat(gy_ref), TN)]
+    for j, g in enumerate(grads):
+        keep, send = split_cols(g.astype(BF), core)
         for o in range(owners):
             gkeep_ref[o ^ mine_at, j * rows : (j + 1) * rows] = keep[o * rows : (o + 1) * rows]
             gsend_ref[o ^ other_at, j * rows : (j + 1) * rows] = send[o * rows : (o + 1) * rows]
@@ -311,7 +315,7 @@
             shape_of((owners, rows, half), BF), shape_of((owners, rows, half), BF),
         ],
         scratch_shapes=[pltpu.VMEM((images, px + 2 * side, 3 * ch), BF), pltpu.VMEM(whole, F32)]
-        + [pltpu.VMEM(whole, BF)] * 5,
+        + [pltpu.VMEM(whole, BF), pltpu.VMEM((images, px, 3 * ch), BF), pltpu.VMEM(whole, BF)],
         cost_estimate=took(13.5),
         compiler_params=pltpu.CompilerParams(vmem_limit_bytes=20 << 20),
     )(place, x, own, near, gy, ckeep, csend, vec, *weights)
@@ -420,7 +424,7 @@
             pltpu.VMEM(part, BF),
             pltpu.SemaphoreType.DMA(()),
         ],
-        cost_estimate=took(5.4),
+        cost_estimate=took(0.1),
         compiler_params=pltpu.CompilerParams(vmem_limit_bytes=12 << 20),
     )(place, dfull, x, dres, vec, w1)
 
@@ -447,29 +451,51 @@
     )(place, got, into)
 
 
-def kernel_grad_body(place_ref, *refs, side, which):
-    acts, grads = refs[:4], refs[4:8]
-    out_ref, s_ref, d_ref = refs[-3:]
+def turn(a, i, s_ref, at, side):
+    px, part = a.shape[-2:]
+    for j, t in enumerate(shifted(a[i].astype(F32), side)):
+        s_ref[j * part : (j + 1) * part, pl.ds(pl.multiple_of(at * px, px), px)] = t.astype(BF).T
+
+
+def turn_body(*refs, side, which):
+    *acts, s_ref = refs
+    images = acts[0].shape[1]
+    for n, a in enumerate(acts):
+
+        def fill(i, carry, a=a, n=n):
+            turn(a.at[which], i, s_ref, n * images + i, side)
+            return carry
+
+        lax.fori_loop(0, images, fill, 0)
+
+
+def run_turn(which, acts, side):
     _, images, px, part = acts[0].shape
-    half = grads[0].shape[2]
+    return pl.pallas_call(
+        functools.partial(turn_body, side=side, which=which),
+        name="turn",
+        in_specs=[VMEM] * 4,
+        out_specs=VMEM,
+        out_shape=shape_of((3 * part, 4 * images * px), BF),
+        cost_estimate=took(2),
+        compiler_params=pltpu.CompilerParams(vmem_limit_bytes=6 << 20),
+    )(*acts)
+
+
+def kernel_grad_body(place_ref, s_ref, *refs, side):
+    *grads, out_ref, d_ref = refs
+    images, px, half = grads[0].shape
+    part = s_ref.shape[0] // 3
     bits = place_ref[8]
     first, second, _, _ = out_ref.shape
     owners = first * second
     rows = part // owners
     zero = jnp.zeros((side, half), BF)
-    for n in range(4 * images):
-        d_ref[n, 0:side, :] = zero
-        d_ref[n, px + side :, :] = zero
-    for n, (a, d) in enumerate(zip(acts, grads)):
-
-        def fill(i, carry, a=a, d=d, n=n):
-            at = n * images + i
-            d_ref[at, side : px + side, :] = d[i]
-            for j, t in enumerate(shifted(a[which, i].astype(F32), side)):
-                s_ref[j * part : (j + 1) * part, pl.ds(pl.multiple_of(at * px, px), px)] = t.astype(BF).T
-            return carry
-
-        lax.fori_loop(0, images, fill, 0)
+    for n, d in enumerate(grads):
+        for i in range(images):
+            d_ref[n * images + i, 0:side, :] = zero
+            d_ref[n * images + i, side : px + side, :] = d[i]
+            d_ref[n * images + i, px + side :, :] = zero
     for dh in range(3):
         start = (2 - dh) * side
         d = jnp.concatenate([d_ref[n, start : start + px, :] for n in range(4 * images)], axis=0)
@@ -482,23 +508,20 @@
                 out_ref[at // second, at % second, tap * rows : (tap + 1) * rows, :] = g[begin : begin + rows]
 
 
-def run_kernel_grad(place, which, acts, grads, lead, side, name):
-    _, images, px, part = acts[0].shape
-    half = grads[0].shape[2]
+def run_kernel_grad(place, turned, grads, lead, side, us, name):
+    images, px, half = grads[0].shape
+    part = turned.shape[0] // 3
     rows = 9 * (part // (lead[0] * lead[1]))
     return pl.pallas_call(
-        functools.partial(kernel_grad_body, side=side, which=which),
+        functools.partial(kernel_grad_body, side=side),
         name=name,
-        in_specs=[SMEM] + [VMEM] * 8,
+        in_specs=[SMEM] + [VMEM] * 5,
         out_specs=VMEM,
         out_shape=shape_of((lead[0], lead[1], rows, half), BF),
-        scratch_shapes=[
-            pltpu.VMEM((3 * part, 4 * images * px), BF),
-            pltpu.VMEM((4 * images, px + 2 * side, half), BF),
-        ],
-        cost_estimate=took(4.8),
-        compiler_params=pltpu.CompilerParams(vmem_limit_bytes=14 << 20),
-    )(place, *acts, *grads)
+        scratch_shapes=[pltpu.VMEM((4 * images, px + 2 * side, half), BF)],
+        cost_estimate=took(us),
+        compiler_params=pltpu.CompilerParams(vmem_limit_bytes=10 << 20),
+    )(place, turned, *grads)
 
 
 def prepare_body(place_ref, ids_hbm, dead_hbm, replace_hbm, latents_hbm, w1_hbm, *refs):
@@ -797,11 +820,7 @@
     grads2 = [dkeep2, links.partner(dsend2), links.send(dkeep2, 1), links.far(dsend2)]
     attn = (gkeep.astype(F32) + links.partner(gsend).astype(F32)).astype(BF)
     attn = attn.reshape((2, low) + attn.shape[1:])
-    attn_keep, attn_send, dres = together(attn[0], attn[1], dres)
-    attn_got = links.send(attn_send, 1)
-    dkeep1, dsend1, dfull1, stat_b = run_back2(place, dres, norm2, scale2, vec, w2, side)
-    grads2[0], stat_b = together(grads2[0], stat_b)
-    grads1 = [dkeep1, links.partner(dsend1), links.send(dkeep1, 1), links.far(dsend1)]
+    attn_got = links.send(attn[1], 1)
     lead = links.lead()
     rest = range(1, len(lead))
     split = (lead[0], low // lead[0])
@@ -819,45 +838,45 @@
     def owned(value):
         return value.reshape((low,) + value.shape[-2:])
 
-    sum2 = run_kernel_grad(place, 1, acts, grads2, split, side, "conv2_grad")
-    sum2_keep, attn_got, grads1[0] = together(sum2, attn_got, grads1[0])
-    sum1 = run_kernel_grad(place, 0, acts, grads1, split, side, "conv1_grad")
-    attn = (attn_keep.astype(F32) + attn_got.astype(F32)).astype(BF)
+    sum2 = run_kernel_grad(place, run_turn(1, acts, side), grads2, split, side, 3, "conv2_grad")
+    sum2_keep, dres = together(sum2, dres)
+    dkeep1, dsend1, dfull1, stat_b = run_back2(place, dres, norm2, scale2, vec, w2, side)
+    attn = (attn[0].astype(F32) + attn_got.astype(F32)).astype(BF)
     attn = attn.reshape(lead + attn.shape[1:])
     sum2 = sum2.reshape(lead + sum2.shape[2:])
-    sum2_keep = sum2_keep.reshape(sum2.shape)
-    sum1 = sum1.reshape(lead + sum1.shape[2:])
     attn = reduce(attn, [0])
-    sum2 = links.reduce(sum2, 0, sum2_keep)
-    attn, sum2, sum1, dfull1 = together(attn, sum2, sum1, dfull1)
-    conv_rows = sum2.shape[-2]
+    sum2 = links.reduce(sum2, 0, sum2_keep.reshape(sum2.shape))
+    grads1 = [dkeep1, links.partner(dsend1), links.send(dkeep1, 1), links.far(dsend1)]
+    attn, sum2, stat_b, dfull1, grads1[0], *acts = together(attn, sum2, stat_b, dfull1, dkeep1, *acts)
     sum2 = reduce(jnp.concatenate([sum2, attn], axis=-2), rest)
-    sum1 = reduce(sum1, [0])
+    sum1 = run_kernel_grad(place, run_turn(0, acts, side), grads1, split, side, 0.1, "conv1_grad")
     rows_out, in_send, stat_c = run_back1(place, dfull1, x, dres, vec, w1, side)
     sum2, sum1, in_send, stat_c = together(sum2, sum1, in_send, stat_c)
     vectors = jnp.concatenate([stat_c[:2], stat_b[2:3], stat_b[:2], stat_a[:6], counts[:1].reshape(-1, ch)])
     steps = links.small_steps()
     sum2 = gather(sum2, rest)
+    sum1 = sum1.reshape(lead + sum1.shape[2:])
+    sum1 = reduce(sum1, [0])
     in_got = links.partner(in_send)
     vectors = steps[0](vectors)
     sum2, sum1, in_got, vectors = together(sum2, sum1, in_got, vectors)
     sum2 = owned(gather(sum2, [0]))
     sum1 = reduce(sum1, rest)
     vectors = steps[1](vectors)
-    input_grad, _ = run_place_rows(place, in_got, rows_out)
-    sum2, sum1, vectors, input_grad = together(sum2, sum1, vectors, input_grad)
+    sum2, sum1, vectors = together(sum2, sum1, vectors)
     far2 = links.send(sum2, 1)
     other2 = links.partner(sum2)
     sum1 = gather(sum1, rest)
     vectors = steps[2](vectors)
+    input_grad, _ = run_place_rows(place, in_got, rows_out)
+    sum1, vectors, other2, input_grad = together(sum1, vectors, other2, input_grad)
+    sum1 = owned(gather(sum1, [0]))
+    vectors = steps[3](vectors)
     grad2 = run_conv_finish(place, sum2, other2, None, ch, "conv2_finish")
-    far2, sum1, vectors, grad2 = together(far2, sum1, vectors, grad2)
-    sum1 = owned(gather(sum1, [0]))
-    other_far2 = links.partner(far2)
-    vectors = steps[3](vectors)
-    sum1, vectors, other_far2 = together(sum1, vectors, other_far2)
+    sum1, far2, vectors, grad2 = together(sum1, far2, vectors, grad2)
     far1 = links.send(sum1, 1)
     other1 = links.partner(sum1)
+    other_far2 = links.partner(far2)
     for step in steps[4:]:
         vectors = step(vectors)
     qg, kg, vg, og, new_codebook = run_attention_finish(
@@ -865,9 +884,9 @@
     )
     grad2 = run_conv_finish(place, far2, other_far2, grad2, ch, "conv2_finish")
     grad1 = run_conv_finish(place, sum1, other1, None, ch, "conv1_finish")
+    far1, grad2, grad1, vectors, new_codebook = together(far1, grad2, grad1, vectors, new_codebook)
     *vec_grads, usage, perplexity = run_vectors(vectors, 11, codes)
     (g1, b1, cb1, g2, b2, cb2, g3, b3, qb, vb, ob) = [v.reshape(ch) for v in vec_grads]
-    far1, grad2, grad1, perplexity, new_codebook = together(far1, grad2, grad1, perplexity, new_codebook)
     grad1 = run_conv_finish(place, far1, links.partner(far1), grad1, ch, "conv1_finish")
     input_grad = input_grad.reshape(image_rows.shape)
     kernel_shape = (3, 3, ch, ch)

time: 175 us -> 168 us (0.960)
  waiting for transfers between devices: 74 us -> 61.1 us
  starting transfers between devices: 38.7 us -> 43.2 us
    ppermute x27, waiting for transfers between devices: 70.3 us -> 58.5 us  [send(): return lax.ppermute(value, AXES, pairs)]
    ppermute x27, starting transfers between devices: 31.1 us -> 35 us  [send(): return lax.ppermute(value, AXES, pairs)]
    pallas_call x2 -> x4, Pallas kernels: 9.18 us -> 9.04 us  [the longest x2 6.34 us: run_kernel_grad(): pl.pallas_call(functools.partial(kernel_grad_body, side=side), name=name,...]
  transfers between devices with their start and end apart: 41 -> 41, of which waited for: 19 -> 19; matrix products, arithmetic and copies ran while one was open for 1% -> 2% of each run, Pallas kernels for 27% -> 28%
where the time goes in v3:
time: 168 us
  waiting for transfers between devices  61.1 us (36%)
  Pallas kernels  56.5 us (34%)
  starting transfers between devices  43.2 us (26%)
  other arithmetic  3.23 us (2%)
  local copies, waits for them, and re-layouts  2.32 us (1%)
    ppermute x27, waiting for transfers between devices, send(): return lax.ppermute(value, AXES, pairs)  58.5 us
    ppermute x27, starting transfers between devices, send(): return lax.ppermute(value, AXES, pairs)  35 us
    pallas_call x4, Pallas kernels, run_conv_finish(): pl.pallas_call(functools.partial(conv_finish_body, far=len(given)), name=...  10.9 us
    pallas_call x1, Pallas kernels, run_attention(): pl.pallas_call(functools.partial(attention_body, side=side), name='attent...  10.3 us
    pallas_call x1, Pallas kernels, run_entry(): pl.pallas_call(functools.partial(entry_body, side=side), name='entry', in...  6.76 us
    pallas_call x2, Pallas kernels, run_kernel_grad(): pl.pallas_call(functools.partial(kernel_grad_body, side=side), name=name,...  6.34 us
    ppermute x3, starting transfers between devices, far(): return lax.ppermute(value, AXES, pairs)  5.65 us
    pallas_call x1, Pallas kernels, run_back1(): pl.pallas_call(functools.partial(back1_body, side=side), name='conv1_back...  4.87 us
  transfers between devices with their start and end apart: 41, of which 19 were waited for; matrix products, arithmetic and copies ran while one was open for 2% of the time, Pallas kernels for 28%

profile of v3, /device:TPU:0, one launch (start us, length us, event | category | flops | bytes accessed | tf_op | source)
XLA Modules:
  0.0 167.6 jit_solution(15685846292115245383)
XLA Ops:
  2.2 3.3 %prepare.1 = (f32[8,1024]{1,0:T(8,128)S(1)}, bf16[256,1024]{1,0:T(8,128)(2,1)S(1)}, bf16[16,8,256]{2,1,0:T(8,128)(2,1)S(1)}, bf16[16,8,256]{2,1,0:T(8,128)(2,1)S...) custom-call(s32[9]{0:T(128)S(1)} %stack.87.place_ref, s32[1,512]{1,0:T(1,128)} %bitcast.108, ...), custom_call_target="tpu_custom_call" | custom-call | flops 2529999872 | bytes 1048576 | tf_op jit(solution)/shard_map/prepare/pallas_call | solution.py:581
  5.5 6.8 %entry.1 = (bf16[2,2,256,256]{3,2,1,0:T(8,128)(2,1)S(1)}, bf16[2,2,256,256]{3,2,1,0:T(8,128)(2,1)S(1)}, bf16[2,2,256,256]{3,2,1,0:T(8,128)(2,1)S(1)}, bf16[2,2,2...) custom-call(s32[9]{0:T(128)S(1)} %stack.87.place_ref, ...), custom_call_target="tpu_custom_call" | custom-call | flops 9774999552 | bytes 1048576 | tf_op jit(solution)/shard_map/entry/pallas_call | solution.py:194
  12.5 2.6 %collective-permute-start.3 = (bf16[2,2,256,256]{3,2,1,0:T(8,128)(2,1)S(1)}, bf16[2,2,256,256]{3,2,1,0:T(8,128)(2,1)S(1)}, u32[]{:S(2)}, u32[]{:S(2)}) collective-permute-start(bf16[2,2,256,256]{3,2,1,0:T(8,128)(2,1)S(1)} %get-tuple-element.136), channel_id=1, source_target_pairs={{0,5},{1,2},{2,7},{3,0},{4,1},{5,6},{6,3},{7,4},{8,13},{9,10},{10,... | collective-permute-start | bytes 1572872 | tf_op jit(solution)/shard_map/ppermute | solution.py:753
  16.6 10.3 %attention.1 = (bf16[2,256,512]{2,1,0:T(8,128)(2,1)}, f32[2,256,512]{2,1,0:T(8,128)S(1)}, bf16[2,256,256]{2,1,0:T(8,128)(2,1)S(1)}, bf16[2,256,256]{2,1,0:T(8,12...) custom-call(s32[9]{0:T(128)S(1)} %stack.87.place_ref, ...), custom_call_target="tpu_custom_call" | custom-call | flops 15525000192 | bytes 1048576 | tf_op jit(solution)/shard_map/attention/pallas_call | solution.py:306
  33.7 2.9 %collective-permute-done.8.refs_2_ = bf16[2,256,256]{2,1,0:T(8,128)(2,1)S(1)} collective-permute-done((bf16[2,256,256]{2,1,0:T(8,128)(2,1)S(1)}, bf16[2,256,256]{2,1,0:T(8,128)(2,1)S(1)}, u32[]{:S(2)}, u32[]{:S(2)}) %collective-permute-start.8) | collective-permute-done | bytes 262176 | tf_op jit(solution)/shard_map/ppermute | solution.py:745
  36.6 3.2 %conv2_grad.1 = bf16[2,4,288,256]{3,2,1,0:T(8,128)(2,1)S(1)} custom-call(s32[9]{0:T(128)S(1)} %stack.87.place_ref, bf16[768,2048]{1,0:T(8,128)(2,1)S(1)} %turn.2.s_ref, bf16[2,256,256]{2,1,0:T(8,128)(2,1)S(1)} %get-tuple-element.141.refs_0_, bf16[2,256,256]{2,1,0:T(8,128)(2,1)S(1)} %collective-permute-done.7.refs_1_, ...), custom_call_target="tpu_custom_call" | custom-call | flops 3449999872 | bytes 1048576 | tf_op jit(solution)/shard_map/conv2_grad/pallas_call | solution.py:515
  44.6 4.3 %conv2_back.1 = (bf16[2,256,256]{2,1,0:T(8,128)(2,1)S(1)}, bf16[2,256,256]{2,1,0:T(8,128)(2,1)S(1)}, bf16[2,256,512]{2,1,0:T(8,128)(2,1)S(1)}, f32[8,512]{1,0:T(8,128)S(1)}) custom-call(s32[9]{0:T(128)S(1)} %stack.87.place_ref, f32[2,256,512]{2,1,0:T(8,128)S(1)} %get-tuple-element.145.dres_ref, f32[2,256,512]{2,1,0:T(8,128)S(1)} %get-tuple-element.146.norm2_ref, ...), custom_call_target="tpu_custom_call" | custom-call | flops 5750000128 | bytes 1048576 | tf_op jit(solution)/shard_map/conv2_back/pallas_call | solution.py:368
  53.0 1.9 %collective-permute-start.11 = (bf16[424,256]{1,0:T(8,128)(2,1)S(1)}, bf16[424,256]{1,0:T(8,128)(2,1)S(1)}, u32[]{:S(2)}, u32[]{:S(2)}) collective-permute-start(bf16[424,256]{1,0:T(8,128)(2,1)S(1)} %get-tuple-element.210), channel_id=1, source_target_pairs={{0,8},{1,9},{2,10},{3,11},{4,12},{5,13},{6,14},{7,15},{8,0},{9,1},... | collective-permute-start | bytes 651272 | tf_op jit(solution)/shard_map/ppermute | solution.py:745
  54.8 2.5 %collective-permute-start.13 = (bf16[424,256]{1,0:T(8,128)(2,1)S(1)}, bf16[424,256]{1,0:T(8,128)(2,1)S(1)}, u32[]{:S(2)}, u32[]{:S(2)}) collective-permute-start(bf16[424,256]{1,0:T(8,128)(2,1)S(1)} %get-tuple-element.211), channel_id=1, source_target_pairs={{0,24},{1,25},{2,26},{3,27},{4,28},{5,29},{6,30},{7,31},{8,16},{9,... | collective-permute-start | bytes 651272 | tf_op jit(solution)/shard_map/ppermute | solution.py:745
  57.3 4.9 %conv1_back.1 = (bf16[4,128,512]{2,1,0:T(8,128)(2,1)}, bf16[2,128,512]{2,1,0:T(8,128)(2,1)S(1)}, f32[8,512]{1,0:T(8,128)S(1)}) custom-call(s32[9]{0:T(128)S(1)} %stack.87.place_ref, bf16[2,256,512]{2,1,0:T(8,128)(2,1)S(1)} %get-tuple-element.159.dfull_ref, bf16[2,256,512]{2,1,0:T(8,128)(2,1)S(1)} %get-tuple-element.118.x_ref, ...), custom_call_target="tpu_custom_call" | custom-call | flops 115000000 | bytes 1048576 | tf_op jit(solution)/shard_map/conv1_back/pallas_call | solution.py:416
  63.8 3.2 %conv1_grad.1 = bf16[2,4,288,256]{3,2,1,0:T(8,128)(2,1)S(1)} custom-call(s32[9]{0:T(128)S(1)} %stack.87.place_ref, bf16[768,2048]{1,0:T(8,128)(2,1)S(1)} %turn.3.s_ref, bf16[2,256,256]{2,1,0:T(8,128)(2,1)S(1)} %get-tuple-element.157.refs_0_, bf16[2,256,256]{2,1,0:T(8,128)(2,1)S(1)} %collective-permute-done.14.refs_1_, ...), custom_call_target="tpu_custom_call" | custom-call | flops 115000000 | bytes 1048576 | tf_op jit(solution)/shard_map/conv1_grad/pallas_call | solution.py:515
  68.3 8.1 %collective-permute-done.12 = bf16[424,256]{1,0:T(8,128)(2,1)S(1)} collective-permute-done((bf16[424,256]{1,0:T(8,128)(2,1)S(1)}, bf16[424,256]{1,0:T(8,128)(2,1)S(1)}, u32[]{:S(2)}, u32[]{:S(2)}) %collective-permute-start.12) | collective-permute-done | bytes 217120 | tf_op jit(solution)/shard_map/ppermute | solution.py:745
  78.9 2.7 %collective-permute-start.19 = (bf16[424,256]{1,0:T(8,128)(2,1)S(1)}, bf16[424,256]{1,0:T(8,128)(2,1)S(1)}, u32[]{:S(2)}, u32[]{:S(2)}) collective-permute-start(bf16[424,256]{1,0:T(8,128)(2,1)S(1)} %fusion.4), channel_id=1, source_target_pairs={{0,24},{1,25},{2,26},{3,27},{4,28},{5,29},{6,30},{7,31},{8,16},{9,... | collective-permute-start | bytes 651272 | tf_op jit(solution)/shard_map/ppermute | solution.py:745
  84.9 4.1 %collective-permute-done.19 = bf16[424,256]{1,0:T(8,128)(2,1)S(1)} collective-permute-done((bf16[424,256]{1,0:T(8,128)(2,1)S(1)}, bf16[424,256]{1,0:T(8,128)(2,1)S(1)}, u32[]{:S(2)}, u32[]{:S(2)}) %collective-permute-start.19) | collective-permute-done | bytes 217120 | tf_op jit(solution)/shard_map/ppermute | solution.py:745
  89.0 9.0 %collective-permute-done.18 = bf16[424,256]{1,0:T(8,128)(2,1)S(1)} collective-permute-done((bf16[424,256]{1,0:T(8,128)(2,1)S(1)}, bf16[424,256]{1,0:T(8,128)(2,1)S(1)}, u32[]{:S(2)}, u32[]{:S(2)}) %collective-permute-start.18) | collective-permute-done | bytes 217120 | tf_op jit(solution)/shard_map/ppermute | solution.py:745
  99.4 2.0 %collective-permute-start.23 = (bf16[4,424,256]{2,1,0:T(8,128)(2,1)S(1)}, bf16[4,424,256]{2,1,0:T(8,128)(2,1)S(1)}, u32[]{:S(2)}, u32[]{:S(2)}) collective-permute-start(bf16[4,424,256]{2,1,0:T(8,128)(2,1)S(1)} %pad_maximum_fusion.2), channel_id=1, source_target_pairs={{0,4},{1,3},{2,6},{3,1},{4,0},{5,7},{6,2},{7,5},{8,12},{9,11},{10,... | collective-permute-start | bytes 2605064 | tf_op jit(solution)/shard_map/ppermute | solution.py:745
  105.3 4.0 %collective-permute-done.27 = f32[13,512]{1,0:T(8,128)S(1)} collective-permute-done((f32[13,512]{1,0:T(8,128)S(1)}, f32[13,512]{1,0:T(8,128)S(1)}, u32[]{:S(2)}, u32[]{:S(2)}) %collective-permute-start.27) | collective-permute-done | bytes 26656 | tf_op jit(solution)/shard_map/ppermute | solution.py:745
  109.8 5.5 %collective-permute-done.25 = bf16[288,256]{1,0:T(8,128)(2,1)S(1)} collective-permute-done((bf16[288,256]{1,0:T(8,128)(2,1)S(1)}, bf16[288,256]{1,0:T(8,128)(2,1)S(1)}, u32[]{:S(2)}, u32[]{:S(2)}) %collective-permute-start.25) | collective-permute-done | bytes 147488 | tf_op jit(solution)/shard_map/ppermute | solution.py:745
  117.4 2.4 %collective-permute-start.31 = (f32[13,512]{1,0:T(8,128)S(1)}, f32[13,512]{1,0:T(8,128)S(1)}, u32[]{:S(2)}, u32[]{:S(2)}) collective-permute-start(f32[13,512]{1,0:T(8,128)S(1)} %add.75), channel_id=1, source_target_pairs={{0,4},{1,3},{2,6},{3,1},{4,0},{5,7},{6,2},{7,5},{8,12},{9,11},{10,... | collective-permute-start | bytes 79880 | tf_op jit(solution)/shard_map/ppermute | solution.py:745
  119.9 2.1 %collective-permute-start.30 = (bf16[288,256]{1,0:T(8,128)(2,1)S(1)}, bf16[288,256]{1,0:T(8,128)(2,1)S(1)}, u32[]{:S(2)}, u32[]{:S(2)}) collective-permute-start(bf16[288,256]{1,0:T(8,128)(2,1)S(1)} %fusion.7), channel_id=1, source_target_pairs={{0,24},{1,25},{2,26},{3,27},{4,28},{5,29},{6,30},{7,31},{8,16},{9,... | collective-permute-start | bytes 442376 | tf_op jit(solution)/shard_map/ppermute | solution.py:745
  122.2 2.1 %collective-permute-start.28 = (bf16[288,256]{1,0:T(8,128)(2,1)S(1)}, bf16[288,256]{1,0:T(8,128)(2,1)S(1)}, u32[]{:S(2)}, u32[]{:S(2)}) collective-permute-start(bf16[288,256]{1,0:T(8,128)(2,1)S(1)} %fusion.7), channel_id=1, source_target_pairs={{0,8},{1,9},{2,10},{3,11},{4,12},{5,13},{6,14},{7,15},{8,0},{9,1},... | collective-permute-start | bytes 442376 | tf_op jit(solution)/shard_map/ppermute | solution.py:745
  124.2 1.8 %place_rows.1 = (bf16[4,128,512]{2,1,0:T(8,128)(2,1)}, f32[8,128]{1,0:T(8,128)}) custom-call(s32[9]{0:T(128)S(1)} %stack.87.place_ref, bf16[2,128,512]{2,1,0:T(8,128)(2,1)S(1)} %collective-permute-done.21.got_ref, bf16[4,128,512]{2,1,0:T(8,128)(2,1)} %get-tuple-element.176.into_hbm), custom_call_target="tpu_custom_call", output_to_operand_aliasing={{0}: (2, {})} | custom-call | flops 1150000000 | bytes 1048576 | tf_op jit(solution)/shard_map/place_rows/pallas_call | solution.py:441
  126.1 2.4 %collective-permute-done.30 = bf16[288,256]{1,0:T(8,128)(2,1)S(1)} collective-permute-done((bf16[288,256]{1,0:T(8,128)(2,1)S(1)}, bf16[288,256]{1,0:T(8,128)(2,1)S(1)}, u32[]{:S(2)}, u32[]{:S(2)}) %collective-permute-start.30) | collective-permute-done | bytes 147488 | tf_op jit(solution)/shard_map/ppermute | solution.py:745
  128.5 5.2 %collective-permute-done.29 = bf16[288,256]{1,0:T(8,128)(2,1)S(1)} collective-permute-done((bf16[288,256]{1,0:T(8,128)(2,1)S(1)}, bf16[288,256]{1,0:T(8,128)(2,1)S(1)}, u32[]{:S(2)}, u32[]{:S(2)}) %collective-permute-start.29) | collective-permute-done | bytes 147488 | tf_op jit(solution)/shard_map/ppermute | solution.py:745
  134.4 2.7 %conv2_finish.2.refs_0_ = f32[9,512,512]{2,1,0:T(8,128)} custom-call(s32[9]{0:T(128)S(1)} %stack.87.place_ref, bf16[8,424,256]{2,1,0:T(8,128)(2,1)S(1)} %bitcast.80, bf16[8,424,256]{2,1,0:T(8,128)(2,1)S(1)} %collective-permute-done.32.other.other0), custom_call_target="tpu_custom_call" | custom-call | flops 4024999936 | bytes 1048576 | tf_op jit(solution)/shard_map/conv2_finish/pallas_call | solution.py:676
  138.1 6.3 %collective-permute-done.33 = bf16[4,288,256]{2,1,0:T(8,128)(2,1)S(1)} collective-permute-done((bf16[4,288,256]{2,1,0:T(8,128)(2,1)S(1)}, bf16[4,288,256]{2,1,0:T(8,128)(2,1)S(1)}, u32[]{:S(2)}, u32[]{:S(2)}) %collective-permute-start.33) | collective-permute-done | bytes 589856 | tf_op jit(solution)/shard_map/ppermute | solution.py:745
  145.1 2.1 %collective-permute-start.36 = (bf16[8,288,256]{2,1,0:T(8,128)(2,1)S(1)}, bf16[8,288,256]{2,1,0:T(8,128)(2,1)S(1)}, u32[]{:S(2)}, u32[]{:S(2)}) collective-permute-start(bf16[8,288,256]{2,1,0:T(8,128)(2,1)S(1)} %bitcast.83), channel_id=1, source_target_pairs={{0,2},{1,5},{2,0},{3,7},{4,6},{5,1},{6,4},{7,3},{8,10},{9,13},{10,... | collective-permute-start | bytes 3538952 | tf_op jit(solution)/shard_map/ppermute | solution.py:745
  147.1 4.8 %collective-permute-done.39 = f32[13,512]{1,0:T(8,128)S(1)} collective-permute-done((f32[13,512]{1,0:T(8,128)S(1)}, f32[13,512]{1,0:T(8,128)S(1)}, u32[]{:S(2)}, u32[]{:S(2)}) %collective-permute-start.39) | collective-permute-done | bytes 26656 | tf_op jit(solution)/shard_map/ppermute | solution.py:745
  152.5 2.7 %conv1_finish.2.refs_0_ = f32[9,512,512]{2,1,0:T(8,128)} custom-call(s32[9]{0:T(128)S(1)} %stack.87.place_ref, bf16[8,288,256]{2,1,0:T(8,128)(2,1)S(1)} %bitcast.84, bf16[8,288,256]{2,1,0:T(8,128)(2,1)S(1)} %collective-permute-done.38.other), custom_call_target="tpu_custom_call" | custom-call | flops 4024999936 | bytes 1048576 | tf_op jit(solution)/shard_map/conv1_finish/pallas_call | solution.py:676
  155.3 3.7 %attention_finish.1 = (f32[512,512]{1,0:T(8,128)}, f32[512,512]{1,0:T(8,128)}, f32[512,512]{1,0:T(8,128)}, f32[512,512]{1,0:T(8,128)}, f32[32,256]{1,0:T(8,128)}) custom-call(s32[9]{0:T(128)S(1)} %stack.87.place_ref, bf16[8,424,256]{2,1,0:T(8,128)(2,1)S(1)} %bitcast.81, bf16[8,424,256]{2,1,0:T(8,128)(2,1)S(1)} %collective-permute-done.32.other.other0, ...), custom_call_target="tpu_custom_call" | custom-call | flops 3449999872 | bytes 1048576 | tf_op jit(solution)/shard_map/attention_finish/pallas_call | solution.py:651
  159.0 2.7 %conv2_finish.3 = f32[9,512,512]{2,1,0:T(8,128)} custom-call(s32[9]{0:T(128)S(1)} %stack.87.place_ref, bf16[8,424,256]{2,1,0:T(8,128)(2,1)S(1)} %collective-permute-done.34.mine.mine1, bf16[8,424,256]{2,1,0:T(8,128)(2,1)S(1)} %collective-permute-done.37.other.other1, f32[9,512,512]{2,1,0:T(8,128)} %conv2_finish.2.refs_0_), custom_call_target="tpu_custom_call", output_to_operand_aliasing={{}: (3, {})} | custom-call | flops 4024999936 | bytes 1048576 | tf_op jit(solution)/shard_map/conv2_finish/pallas_call | solution.py:676
  164.7 2.7 %conv1_finish.3 = f32[9,512,512]{2,1,0:T(8,128)} custom-call(s32[9]{0:T(128)S(1)} %stack.87.place_ref, bf16[8,288,256]{2,1,0:T(8,128)(2,1)S(1)} %collective-permute-done.36.mine, bf16[8,288,256]{2,1,0:T(8,128)(2,1)S(1)} %collective-permute-done.40.other, f32[9,512,512]{2,1,0:T(8,128)} %conv1_finish.2.refs_0_), custom_call_target="tpu_custom_call", output_to_operand_aliasing={{}: (3, {})} | custom-call | flops 4024999936 | bytes 1048576 | tf_op jit(solution)/shard_map/conv1_finish/pallas_call | solution.py:676
  (100 shorter events, 41.4 us)
Async XLA Ops:
  12.3 14.6 %collective-permute-start.1 = (bf16[2,2,256,256]{3,2,1,0:T(8,128)(2,1)S(1)}, bf16[2,2,256,256]{3,2,1,0:T(8,128)(2,1)S(1)}, u32[]{:S(2)}, u32[]{:S(2)}) collective-permute-start(bf16[2,2,256,256]{3,2,1,0:T(8,128)(2,1)S(1)} %get-tuple-element.135), channel_id=1, source_target_pairs={{0,1},{1,0},{2,3},{3,2},{4,5},{5,4},{6,7},{7,6},{8,9},{9,8},{10,11... | collective-permute-start | bytes 1572872 | tf_op jit(solution)/shard_map/ppermute | solution.py:749
  12.5 14.4 %collective-permute-start.3 = (bf16[2,2,256,256]{3,2,1,0:T(8,128)(2,1)S(1)}, bf16[2,2,256,256]{3,2,1,0:T(8,128)(2,1)S(1)}, u32[]{:S(2)}, u32[]{:S(2)}) collective-permute-start(bf16[2,2,256,256]{3,2,1,0:T(8,128)(2,1)S(1)} %get-tuple-element.136), channel_id=1, source_target_pairs={{0,5},{1,2},{2,7},{3,0},{4,1},{5,6},{6,3},{7,4},{8,13},{9,10},{10,... | collective-permute-start | bytes 1572872 | tf_op jit(solution)/shard_map/ppermute | solution.py:753
  15.1 12.5 %collective-permute-start.2 = (bf16[2,2,256,256]{3,2,1,0:T(8,128)(2,1)S(1)}, bf16[2,2,256,256]{3,2,1,0:T(8,128)(2,1)S(1)}, u32[]{:S(2)}, u32[]{:S(2)}) collective-permute-start(bf16[2,2,256,256]{3,2,1,0:T(8,128)(2,1)S(1)} %get-tuple-element.120.near_ref), channel_id=1, source_target_pairs={{0,2},{1,5},{2,0},{3,7},{4,6},{5,1},{6,4},{7,3},{8,10},{9,13},{10,... | collective-permute-start | bytes 1572872 | tf_op jit(solution)/shard_map/ppermute | solution.py:745
  28.0 8.6 %collective-permute-start.9 = (bf16[2,256,256]{2,1,0:T(8,128)(2,1)S(1)}, bf16[2,256,256]{2,1,0:T(8,128)(2,1)S(1)}, u32[]{:S(2)}, u32[]{:S(2)}) collective-permute-start(bf16[2,256,256]{2,1,0:T(8,128)(2,1)S(1)} %get-tuple-element.142), channel_id=1, source_target_pairs={{0,5},{1,2},{2,7},{3,0},{4,1},{5,6},{6,3},{7,4},{8,13},{9,10},{10,... | collective-permute-start | bytes 786440 | tf_op jit(solution)/shard_map/ppermute | solution.py:753
  29.7 6.9 %collective-permute-start.7 = (bf16[2,256,256]{2,1,0:T(8,128)(2,1)S(1)}, bf16[2,256,256]{2,1,0:T(8,128)(2,1)S(1)}, u32[]{:S(2)}, u32[]{:S(2)}) collective-permute-start(bf16[2,256,256]{2,1,0:T(8,128)(2,1)S(1)} %get-tuple-element.142), channel_id=1, source_target_pairs={{0,1},{1,0},{2,3},{3,2},{4,5},{5,4},{6,7},{7,6},{8,9},{9,8},{10,11... | collective-permute-start | bytes 786440 | tf_op jit(solution)/shard_map/ppermute | solution.py:749
  33.0 9.6 %collective-permute-start.5 = (bf16[8,136,256]{2,1,0:T(8,128)(2,1)S(1)}, bf16[8,136,256]{2,1,0:T(8,128)(2,1)S(1)}, u32[]{:S(2)}, u32[]{:S(2)}) collective-permute-start(bf16[8,136,256]{2,1,0:T(8,128)(2,1)S(1)} %slice.89), channel_id=1, source_target_pairs={{0,2},{1,5},{2,0},{3,7},{4,6},{5,1},{6,4},{7,3},{8,10},{9,13},{10,... | collective-permute-start | bytes 1671176 | tf_op jit(solution)/shard_map/ppermute | solution.py:745
  39.8 11.2 %collective-permute-start.10 = (bf16[4,288,256]{2,1,0:T(8,128)(2,1)S(1)}, bf16[4,288,256]{2,1,0:T(8,128)(2,1)S(1)}, u32[]{:S(2)}, u32[]{:S(2)}) collective-permute-start(bf16[4,288,256]{2,1,0:T(8,128)(2,1)S(1)} %slice_bitcast_fusion), channel_id=1, source_target_pairs={{0,4},{1,3},{2,6},{3,1},{4,0},{5,7},{6,2},{7,5},{8,12},{9,11},{10,... | collective-permute-start | bytes 1769480 | tf_op jit(solution)/shard_map/ppermute | solution.py:745
  42.8 10.0 %collective-permute-start.6 = (bf16[4,136,256]{2,1,0:T(8,128)(2,1)S(1)}, bf16[4,136,256]{2,1,0:T(8,128)(2,1)S(1)}, u32[]{:S(2)}, u32[]{:S(2)}) collective-permute-start(bf16[4,136,256]{2,1,0:T(8,128)(2,1)S(1)} %slice.91), channel_id=1, source_target_pairs={{0,4},{1,3},{2,6},{3,1},{4,0},{5,7},{6,2},{7,5},{8,12},{9,11},{10,... | collective-permute-start | bytes 835592 | tf_op jit(solution)/shard_map/ppermute | solution.py:745
  48.8 14.9 %collective-permute-start.16 = (bf16[2,256,256]{2,1,0:T(8,128)(2,1)S(1)}, bf16[2,256,256]{2,1,0:T(8,128)(2,1)S(1)}, u32[]{:S(2)}, u32[]{:S(2)}) collective-permute-start(bf16[2,256,256]{2,1,0:T(8,128)(2,1)S(1)} %get-tuple-element.158), channel_id=1, source_target_pairs={{0,5},{1,2},{2,7},{3,0},{4,1},{5,6},{6,3},{7,4},{8,13},{9,10},{10,... | collective-permute-start | bytes 786440 | tf_op jit(solution)/shard_map/ppermute | solution.py:753
  50.1 13.6 %collective-permute-start.14 = (bf16[2,256,256]{2,1,0:T(8,128)(2,1)S(1)}, bf16[2,256,256]{2,1,0:T(8,128)(2,1)S(1)}, u32[]{:S(2)}, u32[]{:S(2)}) collective-permute-start(bf16[2,256,256]{2,1,0:T(8,128)(2,1)S(1)} %get-tuple-element.158), channel_id=1, source_target_pairs={{0,1},{1,0},{2,3},{3,2},{4,5},{5,4},{6,7},{7,6},{8,9},{9,8},{10,11... | collective-permute-start | bytes 786440 | tf_op jit(solution)/shard_map/ppermute | solution.py:749
  50.5 11.7 %collective-permute-start.15 = (bf16[2,256,256]{2,1,0:T(8,128)(2,1)S(1)}, bf16[2,256,256]{2,1,0:T(8,128)(2,1)S(1)}, u32[]{:S(2)}, u32[]{:S(2)}) collective-permute-start(bf16[2,256,256]{2,1,0:T(8,128)(2,1)S(1)} %get-tuple-element.157.refs_0_), channel_id=1, source_target_pairs={{0,2},{1,5},{2,0},{3,7},{4,6},{5,1},{6,4},{7,3},{8,10},{9,13},{10,... | collective-permute-start | bytes 786440 | tf_op jit(solution)/shard_map/ppermute | solution.py:745
  53.0 14.0 %collective-permute-start.11 = (bf16[424,256]{1,0:T(8,128)(2,1)S(1)}, bf16[424,256]{1,0:T(8,128)(2,1)S(1)}, u32[]{:S(2)}, u32[]{:S(2)}) collective-permute-start(bf16[424,256]{1,0:T(8,128)(2,1)S(1)} %get-tuple-element.210), channel_id=1, source_target_pairs={{0,8},{1,9},{2,10},{3,11},{4,12},{5,13},{6,14},{7,15},{8,0},{9,1},... | collective-permute-start | bytes 651272 | tf_op jit(solution)/shard_map/ppermute | solution.py:745
  54.8 13.4 %collective-permute-start.13 = (bf16[424,256]{1,0:T(8,128)(2,1)S(1)}, bf16[424,256]{1,0:T(8,128)(2,1)S(1)}, u32[]{:S(2)}, u32[]{:S(2)}) collective-permute-start(bf16[424,256]{1,0:T(8,128)(2,1)S(1)} %get-tuple-element.211), channel_id=1, source_target_pairs={{0,24},{1,25},{2,26},{3,27},{4,28},{5,29},{6,30},{7,31},{8,16},{9,... | collective-permute-start | bytes 651272 | tf_op jit(solution)/shard_map/ppermute | solution.py:745
  62.2 14.2 %collective-permute-start.12 = (bf16[424,256]{1,0:T(8,128)(2,1)S(1)}, bf16[424,256]{1,0:T(8,128)(2,1)S(1)}, u32[]{:S(2)}, u32[]{:S(2)}) collective-permute-start(bf16[424,256]{1,0:T(8,128)(2,1)S(1)} %get-tuple-element.212), channel_id=1, source_target_pairs={{0,16},{1,17},{2,18},{3,19},{4,20},{5,21},{6,22},{7,23},{8,24},{9,... | collective-permute-start | bytes 651272 | tf_op jit(solution)/shard_map/ppermute | solution.py:745
  77.4 20.8 %collective-permute-start.20 = (bf16[4,288,256]{2,1,0:T(8,128)(2,1)}, bf16[4,288,256]{2,1,0:T(8,128)(2,1)}, u32[]{:S(2)}, u32[]{:S(2)}) collective-permute-start(bf16[4,288,256]{2,1,0:T(8,128)(2,1)} %slice_bitcast_fusion.1), channel_id=1, source_target_pairs={{0,4},{1,3},{2,6},{3,1},{4,0},{5,7},{6,2},{7,5},{8,12},{9,11},{10,... | collective-permute-start | bytes 1769480 | tf_op jit(solution)/shard_map/ppermute | solution.py:745
  78.9 10.1 %collective-permute-start.19 = (bf16[424,256]{1,0:T(8,128)(2,1)S(1)}, bf16[424,256]{1,0:T(8,128)(2,1)S(1)}, u32[]{:S(2)}, u32[]{:S(2)}) collective-permute-start(bf16[424,256]{1,0:T(8,128)(2,1)S(1)} %fusion.4), channel_id=1, source_target_pairs={{0,24},{1,25},{2,26},{3,27},{4,28},{5,29},{6,30},{7,31},{8,16},{9,... | collective-permute-start | bytes 651272 | tf_op jit(solution)/shard_map/ppermute | solution.py:745
  81.6 16.5 %collective-permute-start.18 = (bf16[424,256]{1,0:T(8,128)(2,1)S(1)}, bf16[424,256]{1,0:T(8,128)(2,1)S(1)}, u32[]{:S(2)}, u32[]{:S(2)}) collective-permute-start(bf16[424,256]{1,0:T(8,128)(2,1)S(1)} %fusion.4), channel_id=1, source_target_pairs={{0,16},{1,17},{2,18},{3,19},{4,20},{5,21},{6,22},{7,23},{8,24},{9,... | collective-permute-start | bytes 651272 | tf_op jit(solution)/shard_map/ppermute | solution.py:745
  81.6 16.5 %collective-permute-start.17 = (bf16[424,256]{1,0:T(8,128)(2,1)S(1)}, bf16[424,256]{1,0:T(8,128)(2,1)S(1)}, u32[]{:S(2)}, u32[]{:S(2)}) collective-permute-start(bf16[424,256]{1,0:T(8,128)(2,1)S(1)} %fusion.4), channel_id=1, source_target_pairs={{0,8},{1,9},{2,10},{3,11},{4,12},{5,13},{6,14},{7,15},{8,0},{9,1},... | collective-permute-start | bytes 651272 | tf_op jit(solution)/shard_map/ppermute | solution.py:745
  84.7 14.6 %collective-permute-start.21 = (bf16[2,128,512]{2,1,0:T(8,128)(2,1)S(1)}, bf16[2,128,512]{2,1,0:T(8,128)(2,1)S(1)}, u32[]{:S(2)}, u32[]{:S(2)}) collective-permute-start(bf16[2,128,512]{2,1,0:T(8,128)(2,1)S(1)} %get-tuple-element.164), channel_id=1, source_target_pairs={{0,1},{1,0},{2,3},{3,2},{4,5},{5,4},{6,7},{7,6},{8,9},{9,8},{10,11... | collective-permute-start | bytes 786440 | tf_op jit(solution)/shard_map/ppermute | solution.py:749
  99.4 16.0 %collective-permute-start.23 = (bf16[4,424,256]{2,1,0:T(8,128)(2,1)S(1)}, bf16[4,424,256]{2,1,0:T(8,128)(2,1)S(1)}, u32[]{:S(2)}, u32[]{:S(2)}) collective-permute-start(bf16[4,424,256]{2,1,0:T(8,128)(2,1)S(1)} %pad_maximum_fusion.2), channel_id=1, source_target_pairs={{0,4},{1,3},{2,6},{3,1},{4,0},{5,7},{6,2},{7,5},{8,12},{9,11},{10,... | collective-permute-start | bytes 2605064 | tf_op jit(solution)/shard_map/ppermute | solution.py:745
  101.4 7.9 %collective-permute-start.24 = (bf16[288,256]{1,0:T(8,128)(2,1)S(1)}, bf16[288,256]{1,0:T(8,128)(2,1)S(1)}, u32[]{:S(2)}, u32[]{:S(2)}) collective-permute-start(bf16[288,256]{1,0:T(8,128)(2,1)S(1)} %get-tuple-element.213), channel_id=1, source_target_pairs={{0,8},{1,9},{2,10},{3,11},{4,12},{5,13},{6,14},{7,15},{8,0},{9,1},... | collective-permute-start | bytes 442376 | tf_op jit(solution)/shard_map/ppermute | solution.py:745
  101.5 8.3 %collective-permute-start.26 = (bf16[288,256]{1,0:T(8,128)(2,1)S(1)}, bf16[288,256]{1,0:T(8,128)(2,1)S(1)}, u32[]{:S(2)}, u32[]{:S(2)}) collective-permute-start(bf16[288,256]{1,0:T(8,128)(2,1)S(1)} %get-tuple-element.214), channel_id=1, source_target_pairs={{0,24},{1,25},{2,26},{3,27},{4,28},{5,29},{6,30},{7,31},{8,16},{9,... | collective-permute-start | bytes 442376 | tf_op jit(solution)/shard_map/ppermute | solution.py:745
  103.3 12.0 %collective-permute-start.25 = (bf16[288,256]{1,0:T(8,128)(2,1)S(1)}, bf16[288,256]{1,0:T(8,128)(2,1)S(1)}, u32[]{:S(2)}, u32[]{:S(2)}) collective-permute-start(bf16[288,256]{1,0:T(8,128)(2,1)S(1)} %get-tuple-element.215), channel_id=1, source_target_pairs={{0,16},{1,17},{2,18},{3,19},{4,20},{5,21},{6,22},{7,23},{8,24},{9,... | collective-permute-start | bytes 442376 | tf_op jit(solution)/shard_map/ppermute | solution.py:745
  115.5 18.2 %collective-permute-start.32 = (bf16[8,424,256]{2,1,0:T(8,128)(2,1)S(1)}, bf16[8,424,256]{2,1,0:T(8,128)(2,1)S(1)}, u32[]{:S(2)}, u32[]{:S(2)}) collective-permute-start(bf16[8,424,256]{2,1,0:T(8,128)(2,1)S(1)} %bitcast.78), channel_id=1, source_target_pairs={{0,1},{1,0},{2,3},{3,2},{4,5},{5,4},{6,7},{7,6},{8,9},{9,8},{10,11... | collective-permute-start | bytes 5210120 | tf_op jit(solution)/shard_map/ppermute | solution.py:749
  115.6 28.9 %collective-permute-start.34 = (bf16[8,424,256]{2,1,0:T(8,128)(2,1)S(1)}, bf16[8,424,256]{2,1,0:T(8,128)(2,1)S(1)}, u32[]{:S(2)}, u32[]{:S(2)}) collective-permute-start(bf16[8,424,256]{2,1,0:T(8,128)(2,1)S(1)} %bitcast.79), channel_id=1, source_target_pairs={{0,2},{1,5},{2,0},{3,7},{4,6},{5,1},{6,4},{7,3},{8,10},{9,13},{10,... | collective-permute-start | bytes 5210120 | tf_op jit(solution)/shard_map/ppermute | solution.py:745
  119.9 8.7 %collective-permute-start.30 = (bf16[288,256]{1,0:T(8,128)(2,1)S(1)}, bf16[288,256]{1,0:T(8,128)(2,1)S(1)}, u32[]{:S(2)}, u32[]{:S(2)}) collective-permute-start(bf16[288,256]{1,0:T(8,128)(2,1)S(1)} %fusion.7), channel_id=1, source_target_pairs={{0,24},{1,25},{2,26},{3,27},{4,28},{5,29},{6,30},{7,31},{8,16},{9,... | collective-permute-start | bytes 442376 | tf_op jit(solution)/shard_map/ppermute | solution.py:745
  121.9 11.8 %collective-permute-start.29 = (bf16[288,256]{1,0:T(8,128)(2,1)S(1)}, bf16[288,256]{1,0:T(8,128)(2,1)S(1)}, u32[]{:S(2)}, u32[]{:S(2)}) collective-permute-start(bf16[288,256]{1,0:T(8,128)(2,1)S(1)} %fusion.7), channel_id=1, source_target_pairs={{0,16},{1,17},{2,18},{3,19},{4,20},{5,21},{6,22},{7,23},{8,24},{9,... | collective-permute-start | bytes 442376 | tf_op jit(solution)/shard_map/ppermute | solution.py:745
  122.2 11.5 %collective-permute-start.28 = (bf16[288,256]{1,0:T(8,128)(2,1)S(1)}, bf16[288,256]{1,0:T(8,128)(2,1)S(1)}, u32[]{:S(2)}, u32[]{:S(2)}) collective-permute-start(bf16[288,256]{1,0:T(8,128)(2,1)S(1)} %fusion.7), channel_id=1, source_target_pairs={{0,8},{1,9},{2,10},{3,11},{4,12},{5,13},{6,14},{7,15},{8,0},{9,1},... | collective-permute-start | bytes 442376 | tf_op jit(solution)/shard_map/ppermute | solution.py:745
  133.8 10.6 %collective-permute-start.33 = (bf16[4,288,256]{2,1,0:T(8,128)(2,1)S(1)}, bf16[4,288,256]{2,1,0:T(8,128)(2,1)S(1)}, u32[]{:S(2)}, u32[]{:S(2)}) collective-permute-start(bf16[4,288,256]{2,1,0:T(8,128)(2,1)S(1)} %pad_maximum_fusion.3), channel_id=1, source_target_pairs={{0,4},{1,3},{2,6},{3,1},{4,0},{5,7},{6,2},{7,5},{8,12},{9,11},{10,... | collective-permute-start | bytes 1769480 | tf_op jit(solution)/shard_map/ppermute | solution.py:745
  144.5 10.8 %collective-permute-start.37 = (bf16[8,424,256]{2,1,0:T(8,128)(2,1)S(1)}, bf16[8,424,256]{2,1,0:T(8,128)(2,1)S(1)}, u32[]{:S(2)}, u32[]{:S(2)}) collective-permute-start(bf16[8,424,256]{2,1,0:T(8,128)(2,1)S(1)} %collective-permute-done.34.mine.mine1), channel_id=1, source_target_pairs={{0,1},{1,0},{2,3},{3,2},{4,5},{5,4},{6,7},{7,6},{8,9},{9,8},{10,11... | collective-permute-start | bytes 5210120 | tf_op jit(solution)/shard_map/ppermute | solution.py:749
  144.7 7.9 %collective-permute-start.38 = (bf16[8,288,256]{2,1,0:T(8,128)(2,1)S(1)}, bf16[8,288,256]{2,1,0:T(8,128)(2,1)S(1)}, u32[]{:S(2)}, u32[]{:S(2)}) collective-permute-start(bf16[8,288,256]{2,1,0:T(8,128)(2,1)S(1)} %bitcast.82), channel_id=1, source_target_pairs={{0,1},{1,0},{2,3},{3,2},{4,5},{5,4},{6,7},{7,6},{8,9},{9,8},{10,11... | collective-permute-start | bytes 3538952 | tf_op jit(solution)/shard_map/ppermute | solution.py:749
  145.1 16.7 %collective-permute-start.36 = (bf16[8,288,256]{2,1,0:T(8,128)(2,1)S(1)}, bf16[8,288,256]{2,1,0:T(8,128)(2,1)S(1)}, u32[]{:S(2)}, u32[]{:S(2)}) collective-permute-start(bf16[8,288,256]{2,1,0:T(8,128)(2,1)S(1)} %bitcast.83), channel_id=1, source_target_pairs={{0,2},{1,5},{2,0},{3,7},{4,6},{5,1},{6,4},{7,3},{8,10},{9,13},{10,... | collective-permute-start | bytes 3538952 | tf_op jit(solution)/shard_map/ppermute | solution.py:745
  (10 other events, 40.5 us)

commit v4 on v3

--- a/solution.py
+++ b/solution.py
@@ -139,8 +139,9 @@
 
 
 def entry_body(
-    place_ref, mine_hbm, other_ref, vec_ref, w1, gy_hbm, w2_hbm, wq_hbm, wk_hbm, wv_hbm, wo_hbm,
-    own_ref, chip_ref, near_ref, far_ref, norm2_ref, scale2_ref, x_ref, gy_ref, w2, wq, wk, wv, wo, s_ref, sems, *, side,
+    place_ref, mine_hbm, other_ref, vec_ref, w1_hbm, gy_hbm, w2_hbm, wq_hbm, wk_hbm, wv_hbm, wo_hbm,
+    own_ref, chip_ref, near_ref, far_ref, norm2_ref, scale2_ref, x_ref, gy_ref, w2, wq, wk, wv, wo, w1, s_ref, sems,
+    *, side,
 ):
     images, px, ch = x_ref.shape
     part = px // 2
@@ -150,7 +151,7 @@
     there = pl.multiple_of((1 - core) * part, part)
     copies = start_copies(
         [(mine_hbm.at[core * images + i], x_ref.at[i, pl.ds(here, part)]) for i in range(images)]
-        + [(w2_hbm, w2), (gy_hbm, gy_ref), (wq_hbm, wq), (wk_hbm, wk), (wv_hbm, wv), (wo_hbm, wo)],
+        + [(w1_hbm, w1), (w2_hbm, w2), (gy_hbm, gy_ref), (wq_hbm, wq), (wk_hbm, wk), (wv_hbm, wv), (wo_hbm, wo)],
         sems,
     )
 
@@ -165,7 +166,7 @@
 
     clear_edges(s_ref, side)
     for i in range(images):
-        x_ref[i, pl.ds(there, part), :] = other_ref[i]
+        x_ref[i, pl.ds(there, part), :] = other_ref[core * images + i]
     for c in copies[:images]:
         c.wait()
     active = []
@@ -174,6 +175,7 @@
         active.append(y * sigmoid(y))
         put_shifts(s_ref, i, active[i], side)
     give(0, active)
+    copies[images].wait()
     filtered = conv(s_ref, w1, px, side, ch) + row(2)
     active = []
     for i, (n, r) in enumerate(normalized([filtered[i * px : (i + 1) * px] for i in range(images)])):
@@ -182,30 +184,30 @@
         y = n * row(3) + row(4)
         active.append(y * sigmoid(y))
     give(1, active)
-    for c in copies[images:]:
+    for c in copies[images + 1 :]:
         c.wait()
 
 
 def run_entry(place, mine, other, vec, w1, gy, w2, weights, side):
-    images, part, ch = other.shape
-    px = 2 * part
+    images, px, ch = gy.shape
     acts = shape_of((2, images, px, ch // 2), BF)
     whole = (images, px, ch)
     return pl.pallas_call(
         functools.partial(entry_body, side=side),
         name="entry",
-        in_specs=[SMEM, HBM] + [VMEM] * 3 + [HBM] * 6,
+        in_specs=[SMEM, HBM] + [VMEM] * 2 + [HBM] * 7,
         out_specs=[VMEM] * 13,
         out_shape=[acts] * 4
         + [shape_of(whole, F32), shape_of((images, ch), F32), shape_of(whole, BF), shape_of(whole, BF), shape_of(w2.shape, BF)]
         + [shape_of((ch, ch), BF)] * 4,
         scratch_shapes=[
+            pltpu.VMEM(w1.shape, BF),
             pltpu.VMEM((images, px + 2 * side, 3 * ch), BF),
-            pltpu.SemaphoreType.DMA((images + 6,)),
+            pltpu.SemaphoreType.DMA((images + 7,)),
         ],
         cost_estimate=took(8.5),
-        compiler_params=pltpu.CompilerParams(vmem_limit_bytes=12 << 20),
-    )(place, hbm(mine), other, vec, w1, *[hbm(v) for v in (gy, w2, *weights)])
+        compiler_params=pltpu.CompilerParams(vmem_limit_bytes=16 << 20),
+    )(place, hbm(mine), other, vec, *[hbm(v) for v in (w1, gy, w2, *weights)])
 
 
 def attention_body(
@@ -247,18 +249,18 @@
     keys = mm(nb, wk[...]).astype(BF)
     values = (mm(nb, wv[...]) + row(9)).astype(BF)
     scale = ch ** -0.5
-    for i, qi, ki, vi, di in zip(every, spans(queries), spans(keys), spans(values), spans(dm)):
-        scores = mm(qi, ki, NT) * scale
-        dp = mm(di, vi, NT)
-        peak = jnp.max(scores, axis=1, keepdims=True)
-        lifted = jnp.exp(scores - peak)
-        probs = lifted / jnp.sum(lifted, axis=1, keepdims=True)
-        pb = probs.astype(BF)
-        mixed[i] = mm(pb, vi).astype(BF)
-        qkv[i, :, 2 * ch :] = mm(pb, di, TN).astype(BF)
-        ds = (probs * (dp - jnp.sum(probs * dp, axis=1, keepdims=True))).astype(BF)
-        qkv[i, :, :ch] = (mm(ds, ki) * scale).astype(BF)
-        qkv[i, :, ch : 2 * ch] = (mm(ds, qi, TN) * scale).astype(BF)
+    q, k, v, d = spans(queries), spans(keys), spans(values), spans(dm)
+    scores = [mm(q[i], k[i], NT) * scale for i in every]
+    dp = [mm(d[i], v[i], NT) for i in every]
+    lifted = [jnp.exp(t - jnp.max(t, axis=1, keepdims=True)) for t in scores]
+    probs = [t / jnp.sum(t, axis=1, keepdims=True) for t in lifted]
+    low = [t.astype(BF) for t in probs]
+    ds = [(p * (t - jnp.sum(p * t, axis=1, keepdims=True))).astype(BF) for p, t in zip(probs, dp)]
+    for i in every:
+        mixed[i] = mm(low[i], v[i]).astype(BF)
+        qkv[i, :, 2 * ch :] = mm(low[i], d[i], TN).astype(BF)
+        qkv[i, :, :ch] = (mm(ds[i], k[i]) * scale).astype(BF)
+        qkv[i, :, ch : 2 * ch] = (mm(ds[i], q[i], TN) * scale).astype(BF)
     cotangents = qkv[...].reshape(images * px, 3 * ch)
     dq, dk, dv = [cotangents[:, j * ch : (j + 1) * ch] for j in range(3)]
     dn = mm(dq, wq[...], NT) + mm(dk, wk[...], NT) + mm(dv, wv[...], NT)
@@ -378,13 +380,15 @@
 
 
 def back1_body(
-    place_ref, dfull_ref, x_ref, dres_ref, vec_ref, w1,
-    out_hbm, send_ref, stat_ref, s_ref, keep_ref, sem, *, side,
+    place_ref, dfull_ref, x_ref, dres_ref, vec_ref, w1_hbm,
+    out_hbm, send_ref, stat_ref, w1, s_ref, keep_ref, sem, *, side,
 ):
     images, px, ch = dres_ref.shape
     part = px // 2
     core = place_ref[0]
     every = range(images)
+    fetch = pltpu.make_async_copy(w1_hbm, w1, sem)
+    fetch.start()
     clear_edges(s_ref, side)
 
     def row(i):
@@ -392,6 +396,7 @@
 
     for i in every:
         put_shifts(s_ref, i, dfull_ref[i].astype(F32), side)
+    fetch.wait()
     da = conv_back(s_ref, w1, px, side, ch)
     norms = normalized([x_ref[i].astype(F32) for i in every])
     ns = [n for n, _ in norms]
@@ -416,17 +421,18 @@
     return pl.pallas_call(
         functools.partial(back1_body, side=side),
         name="conv1_back",
-        in_specs=[SMEM] + [VMEM] * 5,
+        in_specs=[SMEM] + [VMEM] * 4 + [HBM],
         out_specs=[HBM, VMEM, VMEM],
         out_shape=[shape_of((2 * images, px // 2, ch), BF), shape_of(part, BF), shape_of((8, ch), F32)],
         scratch_shapes=[
+            pltpu.VMEM(w1.shape, BF),
             pltpu.VMEM((images, px + 2 * side, 3 * ch), BF),
             pltpu.VMEM(part, BF),
             pltpu.SemaphoreType.DMA(()),
         ],
         cost_estimate=took(0.1),
-        compiler_params=pltpu.CompilerParams(vmem_limit_bytes=12 << 20),
-    )(place, dfull, x, dres, vec, w1)
+        compiler_params=pltpu.CompilerParams(vmem_limit_bytes=16 << 20),
+    )(place, dfull, x, dres, vec, hbm(w1))
 
 
 def place_rows_body(place_ref, got_ref, into_hbm, out_hbm, token_ref, sem):
@@ -469,7 +475,7 @@
         lax.fori_loop(0, images, fill, 0)
 
 
-def run_turn(which, acts, side):
+def run_turn(which, acts, side, us):
     _, images, px, part = acts[0].shape
     return pl.pallas_call(
         functools.partial(turn_body, side=side, which=which),
@@ -477,63 +483,66 @@
         in_specs=[VMEM] * 4,
         out_specs=VMEM,
         out_shape=shape_of((3 * part, 4 * images * px), BF),
-        cost_estimate=took(2),
+        cost_estimate=took(us),
         compiler_params=pltpu.CompilerParams(vmem_limit_bytes=6 << 20),
     )(*acts)
 
 
-def kernel_grad_body(place_ref, s_ref, *refs, side):
+def kernel_grad_body(place_ref, s_ref, *refs, side, other):
     *grads, out_ref, d_ref = refs
     images, px, half = grads[0].shape
     part = s_ref.shape[0] // 3
-    bits = place_ref[8]
-    first, second, _, _ = out_ref.shape
-    owners = first * second
-    rows = part // owners
+    owners = out_ref.shape[0]
+    rows = part // (2 * owners)
+    mine = place_ref[8] // owners
+    bits = place_ref[8] % owners
+    block = (1 - mine) if other else mine
     zero = jnp.zeros((side, half), BF)
     for n, d in enumerate(grads):
         for i in range(images):
             d_ref[n * images + i, 0:side, :] = zero
             d_ref[n * images + i, side : px + side, :] = d[i]
             d_ref[n * images + i, px + side :, :] = zero
+    some = part // 2
+    lhs = jnp.concatenate(
+        [s_ref[pl.ds(pl.multiple_of(dw * part + block * some, some), some), :] for dw in range(3)], axis=0
+    )
     for dh in range(3):
         start = (2 - dh) * side
         d = jnp.concatenate([d_ref[n, start : start + px, :] for n in range(4 * images)], axis=0)
-        g = mm(s_ref[...], d).astype(BF)
+        g = mm(lhs, d).astype(BF)
         for o in range(owners):
-            at = o ^ bits
             for dw in range(3):
                 tap = dh * 3 + dw
-                begin = dw * part + o * rows
-                out_ref[at // second, at % second, tap * rows : (tap + 1) * rows, :] = g[begin : begin + rows]
-
-
-def run_kernel_grad(place, turned, grads, lead, side, us, name):
+                begin = dw * some + o * rows
+                out_ref[o ^ bits, tap * rows : (tap + 1) * rows, :] = g[begin : begin + rows]
+
+
+def run_kernel_grad(place, turned, grads, owners, side, other, us, name):
     images, px, half = grads[0].shape
     part = turned.shape[0] // 3
-    rows = 9 * (part // (lead[0] * lead[1]))
-    return pl.pallas_call(
-        functools.partial(kernel_grad_body, side=side),
+    return pl.pallas_call(
+        functools.partial(kernel_grad_body, side=side, other=other),
         name=name,
         in_specs=[SMEM] + [VMEM] * 5,
         out_specs=VMEM,
-        out_shape=shape_of((lead[0], lead[1], rows, half), BF),
+        out_shape=shape_of((owners, 9 * (part // (2 * owners)), half), BF),
         scratch_shapes=[pltpu.VMEM((4 * images, px + 2 * side, half), BF)],
         cost_estimate=took(us),
         compiler_params=pltpu.CompilerParams(vmem_limit_bytes=10 << 20),
     )(place, turned, *grads)
 
 
-def prepare_body(place_ref, ids_hbm, dead_hbm, replace_hbm, latents_hbm, w1_hbm, *refs):
-    count_vectors = (len(refs) - 12) // 2
+def prepare_body(place_ref, ids_hbm, dead_hbm, replace_hbm, latents_hbm, *refs):
+    count_vectors = (len(refs) - 10) // 2
     vectors = refs[:count_vectors]
-    counts_ref, slots_ref, keep_ref, send_ref, vec_ref, w1_ref = refs[count_vectors : count_vectors + 6]
-    lines = refs[count_vectors + 6 : 2 * count_vectors + 6]
-    ids_ref, dead_ref, replace_ref, latents_ref, sems, _ = refs[2 * count_vectors + 6 :]
+    counts_ref, slots_ref, keep_ref, send_ref, vec_ref = refs[count_vectors : count_vectors + 5]
+    lines = refs[count_vectors + 5 : 2 * count_vectors + 5]
+    ids_ref, dead_ref, replace_ref, latents_ref, sems = refs[2 * count_vectors + 5 :]
     copies = start_copies(
         (
             (ids_hbm, ids_ref), (dead_hbm, dead_ref), (replace_hbm, replace_ref), (latents_hbm, latents_ref),
-            *zip(vectors, lines), (w1_hbm, w1_ref),
+            *zip(vectors, lines),
         ),
         sems,
     )
@@ -573,28 +582,28 @@
         vec_ref[i : i + 1, :] = line[...].astype(F32).reshape(1, -1)
 
 
-def run_prepare(place, ids, dead, replace, latents, w1, vectors, owners):
+def run_prepare(place, ids, dead, replace, latents, vectors, owners):
     codes = dead.shape[1]
     pixels, width = latents.shape
-    ch = w1.shape[1]
+    ch = vectors[0].shape[0]
     rows = shape_of((owners, DEAD // (2 * owners), width), BF)
     return pl.pallas_call(
         prepare_body,
         name="prepare",
-        in_specs=[SMEM] + [HBM] * (5 + len(vectors)),
-        out_specs=[VMEM] * 6,
+        in_specs=[SMEM] + [HBM] * (4 + len(vectors)),
+        out_specs=[VMEM] * 5,
         out_shape=[
             shape_of((8, codes), F32), shape_of((DEAD, codes), BF), rows, rows,
-            shape_of((16, ch), F32), shape_of(w1.shape, BF),
+            shape_of((16, ch), F32),
         ],
         scratch_shapes=[pltpu.VMEM((ch,), BF)] * len(vectors)
         + [
             pltpu.VMEM((1, pixels), jnp.int32), pltpu.VMEM((1, codes), jnp.int32), pltpu.VMEM((1, codes), jnp.int32),
-            pltpu.VMEM((pixels, width), BF), pltpu.SemaphoreType.DMA((5 + len(vectors),)), pltpu.SMEM((1,), jnp.int32),
+            pltpu.VMEM((pixels, width), BF), pltpu.SemaphoreType.DMA((4 + len(vectors),)),
         ],
         cost_estimate=took(2.2),
         compiler_params=pltpu.CompilerParams(vmem_limit_bytes=16 << 20),
-    )(place, *[hbm(v) for v in (ids, dead, replace, latents, w1, *vectors)])
+    )(place, *[hbm(v) for v in (ids, dead, replace, latents, *vectors)])
 
 
 def spread_all(place_ref, pieces, buf, sem, taps_out, outs, start=0):
@@ -602,13 +611,13 @@
     ats = (place_ref[4], place_ref[5])
     copies = []
     step = 0
-    for piece, beyond, far in pieces:
+    for piece, beyond, first in pieces:
         owners = piece.shape[0]
         _, groups, rows, cols = buf.shape
         high = core ^ beyond
         for j in range(owners):
             buf[step] = piece[j, start : start + groups * rows, :].astype(F32).reshape(groups, rows, cols)
-            at = pl.ds(pl.multiple_of(((j + far * owners) ^ ats[beyond]) * rows, rows), rows)
+            at = pl.ds(pl.multiple_of(((j + first) ^ ats[beyond]) * rows, rows), rows)
             to = pl.ds(pl.multiple_of(high * cols, cols), cols)
             if taps_out is None:
                 new = [pltpu.make_async_copy(buf.at[step, g], out.at[at, to], sem) for g, out in enumerate(outs)]
@@ -625,9 +634,9 @@
 def attention_finish_body(place_ref, mine0, other0, mine1, other1, slots_ref, book_ref, *refs):
     *outs, out_ref, rows_ref, buf, sem = refs
     device = place_ref[3]
-    pieces = ((mine0, 0, 0), (other0, 1, 0), (mine1, 0, 1), (other1, 1, 1))
     entries, width = book_ref.shape
     owners, total, _ = mine0.shape
+    pieces = ((mine0, 0, 0), (other0, 1, 0), (mine1, 0, owners), (other1, 1, owners))
     count = DEAD // (4 * owners)
     start = total - count
     rows_ref[:, width:] = jnp.ones((DEAD, 128), F32)
@@ -664,26 +673,30 @@
     )(place, *pieces, slots, book)
 
 
-def conv_finish_body(place_ref, mine, other, *refs, far):
+def conv_finish_body(place_ref, *refs, firsts):
     out_ref, buf, sem = refs[-3:]
-    spread_all(place_ref, ((mine, 0, far), (other, 1, far)), buf, sem, out_ref, ())
-
-
-def run_conv_finish(place, mine, other, into, ch, name):
-    owners, total, half = mine.shape
-    rows = ch // (2 * owners)
+    pieces = [(refs[n], n % 2, firsts[n // 2]) for n in range(2 * len(firsts))]
+    spread_all(place_ref, pieces, buf, sem, out_ref, ())
+
+
+def run_conv_finish(place, pieces, into, ch, total, name):
+    arrays = [a for mine, other, _ in pieces for a in (mine, other)]
+    rows = ch // total
+    half = arrays[0].shape[2]
     given = [] if into is None else [into]
     return pl.pallas_call(
-        functools.partial(conv_finish_body, far=len(given)),
+        functools.partial(conv_finish_body, firsts=[first for _, _, first in pieces]),
         name=name,
-        in_specs=[SMEM] + [VMEM] * 2 + [HBM] * len(given),
+        in_specs=[SMEM] + [VMEM] * len(arrays) + [HBM] * len(given),
         out_specs=HBM,
         out_shape=shape_of((9, ch, ch), F32),
-        scratch_shapes=[pltpu.VMEM((2 * owners, 9, rows, half), F32), pltpu.SemaphoreType.DMA(())],
-        input_output_aliases={3: 0} if given else {},
-        cost_estimate=took(3.5),
+        scratch_shapes=[
+            pltpu.VMEM((sum(a.shape[0] for a in arrays), 9, rows, half), F32), pltpu.SemaphoreType.DMA(()),
+        ],
+        input_output_aliases={1 + len(arrays): 0} if given else {},
+        cost_estimate=took(3),
         compiler_params=pltpu.CompilerParams(vmem_limit_bytes=12 << 20),
-    )(place, mine, other, *given)
+    )(place, *arrays, *given)
 
 
 def together(*values):
@@ -752,10 +765,10 @@
         pairs = [(g * 2 + c, (g ^ self.key(1, 1 - c)) * 2 + 1 - c) for g in range(self.chips) for c in range(2)]
         return lax.ppermute(value, AXES, pairs)
 
-    def reduce(self, value, dim, keep=None):
+    def reduce(self, value, dim):
         shift, size = self.dims[dim]
         got = [self.send(value[k], k << shift) for k in range(1, 1 << size)]
-        total = (value if keep is None else keep)[0].astype(F32)
+        total = value[0].astype(F32)
         for g in got:
             total = total + g.astype(F32)
         return total.astype(BF)
@@ -798,16 +811,16 @@
         mine_at // low, other_at // low, mine_at % low,
     ])
     mine = image_rows.reshape(all_images, part, ch)
-    other = links.partner(lax.dynamic_slice_in_dim(mine, (1 - core) * images, images))
+    other = links.partner(mine)
     vectors = [
         norm1_gain, norm1_bias, conv1_bias, norm2_gain, norm2_bias, conv2_bias,
         norm3_gain, norm3_bias, query_bias, value_bias, out_bias,
     ]
     codes = dead_flags.shape[0]
-    counts, slots, ckeep, csend, vec, w1 = run_prepare(
-        place, code_ids.reshape(1, -1), dead_flags.reshape(1, -1), replace_ids.reshape(1, -1), latents,
-        conv1_kernel.reshape(9 * ch, ch), vectors, owners,
+    counts, slots, ckeep, csend, vec = run_prepare(
+        place, code_ids.reshape(1, -1), dead_flags.reshape(1, -1), replace_ids.reshape(1, -1), latents, vectors, owners
     )
+    w1 = conv1_kernel.reshape(9 * ch, ch)
     own, to_chip, to_near, to_far, norm2, scale2, x, gy, w2, *weights = run_entry(
         place, mine, other, vec, w1, grad_out.reshape(images, px, ch), conv2_kernel.reshape(9 * ch, ch),
         (query_weight, key_weight, value_weight, out_weight), side,
@@ -823,7 +836,6 @@
     attn_got = links.send(attn[1], 1)
     lead = links.lead()
     rest = range(1, len(lead))
-    split = (lead[0], low // lead[0])
 
     def reduce(value, dims):
         for dim in dims:
@@ -838,25 +850,35 @@
     def owned(value):
         return value.reshape((low,) + value.shape[-2:])
 
-    sum2 = run_kernel_grad(place, run_turn(1, acts, side), grads2, split, side, 3, "conv2_grad")
-    sum2_keep, dres = together(sum2, dres)
+    turned = run_turn(1, acts, side, 2)
+    give2 = run_kernel_grad(place, turned, grads2, low // 2, side, True, 1.6, "conv2_grad_other")
+    give2, dres, turned = together(give2, dres, turned)
+    keep2 = run_kernel_grad(place, turned, grads2, low // 2, side, False, 1.6, "conv2_grad")
+    attn_got, keep2, dres = together(attn_got, keep2, dres)
     dkeep1, dsend1, dfull1, stat_b = run_back2(place, dres, norm2, scale2, vec, w2, side)
     attn = (attn[0].astype(F32) + attn_got.astype(F32)).astype(BF)
     attn = attn.reshape(lead + attn.shape[1:])
-    sum2 = sum2.reshape(lead + sum2.shape[2:])
     attn = reduce(attn, [0])
-    sum2 = links.reduce(sum2, 0, sum2_keep.reshape(sum2.shape))
+    first = 1 << links.dims[0][0]
+
+    def paired(keep, give):
+        total = (keep.astype(F32) + links.send(give, first).astype(F32)).astype(BF)
+        return total.reshape(lead[1:] + total.shape[1:])
+
+    sum2 = paired(keep2, give2)
     grads1 = [dkeep1, links.partner(dsend1), links.send(dkeep1, 1), links.far(dsend1)]
     attn, sum2, stat_b, dfull1, grads1[0], *acts = together(attn, sum2, stat_b, dfull1, dkeep1, *acts)
     sum2 = reduce(jnp.concatenate([sum2, attn], axis=-2), rest)
-    sum1 = run_kernel_grad(place, run_turn(0, acts, side), grads1, split, side, 0.1, "conv1_grad")
+    turned = run_turn(0, acts, side, 0.1)
+    give1 = run_kernel_grad(place, turned, grads1, low // 2, side, True, 0.1, "conv1_grad_other")
+    keep1 = run_kernel_grad(place, turned, grads1, low // 2, side, False, 0.1, "conv1_grad")
     rows_out, in_send, stat_c = run_back1(place, dfull1, x, dres, vec, w1, side)
-    sum2, sum1, in_send, stat_c = together(sum2, sum1, in_send, stat_c)
+    sum2, keep1, give1, in_send, stat_c = together(sum2, keep1, give1, in_send, stat_c)
     vectors = jnp.concatenate([stat_c[:2], stat_b[2:3], stat_b[:2], stat_a[:6], counts[:1].reshape(-1, ch)])
     steps = links.small_steps()
     sum2 = gather(sum2, rest)
-    sum1 = sum1.reshape(lead + sum1.shape[2:])
-    sum1 = reduce(sum1, [0])
+    sum1 = paired(keep1, give1)
+    sum1, in_send = together(sum1, in_send)
     in_got = links.partner(in_send)
     vectors = steps[0](vectors)
     sum2, sum1, in_got, vectors = together(sum2, sum1, in_got, vectors)
@@ -870,24 +892,28 @@
     vectors = steps[2](vectors)
     input_grad, _ = run_place_rows(place, in_got, rows_out)
     sum1, vectors, other2, input_grad = together(sum1, vectors, other2, input_grad)
-    sum1 = owned(gather(sum1, [0]))
-    vectors = steps[3](vectors)
-    grad2 = run_conv_finish(place, sum2, other2, None, ch, "conv2_finish")
-    sum1, far2, vectors, grad2 = together(sum1, far2, vectors, grad2)
-    far1 = links.send(sum1, 1)
-    other1 = links.partner(sum1)
+    shift, size = links.dims[0]
+    each = low >> size
+    parts1 = [sum1.reshape((-1,) + sum1.shape[-2:])]
+    parts1 += [links.send(parts1[0], k << shift) for k in range(1, 1 << size)]
+    for step in steps[3:]:
+        vectors = step(vectors)
+    grad2 = run_conv_finish(place, [(sum2, other2, 0)], None, ch, owners, "conv2_finish")
+    *parts1, far2, vectors, grad2 = together(*parts1, far2, vectors, grad2)
+    far1 = [links.send(p, 1) for p in parts1]
+    other1 = [links.partner(p) for p in parts1]
     other_far2 = links.partner(far2)
-    for step in steps[4:]:
-        vectors = step(vectors)
+    near1 = [(m, o, n * each) for n, (m, o) in enumerate(zip(parts1, other1))]
+    grad1 = run_conv_finish(place, near1, None, ch, owners, "conv1_finish")
     qg, kg, vg, og, new_codebook = run_attention_finish(
         place, (sum2, other2, far2, other_far2), slots, codebook, ch
     )
-    grad2 = run_conv_finish(place, far2, other_far2, grad2, ch, "conv2_finish")
-    grad1 = run_conv_finish(place, sum1, other1, None, ch, "conv1_finish")
-    far1, grad2, grad1, vectors, new_codebook = together(far1, grad2, grad1, vectors, new_codebook)
+    grad2 = run_conv_finish(place, [(far2, other_far2, low)], grad2, ch, owners, "conv2_finish")
+    *far1, grad2, grad1, vectors, new_codebook = together(*far1, grad2, grad1, vectors, new_codebook)
     *vec_grads, usage, perplexity = run_vectors(vectors, 11, codes)
     (g1, b1, cb1, g2, b2, cb2, g3, b3, qb, vb, ob) = [v.reshape(ch) for v in vec_grads]
-    grad1 = run_conv_finish(place, far1, links.partner(far1), grad1, ch, "conv1_finish")
+    far1 = [(p, links.partner(p), low + n * each) for n, p in enumerate(far1)]
+    grad1 = run_conv_finish(place, far1, grad1, ch, owners, "conv1_finish")
     input_grad = input_grad.reshape(image_rows.shape)
     kernel_shape = (3, 3, ch, ch)
     return (

time: 168 us -> 163 us (0.970)
  waiting for transfers between devices: 61.1 us -> 52.4 us
  starting transfers between devices: 43.2 us -> 47 us
  Pallas kernels: 56.5 us -> 60 us
  local copies, waits for them, and re-layouts: 2.32 us -> 0.45 us
    ppermute x27 -> x28, waiting for transfers between devices: 58.5 us -> 46.3 us  [send(): return lax.ppermute(value, AXES, pairs)]
    ppermute x27 -> x28, starting transfers between devices: 35 us -> 37.8 us  [send(): return lax.ppermute(value, AXES, pairs)]
    pallas_call x1, Pallas kernels: 4.87 us -> 7.21 us  [run_back1(): pl.pallas_call(functools.partial(back1_body, side=side), name='conv1_back...]
    ppermute x11 -> x13, waiting for transfers between devices: 2.56 us -> 4.4 us  [partner(): return lax.ppermute(value, AXES, pairs)]
    pallas_call x7 -> x9, Pallas kernels: 20.6 us -> 21.4 us  [the longest x4 10.9 us: run_conv_finish(): pl.pallas_call(functools.partial(conv_finish_body, firsts=[first for _, _...]
  transfers between devices with their start and end apart: 41 -> 44, of which waited for: 19 -> 23; matrix products, arithmetic and copies ran while one was open for 2% -> 1% of each run, Pallas kernels for 28% -> 31%
where the time goes in v4:
time: 163 us
  Pallas kernels  60 us (37%)
  waiting for transfers between devices  52.4 us (32%)
  starting transfers between devices  47 us (29%)
  other arithmetic  2.12 us (1%)
    ppermute x28, waiting for transfers between devices, send(): return lax.ppermute(value, AXES, pairs)  46.3 us
    ppermute x28, starting transfers between devices, send(): return lax.ppermute(value, AXES, pairs)  37.8 us
    pallas_call x4, Pallas kernels, run_conv_finish(): pl.pallas_call(functools.partial(conv_finish_body, firsts=[first for _, _...  10.9 us
    pallas_call x1, Pallas kernels, run_attention(): pl.pallas_call(functools.partial(attention_body, side=side), name='attent...  10.1 us
    pallas_call x4, Pallas kernels, run_kernel_grad(): pl.pallas_call(functools.partial(kernel_grad_body, side=side, other=other...  7.81 us
    pallas_call x1, Pallas kernels, run_entry(): pl.pallas_call(functools.partial(entry_body, side=side), name='entry', in...  7.31 us
    pallas_call x1, Pallas kernels, run_back1(): pl.pallas_call(functools.partial(back1_body, side=side), name='conv1_back...  7.21 us
    ppermute x3, starting transfers between devices, far(): return lax.ppermute(value, AXES, pairs)  6.21 us
  transfers between devices with their start and end apart: 44, of which 23 were waited for; matrix products, arithmetic and copies ran while one was open for 1% of the time, Pallas kernels for 31%

profile of v4, /device:TPU:0, one launch (start us, length us, event | category | flops | bytes accessed | tf_op | source)
XLA Modules:
  0.0 163.2 jit_solution(161429415475631533)
XLA Ops:
  1.3 2.7 %prepare.1 = (f32[8,1024]{1,0:T(8,128)S(1)}, bf16[256,1024]{1,0:T(8,128)(2,1)S(1)}, bf16[16,8,256]{2,1,0:T(8,128)(2,1)S(1)}, bf16[16,8,256]{2,1,0:T(8,128)(2,1)S(1)}, f32[16,512]{1,0:T(8,128)S(1)}) custom-call(s32[9]{0:T(128)S(1)} %stack.78.place_ref, s32[1,512]{1,0:T(1,128)} %bitcast.91, s32[1,1024]{1,0:T(1,128)} %bitcast.89, s32[1,1024]{1,0:T(1,128)} %bitcast.90, ...), custom_call_target="tpu_custom_call" | custom-call | flops 2529999872 | bytes 1048576 | tf_op jit(solution)/shard_map/prepare/pallas_call | solution.py:590
  4.0 7.3 %entry.1 = (bf16[2,2,256,256]{3,2,1,0:T(8,128)(2,1)S(1)}, bf16[2,2,256,256]{3,2,1,0:T(8,128)(2,1)S(1)}, bf16[2,2,256,256]{3,2,1,0:T(8,128)(2,1)S(1)}, bf16[2,2,2...) custom-call(s32[9]{0:T(128)S(1)} %stack.78.place_ref, ...), custom_call_target="tpu_custom_call" | custom-call | flops 9774999552 | bytes 1048576 | tf_op jit(solution)/shard_map/entry/pallas_call | solution.py:195
  11.4 2.6 %collective-permute-start.3 = (bf16[2,2,256,256]{3,2,1,0:T(8,128)(2,1)S(1)}, bf16[2,2,256,256]{3,2,1,0:T(8,128)(2,1)S(1)}, u32[]{:S(2)}, u32[]{:S(2)}) collective-permute-start(bf16[2,2,256,256]{3,2,1,0:T(8,128)(2,1)S(1)} %get-tuple-element.143), channel_id=1, source_target_pairs={{0,5},{1,2},{2,7},{3,0},{4,1},{5,6},{6,3},{7,4},{8,13},{9,10},{10,... | collective-permute-start | bytes 1572872 | tf_op jit(solution)/shard_map/ppermute | solution.py:766
  15.6 10.1 %attention.1 = (bf16[2,256,512]{2,1,0:T(8,128)(2,1)}, f32[2,256,512]{2,1,0:T(8,128)S(1)}, bf16[2,256,256]{2,1,0:T(8,128)(2,1)S(1)}, bf16[2,256,256]{2,1,0:T(8,12...) custom-call(s32[9]{0:T(128)S(1)} %stack.78.place_ref, ...), custom_call_target="tpu_custom_call" | custom-call | flops 15525000192 | bytes 1048576 | tf_op jit(solution)/shard_map/attention/pallas_call | solution.py:308
  35.6 2.0 %conv2_grad_other.1 = bf16[4,288,256]{2,1,0:T(8,128)(2,1)S(1)} custom-call(s32[9]{0:T(128)S(1)} %stack.78.place_ref, bf16[768,2048]{1,0:T(8,128)(2,1)S(1)} %turn.2.s_ref, bf16[2,256,256]{2,1,0:T(8,128)(2,1)S(1)} %get-tuple-element.148.refs_0_, bf16[2,256,256]{2,1,0:T(8,128)(2,1)S(1)} %collective-permute-done.6.refs_1_, ...), custom_call_target="tpu_custom_call" | custom-call | flops 1840000000 | bytes 1048576 | tf_op jit(solution)/shard_map/conv2_grad_other/pallas_call | solution.py:524
  39.3 2.0 %conv2_grad.1 = bf16[4,288,256]{2,1,0:T(8,128)(2,1)S(1)} custom-call(s32[9]{0:T(128)S(1)} %stack.78.place_ref, bf16[768,2048]{1,0:T(8,128)(2,1)S(1)} %turn.2.s_ref, bf16[2,256,256]{2,1,0:T(8,128)(2,1)S(1)} %get-tuple-element.148.refs_0_, bf16[2,256,256]{2,1,0:T(8,128)(2,1)S(1)} %collective-permute-done.6.refs_1_, ...), custom_call_target="tpu_custom_call" | custom-call | flops 1840000000 | bytes 1048576 | tf_op jit(solution)/shard_map/conv2_grad/pallas_call | solution.py:524
  44.1 4.3 %conv2_back.1 = (bf16[2,256,256]{2,1,0:T(8,128)(2,1)S(1)}, bf16[2,256,256]{2,1,0:T(8,128)(2,1)S(1)}, bf16[2,256,512]{2,1,0:T(8,128)(2,1)S(1)}, f32[8,512]{1,0:T(8,128)S(1)}) custom-call(s32[9]{0:T(128)S(1)} %stack.78.place_ref, f32[2,256,512]{2,1,0:T(8,128)S(1)} %get-tuple-element.156.dres_ref, f32[2,256,512]{2,1,0:T(8,128)S(1)} %get-tuple-element.157.norm2_ref, ...), custom_call_target="tpu_custom_call" | custom-call | flops 5750000128 | bytes 1048576 | tf_op jit(solution)/shard_map/conv2_back/pallas_call | solution.py:370
  51.4 2.1 %collective-permute-start.11 = (bf16[424,256]{1,0:T(8,128)(2,1)S(1)}, bf16[424,256]{1,0:T(8,128)(2,1)S(1)}, u32[]{:S(2)}, u32[]{:S(2)}) collective-permute-start(bf16[424,256]{1,0:T(8,128)(2,1)S(1)} %get-tuple-element.226), channel_id=1, source_target_pairs={{0,8},{1,9},{2,10},{3,11},{4,12},{5,13},{6,14},{7,15},{8,0},{9,1},... | collective-permute-start | bytes 651272 | tf_op jit(solution)/shard_map/ppermute | solution.py:758
  53.5 2.5 %collective-permute-start.13 = (bf16[424,256]{1,0:T(8,128)(2,1)S(1)}, bf16[424,256]{1,0:T(8,128)(2,1)S(1)}, u32[]{:S(2)}, u32[]{:S(2)}) collective-permute-start(bf16[424,256]{1,0:T(8,128)(2,1)S(1)} %get-tuple-element.227), channel_id=1, source_target_pairs={{0,24},{1,25},{2,26},{3,27},{4,28},{5,29},{6,30},{7,31},{8,16},{9,... | collective-permute-start | bytes 651272 | tf_op jit(solution)/shard_map/ppermute | solution.py:758
  57.1 2.6 %collective-permute-start.12 = (bf16[424,256]{1,0:T(8,128)(2,1)S(1)}, bf16[424,256]{1,0:T(8,128)(2,1)S(1)}, u32[]{:S(2)}, u32[]{:S(2)}) collective-permute-start(bf16[424,256]{1,0:T(8,128)(2,1)S(1)} %get-tuple-element.228), channel_id=1, source_target_pairs={{0,16},{1,17},{2,18},{3,19},{4,20},{5,21},{6,22},{7,23},{8,24},{9,... | collective-permute-start | bytes 651272 | tf_op jit(solution)/shard_map/ppermute | solution.py:758
  59.7 7.2 %conv1_back.1 = (bf16[4,128,512]{2,1,0:T(8,128)(2,1)}, bf16[2,128,512]{2,1,0:T(8,128)(2,1)S(1)}, f32[8,512]{1,0:T(8,128)S(1)}) custom-call(s32[9]{0:T(128)S(1)} %stack.78.place_ref, bf16[2,256,512]{2,1,0:T(8,128)(2,1)S(1)} %get-tuple-element.170.dfull_ref, bf16[2,256,512]{2,1,0:T(8,128)(2,1)S(1)} %get-tuple-element.125.x_ref, ...), custom_call_target="tpu_custom_call" | custom-call | flops 115000000 | bytes 1048576 | tf_op jit(solution)/shard_map/conv1_back/pallas_call | solution.py:421
  68.3 2.0 %conv1_grad_other.1 = bf16[4,288,256]{2,1,0:T(8,128)(2,1)S(1)} custom-call(s32[9]{0:T(128)S(1)} %stack.78.place_ref, bf16[768,2048]{1,0:T(8,128)(2,1)S(1)} %turn.3.s_ref, bf16[2,256,256]{2,1,0:T(8,128)(2,1)S(1)} %get-tuple-element.168.refs_0_, bf16[2,256,256]{2,1,0:T(8,128)(2,1)S(1)} %collective-permute-done.14.refs_1_, ...), custom_call_target="tpu_custom_call" | custom-call | flops 115000000 | bytes 1048576 | tf_op jit(solution)/shard_map/conv1_grad_other/pallas_call | solution.py:524
  70.2 2.0 %conv1_grad.1 = bf16[4,288,256]{2,1,0:T(8,128)(2,1)S(1)} custom-call(s32[9]{0:T(128)S(1)} %stack.78.place_ref, bf16[768,2048]{1,0:T(8,128)(2,1)S(1)} %turn.3.s_ref, bf16[2,256,256]{2,1,0:T(8,128)(2,1)S(1)} %get-tuple-element.168.refs_0_, bf16[2,256,256]{2,1,0:T(8,128)(2,1)S(1)} %collective-permute-done.14.refs_1_, ...), custom_call_target="tpu_custom_call" | custom-call | flops 115000000 | bytes 1048576 | tf_op jit(solution)/shard_map/conv1_grad/pallas_call | solution.py:524
  72.2 2.6 %collective-permute-done.12 = bf16[424,256]{1,0:T(8,128)(2,1)S(1)} collective-permute-done((bf16[424,256]{1,0:T(8,128)(2,1)S(1)}, bf16[424,256]{1,0:T(8,128)(2,1)S(1)}, u32[]{:S(2)}, u32[]{:S(2)}) %collective-permute-start.12) | collective-permute-done | bytes 217120 | tf_op jit(solution)/shard_map/ppermute | solution.py:758
  76.5 2.6 %collective-permute-start.19 = (bf16[424,256]{1,0:T(8,128)(2,1)S(1)}, bf16[424,256]{1,0:T(8,128)(2,1)S(1)}, u32[]{:S(2)}, u32[]{:S(2)}) collective-permute-start(bf16[424,256]{1,0:T(8,128)(2,1)S(1)} %fusion.2), channel_id=1, source_target_pairs={{0,24},{1,25},{2,26},{3,27},{4,28},{5,29},{6,30},{7,31},{8,16},{9,... | collective-permute-start | bytes 651272 | tf_op jit(solution)/shard_map/ppermute | solution.py:758
  80.9 4.0 %collective-permute-done.20 = bf16[4,288,256]{2,1,0:T(8,128)(2,1)S(1)} collective-permute-done((bf16[4,288,256]{2,1,0:T(8,128)(2,1)S(1)}, bf16[4,288,256]{2,1,0:T(8,128)(2,1)S(1)}, u32[]{:S(2)}, u32[]{:S(2)}) %collective-permute-start.20) | collective-permute-done | bytes 589856 | tf_op jit(solution)/shard_map/ppermute | solution.py:758
  86.8 9.1 %collective-permute-done.18 = bf16[424,256]{1,0:T(8,128)(2,1)S(1)} collective-permute-done((bf16[424,256]{1,0:T(8,128)(2,1)S(1)}, bf16[424,256]{1,0:T(8,128)(2,1)S(1)}, u32[]{:S(2)}, u32[]{:S(2)}) %collective-permute-start.18) | collective-permute-done | bytes 217120 | tf_op jit(solution)/shard_map/ppermute | solution.py:758
  98.9 2.1 %collective-permute-start.25 = (bf16[288,256]{1,0:T(8,128)(2,1)S(1)}, bf16[288,256]{1,0:T(8,128)(2,1)S(1)}, u32[]{:S(2)}, u32[]{:S(2)}) collective-permute-start(bf16[288,256]{1,0:T(8,128)(2,1)S(1)} %get-tuple-element.231), channel_id=1, source_target_pairs={{0,16},{1,17},{2,18},{3,19},{4,20},{5,21},{6,22},{7,23},{8,24},{9,... | collective-permute-start | bytes 442376 | tf_op jit(solution)/shard_map/ppermute | solution.py:758
  102.4 3.0 %collective-permute-done.27 = f32[13,512]{1,0:T(8,128)S(1)} collective-permute-done((f32[13,512]{1,0:T(8,128)S(1)}, f32[13,512]{1,0:T(8,128)S(1)}, u32[]{:S(2)}, u32[]{:S(2)}) %collective-permute-start.27) | collective-permute-done | bytes 26656 | tf_op jit(solution)/shard_map/ppermute | solution.py:758
  105.9 5.6 %collective-permute-done.25 = bf16[288,256]{1,0:T(8,128)(2,1)S(1)} collective-permute-done((bf16[288,256]{1,0:T(8,128)(2,1)S(1)}, bf16[288,256]{1,0:T(8,128)(2,1)S(1)}, u32[]{:S(2)}, u32[]{:S(2)}) %collective-permute-start.25) | collective-permute-done | bytes 147488 | tf_op jit(solution)/shard_map/ppermute | solution.py:758
  117.4 1.9 %collective-permute-start.28 = (bf16[288,256]{1,0:T(8,128)(2,1)S(1)}, bf16[288,256]{1,0:T(8,128)(2,1)S(1)}, u32[]{:S(2)}, u32[]{:S(2)}) collective-permute-start(bf16[288,256]{1,0:T(8,128)(2,1)S(1)} %fusion.5), channel_id=1, source_target_pairs={{0,8},{1,9},{2,10},{3,11},{4,12},{5,13},{6,14},{7,15},{8,0},{9,1},... | collective-permute-start | bytes 442376 | tf_op jit(solution)/shard_map/ppermute | solution.py:758
  119.3 1.8 %place_rows.1 = (bf16[4,128,512]{2,1,0:T(8,128)(2,1)}, f32[8,128]{1,0:T(8,128)}) custom-call(s32[9]{0:T(128)S(1)} %stack.78.place_ref, bf16[2,128,512]{2,1,0:T(8,128)(2,1)S(1)} %collective-permute-done.21.got_ref, bf16[4,128,512]{2,1,0:T(8,128)(2,1)} %get-tuple-element.190.into_hbm), custom_call_target="tpu_custom_call", output_to_operand_aliasing={{0}: (2, {})} | custom-call | flops 1150000000 | bytes 1048576 | tf_op jit(solution)/shard_map/place_rows/pallas_call | solution.py:447
  121.2 2.4 %collective-permute-done.30 = bf16[288,256]{1,0:T(8,128)(2,1)S(1)} collective-permute-done((bf16[288,256]{1,0:T(8,128)(2,1)S(1)}, bf16[288,256]{1,0:T(8,128)(2,1)S(1)}, u32[]{:S(2)}, u32[]{:S(2)}) %collective-permute-start.30) | collective-permute-done | bytes 147488 | tf_op jit(solution)/shard_map/ppermute | solution.py:758
  123.5 5.1 %collective-permute-done.29 = bf16[288,256]{1,0:T(8,128)(2,1)S(1)} collective-permute-done((bf16[288,256]{1,0:T(8,128)(2,1)S(1)}, bf16[288,256]{1,0:T(8,128)(2,1)S(1)}, u32[]{:S(2)}, u32[]{:S(2)}) %collective-permute-start.29) | collective-permute-done | bytes 147488 | tf_op jit(solution)/shard_map/ppermute | solution.py:758
  129.4 3.6 %collective-permute-done.35 = f32[13,512]{1,0:T(8,128)S(1)} collective-permute-done((f32[13,512]{1,0:T(8,128)S(1)}, f32[13,512]{1,0:T(8,128)S(1)}, u32[]{:S(2)}, u32[]{:S(2)}) %collective-permute-start.35) | collective-permute-done | bytes 26656 | tf_op jit(solution)/shard_map/ppermute | solution.py:758
  133.7 2.7 %conv2_finish.2.refs_2_ = f32[9,512,512]{2,1,0:T(8,128)} custom-call(s32[9]{0:T(128)S(1)} %stack.78.place_ref, bf16[8,424,256]{2,1,0:T(8,128)(2,1)S(1)} %bitcast.67, bf16[8,424,256]{2,1,0:T(8,128)(2,1)S(1)} %collective-permute-done.32.refs_1_.other0), custom_call_target="tpu_custom_call" | custom-call | flops 3449999872 | bytes 1048576 | tf_op jit(solution)/shard_map/conv2_finish/pallas_call | solution.py:687
  138.6 2.1 %collective-permute-done.33.refs_2_ = bf16[4,288,256]{2,1,0:T(8,128)(2,1)S(1)} collective-permute-done((bf16[4,288,256]{2,1,0:T(8,128)(2,1)S(1)}, bf16[4,288,256]{2,1,0:T(8,128)(2,1)S(1)}, u32[]{:S(2)}, u32[]{:S(2)}) %collective-permute-start.33) | collective-permute-done | bytes 589856 | tf_op jit(solution)/shard_map/ppermute | solution.py:758
  146.0 2.7 %conv1_finish.2.refs_4_ = f32[9,512,512]{2,1,0:T(8,128)} custom-call(s32[9]{0:T(128)S(1)} %stack.78.place_ref, bf16[4,288,256]{2,1,0:T(8,128)(2,1)S(1)} %pad_maximum_fusion.2.refs_0_, bf16[4,288,256]{2,1,0:T(8,128)(2,1)S(1)} %collective-permute-done.40.refs_1_, bf16[4,288,256]{2,1,0:T(8,128)(2,1)S(1)} %collective-permute-done.33.refs_2_, ...), custom_call_target="tpu_custom_call" | custom-call | flops 3449999872 | bytes 1048576 | tf_op jit(solution)/shard_map/conv1_finish/pallas_call | solution.py:687
  148.8 2.7 %conv2_finish.3 = f32[9,512,512]{2,1,0:T(8,128)} custom-call(s32[9]{0:T(128)S(1)} %stack.78.place_ref, bf16[8,424,256]{2,1,0:T(8,128)(2,1)S(1)} %collective-permute-done.34.refs_0_.mine1, bf16[8,424,256]{2,1,0:T(8,128)(2,1)S(1)} %collective-permute-done.39.refs_1_.other1, f32[9,512,512]{2,1,0:T(8,128)} %conv2_finish.2.refs_2_), custom_call_target="tpu_custom_call", output_to_operand_aliasing={{}: (3, {})} | custom-call | flops 3449999872 | bytes 1048576 | tf_op jit(solution)/shard_map/conv2_finish/pallas_call | solution.py:687
  151.5 3.7 %attention_finish.1 = (f32[512,512]{1,0:T(8,128)}, f32[512,512]{1,0:T(8,128)}, f32[512,512]{1,0:T(8,128)}, f32[512,512]{1,0:T(8,128)}, f32[32,256]{1,0:T(8,128)}) custom-call(s32[9]{0:T(128)S(1)} %stack.78.place_ref, bf16[8,424,256]{2,1,0:T(8,128)(2,1)S(1)} %bitcast.68, bf16[8,424,256]{2,1,0:T(8,128)(2,1)S(1)} %collective-permute-done.32.refs_1_.other0, ...), custom_call_target="tpu_custom_call" | custom-call | flops 3449999872 | bytes 1048576 | tf_op jit(solution)/shard_map/attention_finish/pallas_call | solution.py:660
  155.2 2.3 %collective-permute-done.38.refs_2_ = bf16[4,288,256]{2,1,0:T(8,128)(2,1)S(1)} collective-permute-done((bf16[4,288,256]{2,1,0:T(8,128)(2,1)S(1)}, bf16[4,288,256]{2,1,0:T(8,128)(2,1)S(1)}, u32[]{:S(2)}, u32[]{:S(2)}) %collective-permute-start.38) | collective-permute-done | bytes 589856 | tf_op jit(solution)/shard_map/ppermute | solution.py:758
  160.3 2.7 %conv1_finish.3 = f32[9,512,512]{2,1,0:T(8,128)} custom-call(s32[9]{0:T(128)S(1)} %stack.78.place_ref, bf16[4,288,256]{2,1,0:T(8,128)(2,1)S(1)} %collective-permute-done.37.refs_0_, bf16[4,288,256]{2,1,0:T(8,128)(2,1)S(1)} %collective-permute-done.42.refs_1_, ...), custom_call_target="tpu_custom_call", output_to_operand_aliasing={{}: (5, {})} | custom-call | flops 3449999872 | bytes 1048576 | tf_op jit(solution)/shard_map/conv1_finish/pallas_call | solution.py:687
  (104 shorter events, 50.0 us)
Async XLA Ops:
  11.3 14.3 %collective-permute-start.1 = (bf16[2,2,256,256]{3,2,1,0:T(8,128)(2,1)S(1)}, bf16[2,2,256,256]{3,2,1,0:T(8,128)(2,1)S(1)}, u32[]{:S(2)}, u32[]{:S(2)}) collective-permute-start(bf16[2,2,256,256]{3,2,1,0:T(8,128)(2,1)S(1)} %get-tuple-element.142), channel_id=1, source_target_pairs={{0,1},{1,0},{2,3},{3,2},{4,5},{5,4},{6,7},{7,6},{8,9},{9,8},{10,11... | collective-permute-start | bytes 1572872 | tf_op jit(solution)/shard_map/ppermute | solution.py:762
  11.4 14.2 %collective-permute-start.3 = (bf16[2,2,256,256]{3,2,1,0:T(8,128)(2,1)S(1)}, bf16[2,2,256,256]{3,2,1,0:T(8,128)(2,1)S(1)}, u32[]{:S(2)}, u32[]{:S(2)}) collective-permute-start(bf16[2,2,256,256]{3,2,1,0:T(8,128)(2,1)S(1)} %get-tuple-element.143), channel_id=1, source_target_pairs={{0,5},{1,2},{2,7},{3,0},{4,1},{5,6},{6,3},{7,4},{8,13},{9,10},{10,... | collective-permute-start | bytes 1572872 | tf_op jit(solution)/shard_map/ppermute | solution.py:766
  14.1 12.5 %collective-permute-start.2 = (bf16[2,2,256,256]{3,2,1,0:T(8,128)(2,1)S(1)}, bf16[2,2,256,256]{3,2,1,0:T(8,128)(2,1)S(1)}, u32[]{:S(2)}, u32[]{:S(2)}) collective-permute-start(bf16[2,2,256,256]{3,2,1,0:T(8,128)(2,1)S(1)} %get-tuple-element.127.near_ref), channel_id=1, source_target_pairs={{0,2},{1,5},{2,0},{3,7},{4,6},{5,1},{6,4},{7,3},{8,10},{9,13},{10,... | collective-permute-start | bytes 1572872 | tf_op jit(solution)/shard_map/ppermute | solution.py:758
  27.0 7.8 %collective-permute-start.8 = (bf16[2,256,256]{2,1,0:T(8,128)(2,1)S(1)}, bf16[2,256,256]{2,1,0:T(8,128)(2,1)S(1)}, u32[]{:S(2)}, u32[]{:S(2)}) collective-permute-start(bf16[2,256,256]{2,1,0:T(8,128)(2,1)S(1)} %get-tuple-element.149), channel_id=1, source_target_pairs={{0,5},{1,2},{2,7},{3,0},{4,1},{5,6},{6,3},{7,4},{8,13},{9,10},{10,... | collective-permute-start | bytes 786440 | tf_op jit(solution)/shard_map/ppermute | solution.py:766
  28.8 6.8 %collective-permute-start.7 = (bf16[2,256,256]{2,1,0:T(8,128)(2,1)S(1)}, bf16[2,256,256]{2,1,0:T(8,128)(2,1)S(1)}, u32[]{:S(2)}, u32[]{:S(2)}) collective-permute-start(bf16[2,256,256]{2,1,0:T(8,128)(2,1)S(1)} %get-tuple-element.148.refs_0_), channel_id=1, source_target_pairs={{0,2},{1,5},{2,0},{3,7},{4,6},{5,1},{6,4},{7,3},{8,10},{9,13},{10,... | collective-permute-start | bytes 786440 | tf_op jit(solution)/shard_map/ppermute | solution.py:758
  30.6 11.5 %collective-permute-start.5 = (bf16[8,136,256]{2,1,0:T(8,128)(2,1)S(1)}, bf16[8,136,256]{2,1,0:T(8,128)(2,1)S(1)}, u32[]{:S(2)}, u32[]{:S(2)}) collective-permute-start(bf16[8,136,256]{2,1,0:T(8,128)(2,1)S(1)} %slice.73), channel_id=1, source_target_pairs={{0,2},{1,5},{2,0},{3,7},{4,6},{5,1},{6,4},{7,3},{8,10},{9,13},{10,... | collective-permute-start | bytes 1671176 | tf_op jit(solution)/shard_map/ppermute | solution.py:758
  37.5 13.3 %collective-permute-start.10 = (bf16[4,288,256]{2,1,0:T(8,128)(2,1)S(1)}, bf16[4,288,256]{2,1,0:T(8,128)(2,1)S(1)}, u32[]{:S(2)}, u32[]{:S(2)}) collective-permute-start(bf16[4,288,256]{2,1,0:T(8,128)(2,1)S(1)} %conv2_grad_other.1), channel_id=1, source_target_pairs={{0,4},{1,3},{2,6},{3,1},{4,0},{5,7},{6,2},{7,5},{8,12},{9,11},{10,... | collective-permute-start | bytes 1769480 | tf_op jit(solution)/shard_map/ppermute | solution.py:758
  42.4 8.8 %collective-permute-start.9 = (bf16[4,136,256]{2,1,0:T(8,128)(2,1)S(1)}, bf16[4,136,256]{2,1,0:T(8,128)(2,1)S(1)}, u32[]{:S(2)}, u32[]{:S(2)}) collective-permute-start(bf16[4,136,256]{2,1,0:T(8,128)(2,1)S(1)} %slice.75), channel_id=1, source_target_pairs={{0,4},{1,3},{2,6},{3,1},{4,0},{5,7},{6,2},{7,5},{8,12},{9,11},{10,... | collective-permute-start | bytes 835592 | tf_op jit(solution)/shard_map/ppermute | solution.py:758
  48.4 19.8 %collective-permute-start.16 = (bf16[2,256,256]{2,1,0:T(8,128)(2,1)S(1)}, bf16[2,256,256]{2,1,0:T(8,128)(2,1)S(1)}, u32[]{:S(2)}, u32[]{:S(2)}) collective-permute-start(bf16[2,256,256]{2,1,0:T(8,128)(2,1)S(1)} %get-tuple-element.169), channel_id=1, source_target_pairs={{0,5},{1,2},{2,7},{3,0},{4,1},{5,6},{6,3},{7,4},{8,13},{9,10},{10,... | collective-permute-start | bytes 786440 | tf_op jit(solution)/shard_map/ppermute | solution.py:766
  50.3 18.0 %collective-permute-start.14 = (bf16[2,256,256]{2,1,0:T(8,128)(2,1)S(1)}, bf16[2,256,256]{2,1,0:T(8,128)(2,1)S(1)}, u32[]{:S(2)}, u32[]{:S(2)}) collective-permute-start(bf16[2,256,256]{2,1,0:T(8,128)(2,1)S(1)} %get-tuple-element.169), channel_id=1, source_target_pairs={{0,1},{1,0},{2,3},{3,2},{4,5},{5,4},{6,7},{7,6},{8,9},{9,8},{10,11... | collective-permute-start | bytes 786440 | tf_op jit(solution)/shard_map/ppermute | solution.py:762
  50.3 6.8 %collective-permute-start.15 = (bf16[2,256,256]{2,1,0:T(8,128)(2,1)S(1)}, bf16[2,256,256]{2,1,0:T(8,128)(2,1)S(1)}, u32[]{:S(2)}, u32[]{:S(2)}) collective-permute-start(bf16[2,256,256]{2,1,0:T(8,128)(2,1)S(1)} %get-tuple-element.168.refs_0_), channel_id=1, source_target_pairs={{0,2},{1,5},{2,0},{3,7},{4,6},{5,1},{6,4},{7,3},{8,10},{9,13},{10,... | collective-permute-start | bytes 786440 | tf_op jit(solution)/shard_map/ppermute | solution.py:758
  51.4 20.8 %collective-permute-start.11 = (bf16[424,256]{1,0:T(8,128)(2,1)S(1)}, bf16[424,256]{1,0:T(8,128)(2,1)S(1)}, u32[]{:S(2)}, u32[]{:S(2)}) collective-permute-start(bf16[424,256]{1,0:T(8,128)(2,1)S(1)} %get-tuple-element.226), channel_id=1, source_target_pairs={{0,8},{1,9},{2,10},{3,11},{4,12},{5,13},{6,14},{7,15},{8,0},{9,1},... | collective-permute-start | bytes 651272 | tf_op jit(solution)/shard_map/ppermute | solution.py:758
  53.5 18.7 %collective-permute-start.13 = (bf16[424,256]{1,0:T(8,128)(2,1)S(1)}, bf16[424,256]{1,0:T(8,128)(2,1)S(1)}, u32[]{:S(2)}, u32[]{:S(2)}) collective-permute-start(bf16[424,256]{1,0:T(8,128)(2,1)S(1)} %get-tuple-element.227), channel_id=1, source_target_pairs={{0,24},{1,25},{2,26},{3,27},{4,28},{5,29},{6,30},{7,31},{8,16},{9,... | collective-permute-start | bytes 651272 | tf_op jit(solution)/shard_map/ppermute | solution.py:758
  57.1 17.7 %collective-permute-start.12 = (bf16[424,256]{1,0:T(8,128)(2,1)S(1)}, bf16[424,256]{1,0:T(8,128)(2,1)S(1)}, u32[]{:S(2)}, u32[]{:S(2)}) collective-permute-start(bf16[424,256]{1,0:T(8,128)(2,1)S(1)} %get-tuple-element.228), channel_id=1, source_target_pairs={{0,16},{1,17},{2,18},{3,19},{4,20},{5,21},{6,22},{7,23},{8,24},{9,... | collective-permute-start | bytes 651272 | tf_op jit(solution)/shard_map/ppermute | solution.py:758
  74.9 9.9 %collective-permute-start.20 = (bf16[4,288,256]{2,1,0:T(8,128)(2,1)S(1)}, bf16[4,288,256]{2,1,0:T(8,128)(2,1)S(1)}, u32[]{:S(2)}, u32[]{:S(2)}) collective-permute-start(bf16[4,288,256]{2,1,0:T(8,128)(2,1)S(1)} %conv1_grad_other.1), channel_id=1, source_target_pairs={{0,4},{1,3},{2,6},{3,1},{4,0},{5,7},{6,2},{7,5},{8,12},{9,11},{10,... | collective-permute-start | bytes 1769480 | tf_op jit(solution)/shard_map/ppermute | solution.py:758
  76.5 10.2 %collective-permute-start.19 = (bf16[424,256]{1,0:T(8,128)(2,1)S(1)}, bf16[424,256]{1,0:T(8,128)(2,1)S(1)}, u32[]{:S(2)}, u32[]{:S(2)}) collective-permute-start(bf16[424,256]{1,0:T(8,128)(2,1)S(1)} %fusion.2), channel_id=1, source_target_pairs={{0,24},{1,25},{2,26},{3,27},{4,28},{5,29},{6,30},{7,31},{8,16},{9,... | collective-permute-start | bytes 651272 | tf_op jit(solution)/shard_map/ppermute | solution.py:758
  79.2 16.7 %collective-permute-start.18 = (bf16[424,256]{1,0:T(8,128)(2,1)S(1)}, bf16[424,256]{1,0:T(8,128)(2,1)S(1)}, u32[]{:S(2)}, u32[]{:S(2)}) collective-permute-start(bf16[424,256]{1,0:T(8,128)(2,1)S(1)} %fusion.2), channel_id=1, source_target_pairs={{0,16},{1,17},{2,18},{3,19},{4,20},{5,21},{6,22},{7,23},{8,24},{9,... | collective-permute-start | bytes 651272 | tf_op jit(solution)/shard_map/ppermute | solution.py:758
  79.2 16.7 %collective-permute-start.17 = (bf16[424,256]{1,0:T(8,128)(2,1)S(1)}, bf16[424,256]{1,0:T(8,128)(2,1)S(1)}, u32[]{:S(2)}, u32[]{:S(2)}) collective-permute-start(bf16[424,256]{1,0:T(8,128)(2,1)S(1)} %fusion.2), channel_id=1, source_target_pairs={{0,8},{1,9},{2,10},{3,11},{4,12},{5,13},{6,14},{7,15},{8,0},{9,1},... | collective-permute-start | bytes 651272 | tf_op jit(solution)/shard_map/ppermute | solution.py:758
  85.0 10.9 %collective-permute-start.21 = (bf16[2,128,512]{2,1,0:T(8,128)(2,1)S(1)}, bf16[2,128,512]{2,1,0:T(8,128)(2,1)S(1)}, u32[]{:S(2)}, u32[]{:S(2)}) collective-permute-start(bf16[2,128,512]{2,1,0:T(8,128)(2,1)S(1)} %get-tuple-element.178), channel_id=1, source_target_pairs={{0,1},{1,0},{2,3},{3,2},{4,5},{5,4},{6,7},{7,6},{8,9},{9,8},{10,11... | collective-permute-start | bytes 786440 | tf_op jit(solution)/shard_map/ppermute | solution.py:762
  96.0 15.6 %collective-permute-start.23 = (bf16[4,424,256]{2,1,0:T(8,128)(2,1)S(1)}, bf16[4,424,256]{2,1,0:T(8,128)(2,1)S(1)}, u32[]{:S(2)}, u32[]{:S(2)}) collective-permute-start(bf16[4,424,256]{2,1,0:T(8,128)(2,1)S(1)} %pad_maximum_fusion.1), channel_id=1, source_target_pairs={{0,4},{1,3},{2,6},{3,1},{4,0},{5,7},{6,2},{7,5},{8,12},{9,11},{10,... | collective-permute-start | bytes 2605064 | tf_op jit(solution)/shard_map/ppermute | solution.py:758
  97.4 7.9 %collective-permute-start.24 = (bf16[288,256]{1,0:T(8,128)(2,1)S(1)}, bf16[288,256]{1,0:T(8,128)(2,1)S(1)}, u32[]{:S(2)}, u32[]{:S(2)}) collective-permute-start(bf16[288,256]{1,0:T(8,128)(2,1)S(1)} %get-tuple-element.229), channel_id=1, source_target_pairs={{0,8},{1,9},{2,10},{3,11},{4,12},{5,13},{6,14},{7,15},{8,0},{9,1},... | collective-permute-start | bytes 442376 | tf_op jit(solution)/shard_map/ppermute | solution.py:758
  97.5 8.4 %collective-permute-start.26 = (bf16[288,256]{1,0:T(8,128)(2,1)S(1)}, bf16[288,256]{1,0:T(8,128)(2,1)S(1)}, u32[]{:S(2)}, u32[]{:S(2)}) collective-permute-start(bf16[288,256]{1,0:T(8,128)(2,1)S(1)} %get-tuple-element.230), channel_id=1, source_target_pairs={{0,24},{1,25},{2,26},{3,27},{4,28},{5,29},{6,30},{7,31},{8,16},{9,... | collective-permute-start | bytes 442376 | tf_op jit(solution)/shard_map/ppermute | solution.py:758
  98.9 12.6 %collective-permute-start.25 = (bf16[288,256]{1,0:T(8,128)(2,1)S(1)}, bf16[288,256]{1,0:T(8,128)(2,1)S(1)}, u32[]{:S(2)}, u32[]{:S(2)}) collective-permute-start(bf16[288,256]{1,0:T(8,128)(2,1)S(1)} %get-tuple-element.231), channel_id=1, source_target_pairs={{0,16},{1,17},{2,18},{3,19},{4,20},{5,21},{6,22},{7,23},{8,24},{9,... | collective-permute-start | bytes 442376 | tf_op jit(solution)/shard_map/ppermute | solution.py:758
  111.8 17.0 %collective-permute-start.32 = (bf16[8,424,256]{2,1,0:T(8,128)(2,1)S(1)}, bf16[8,424,256]{2,1,0:T(8,128)(2,1)S(1)}, u32[]{:S(2)}, u32[]{:S(2)}) collective-permute-start(bf16[8,424,256]{2,1,0:T(8,128)(2,1)S(1)} %bitcast.65), channel_id=1, source_target_pairs={{0,1},{1,0},{2,3},{3,2},{4,5},{5,4},{6,7},{7,6},{8,9},{9,8},{10,11... | collective-permute-start | bytes 5210120 | tf_op jit(solution)/shard_map/ppermute | solution.py:762
  111.8 26.7 %collective-permute-start.34 = (bf16[8,424,256]{2,1,0:T(8,128)(2,1)S(1)}, bf16[8,424,256]{2,1,0:T(8,128)(2,1)S(1)}, u32[]{:S(2)}, u32[]{:S(2)}) collective-permute-start(bf16[8,424,256]{2,1,0:T(8,128)(2,1)S(1)} %bitcast.66), channel_id=1, source_target_pairs={{0,2},{1,5},{2,0},{3,7},{4,6},{5,1},{6,4},{7,3},{8,10},{9,13},{10,... | collective-permute-start | bytes 5210120 | tf_op jit(solution)/shard_map/ppermute | solution.py:758
  114.9 8.6 %collective-permute-start.30 = (bf16[288,256]{1,0:T(8,128)(2,1)S(1)}, bf16[288,256]{1,0:T(8,128)(2,1)S(1)}, u32[]{:S(2)}, u32[]{:S(2)}) collective-permute-start(bf16[288,256]{1,0:T(8,128)(2,1)S(1)} %fusion.5), channel_id=1, source_target_pairs={{0,24},{1,25},{2,26},{3,27},{4,28},{5,29},{6,30},{7,31},{8,16},{9,... | collective-permute-start | bytes 442376 | tf_op jit(solution)/shard_map/ppermute | solution.py:758
  116.7 11.9 %collective-permute-start.29 = (bf16[288,256]{1,0:T(8,128)(2,1)S(1)}, bf16[288,256]{1,0:T(8,128)(2,1)S(1)}, u32[]{:S(2)}, u32[]{:S(2)}) collective-permute-start(bf16[288,256]{1,0:T(8,128)(2,1)S(1)} %fusion.5), channel_id=1, source_target_pairs={{0,16},{1,17},{2,18},{3,19},{4,20},{5,21},{6,22},{7,23},{8,24},{9,... | collective-permute-start | bytes 442376 | tf_op jit(solution)/shard_map/ppermute | solution.py:758
  117.4 11.2 %collective-permute-start.28 = (bf16[288,256]{1,0:T(8,128)(2,1)S(1)}, bf16[288,256]{1,0:T(8,128)(2,1)S(1)}, u32[]{:S(2)}, u32[]{:S(2)}) collective-permute-start(bf16[288,256]{1,0:T(8,128)(2,1)S(1)} %fusion.5), channel_id=1, source_target_pairs={{0,8},{1,9},{2,10},{3,11},{4,12},{5,13},{6,14},{7,15},{8,0},{9,1},... | collective-permute-start | bytes 442376 | tf_op jit(solution)/shard_map/ppermute | solution.py:758
  128.7 11.9 %collective-permute-start.33 = (bf16[4,288,256]{2,1,0:T(8,128)(2,1)S(1)}, bf16[4,288,256]{2,1,0:T(8,128)(2,1)S(1)}, u32[]{:S(2)}, u32[]{:S(2)}) collective-permute-start(bf16[4,288,256]{2,1,0:T(8,128)(2,1)S(1)} %pad_maximum_fusion.2.refs_0_), channel_id=1, source_target_pairs={{0,4},{1,3},{2,6},{3,1},{4,0},{5,7},{6,2},{7,5},{8,12},{9,11},{10,... | collective-permute-start | bytes 1769480 | tf_op jit(solution)/shard_map/ppermute | solution.py:758
  140.7 8.1 %collective-permute-start.39 = (bf16[8,424,256]{2,1,0:T(8,128)(2,1)S(1)}, bf16[8,424,256]{2,1,0:T(8,128)(2,1)S(1)}, u32[]{:S(2)}, u32[]{:S(2)}) collective-permute-start(bf16[8,424,256]{2,1,0:T(8,128)(2,1)S(1)} %collective-permute-done.34.refs_0_.mine1), channel_id=1, source_target_pairs={{0,1},{1,0},{2,3},{3,2},{4,5},{5,4},{6,7},{7,6},{8,9},{9,8},{10,11... | collective-permute-start | bytes 5210120 | tf_op jit(solution)/shard_map/ppermute | solution.py:762
  141.3 13.9 %collective-permute-start.37 = (bf16[4,288,256]{2,1,0:T(8,128)(2,1)S(1)}, bf16[4,288,256]{2,1,0:T(8,128)(2,1)S(1)}, u32[]{:S(2)}, u32[]{:S(2)}) collective-permute-start(bf16[4,288,256]{2,1,0:T(8,128)(2,1)S(1)} %pad_maximum_fusion.2.refs_0_), channel_id=1, source_target_pairs={{0,2},{1,5},{2,0},{3,7},{4,6},{5,1},{6,4},{7,3},{8,10},{9,13},{10,... | collective-permute-start | bytes 1769480 | tf_op jit(solution)/shard_map/ppermute | solution.py:758
  142.3 15.2 %collective-permute-start.38 = (bf16[4,288,256]{2,1,0:T(8,128)(2,1)S(1)}, bf16[4,288,256]{2,1,0:T(8,128)(2,1)S(1)}, u32[]{:S(2)}, u32[]{:S(2)}) collective-permute-start(bf16[4,288,256]{2,1,0:T(8,128)(2,1)S(1)} %collective-permute-done.33.refs_2_), channel_id=1, source_target_pairs={{0,2},{1,5},{2,0},{3,7},{4,6},{5,1},{6,4},{7,3},{8,10},{9,13},{10,... | collective-permute-start | bytes 1769480 | tf_op jit(solution)/shard_map/ppermute | solution.py:758
  (13 other events, 48.7 us)

commit v5 on v4

--- a/solution.py
+++ b/solution.py
@@ -877,7 +877,9 @@
     vectors = jnp.concatenate([stat_c[:2], stat_b[2:3], stat_b[:2], stat_a[:6], counts[:1].reshape(-1, ch)])
     steps = links.small_steps()
     sum2 = gather(sum2, rest)
-    sum1 = paired(keep1, give1)
+    got1 = [links.send(give1[k], first) for k in range(give1.shape[0])]
+    sum1 = jnp.stack([(keep1[k].astype(F32) + g.astype(F32)).astype(BF) for k, g in enumerate(got1)])
+    sum1 = sum1.reshape(lead[1:] + sum1.shape[1:])
     sum1, in_send = together(sum1, in_send)
     in_got = links.partner(in_send)
     vectors = steps[0](vectors)

time: 163 us -> 166 us (1.018)
    ppermute x28 -> x31, starting transfers between devices: 37.8 us -> 38.9 us  [send(): return lax.ppermute(value, AXES, pairs)]
    ppermute x28 -> x31, waiting for transfers between devices: 46.3 us -> 47 us  [send(): return lax.ppermute(value, AXES, pairs)]
  transfers between devices with their start and end apart: 44 -> 47, of which waited for: 23 -> 24; matrix products, arithmetic and copies ran while one was open for 1% -> 1% of each run, Pallas kernels for 31% -> 30%
where the time goes in v5:
time: 166 us; the launch traced here: 165 us
  Pallas kernels  60.2 us (36%)
  waiting for transfers between devices  52.8 us (32%)
  starting transfers between devices  48.4 us (29%)
  other arithmetic  2.16 us (1%)
    ppermute x31, waiting for transfers between devices, send(): return lax.ppermute(value, AXES, pairs)  47 us
    ppermute x31, starting transfers between devices, send(): return lax.ppermute(value, AXES, pairs)  38.9 us
    pallas_call x4, Pallas kernels, run_conv_finish(): pl.pallas_call(functools.partial(conv_finish_body, firsts=[first for _, _...  10.9 us
    pallas_call x1, Pallas kernels, run_attention(): pl.pallas_call(functools.partial(attention_body, side=side), name='attent...  10.1 us
    pallas_call x4, Pallas kernels, run_kernel_grad(): pl.pallas_call(functools.partial(kernel_grad_body, side=side, other=other...  7.81 us
    pallas_call x1, Pallas kernels, run_entry(): pl.pallas_call(functools.partial(entry_body, side=side), name='entry', in...  7.31 us
    pallas_call x1, Pallas kernels, run_back1(): pl.pallas_call(functools.partial(back1_body, side=side), name='conv1_back...  7.21 us
    ppermute x3, starting transfers between devices, far(): return lax.ppermute(value, AXES, pairs)  6.22 us
  transfers between devices with their start and end apart: 47, of which 24 were waited for; matrix products, arithmetic and copies ran while one was open for 1% of the time, Pallas kernels for 30%

profile of v5, /device:TPU:0, one launch (start us, length us, event | category | flops | bytes accessed | tf_op | source)
XLA Modules:
  0.0 165.4 jit_solution(4162457176866230849)
XLA Ops:
  1.3 2.7 %prepare.1 = (f32[8,1024]{1,0:T(8,128)S(1)}, bf16[256,1024]{1,0:T(8,128)(2,1)S(1)}, bf16[16,8,256]{2,1,0:T(8,128)(2,1)S(1)}, bf16[16,8,256]{2,1,0:T(8,128)(2,1)S(1)}, f32[16,512]{1,0:T(8,128)S(1)}) custom-call(s32[9]{0:T(128)S(1)} %stack.93.place_ref, s32[1,512]{1,0:T(1,128)} %bitcast.119, s32[1,1024]{1,0:T(1,128)} %bitcast.117, s32[1,1024]{1,0:T(1,128)} %bitcast.118, ...), custom_call_target="tpu_custom_call" | custom-call | flops 2529999872 | bytes 1048576 | tf_op jit(solution)/shard_map/prepare/pallas_call | solution.py:590
  4.0 7.3 %entry.1 = (bf16[2,2,256,256]{3,2,1,0:T(8,128)(2,1)S(1)}, bf16[2,2,256,256]{3,2,1,0:T(8,128)(2,1)S(1)}, bf16[2,2,256,256]{3,2,1,0:T(8,128)(2,1)S(1)}, bf16[2,2,2...) custom-call(s32[9]{0:T(128)S(1)} %stack.93.place_ref, ...), custom_call_target="tpu_custom_call" | custom-call | flops 9774999552 | bytes 1048576 | tf_op jit(solution)/shard_map/entry/pallas_call | solution.py:195
  11.4 2.6 %collective-permute-start.3 = (bf16[2,2,256,256]{3,2,1,0:T(8,128)(2,1)S(1)}, bf16[2,2,256,256]{3,2,1,0:T(8,128)(2,1)S(1)}, u32[]{:S(2)}, u32[]{:S(2)}) collective-permute-start(bf16[2,2,256,256]{3,2,1,0:T(8,128)(2,1)S(1)} %get-tuple-element.143), channel_id=1, source_target_pairs={{0,5},{1,2},{2,7},{3,0},{4,1},{5,6},{6,3},{7,4},{8,13},{9,10},{10,... | collective-permute-start | bytes 1572872 | tf_op jit(solution)/shard_map/ppermute | solution.py:766
  15.6 10.1 %attention.1 = (bf16[2,256,512]{2,1,0:T(8,128)(2,1)}, f32[2,256,512]{2,1,0:T(8,128)S(1)}, bf16[2,256,256]{2,1,0:T(8,128)(2,1)S(1)}, bf16[2,256,256]{2,1,0:T(8,12...) custom-call(s32[9]{0:T(128)S(1)} %stack.93.place_ref, ...), custom_call_target="tpu_custom_call" | custom-call | flops 15525000192 | bytes 1048576 | tf_op jit(solution)/shard_map/attention/pallas_call | solution.py:308
  35.6 2.0 %conv2_grad_other.1 = bf16[4,288,256]{2,1,0:T(8,128)(2,1)S(1)} custom-call(s32[9]{0:T(128)S(1)} %stack.93.place_ref, bf16[768,2048]{1,0:T(8,128)(2,1)S(1)} %turn.2.s_ref, bf16[2,256,256]{2,1,0:T(8,128)(2,1)S(1)} %get-tuple-element.148.refs_0_, bf16[2,256,256]{2,1,0:T(8,128)(2,1)S(1)} %collective-permute-done.6.refs_1_, ...), custom_call_target="tpu_custom_call" | custom-call | flops 1840000000 | bytes 1048576 | tf_op jit(solution)/shard_map/conv2_grad_other/pallas_call | solution.py:524
  39.3 2.0 %conv2_grad.1 = bf16[4,288,256]{2,1,0:T(8,128)(2,1)S(1)} custom-call(s32[9]{0:T(128)S(1)} %stack.93.place_ref, bf16[768,2048]{1,0:T(8,128)(2,1)S(1)} %turn.2.s_ref, bf16[2,256,256]{2,1,0:T(8,128)(2,1)S(1)} %get-tuple-element.148.refs_0_, bf16[2,256,256]{2,1,0:T(8,128)(2,1)S(1)} %collective-permute-done.6.refs_1_, ...), custom_call_target="tpu_custom_call" | custom-call | flops 1840000000 | bytes 1048576 | tf_op jit(solution)/shard_map/conv2_grad/pallas_call | solution.py:524
  44.1 4.3 %conv2_back.1 = (bf16[2,256,256]{2,1,0:T(8,128)(2,1)S(1)}, bf16[2,256,256]{2,1,0:T(8,128)(2,1)S(1)}, bf16[2,256,512]{2,1,0:T(8,128)(2,1)S(1)}, f32[8,512]{1,0:T(8,128)S(1)}) custom-call(s32[9]{0:T(128)S(1)} %stack.93.place_ref, f32[2,256,512]{2,1,0:T(8,128)S(1)} %get-tuple-element.156.dres_ref, f32[2,256,512]{2,1,0:T(8,128)S(1)} %get-tuple-element.157.norm2_ref, ...), custom_call_target="tpu_custom_call" | custom-call | flops 5750000128 | bytes 1048576 | tf_op jit(solution)/shard_map/conv2_back/pallas_call | solution.py:370
  48.4 1.8 %collective-permute-start.16 = (bf16[2,256,256]{2,1,0:T(8,128)(2,1)S(1)}, bf16[2,256,256]{2,1,0:T(8,128)(2,1)S(1)}, u32[]{:S(2)}, u32[]{:S(2)}) collective-permute-start(bf16[2,256,256]{2,1,0:T(8,128)(2,1)S(1)} %get-tuple-element.169), channel_id=1, source_target_pairs={{0,5},{1,2},{2,7},{3,0},{4,1},{5,6},{6,3},{7,4},{8,13},{9,10},{10,... | collective-permute-start | bytes 786440 | tf_op jit(solution)/shard_map/ppermute | solution.py:766
  51.3 2.1 %collective-permute-start.11 = (bf16[424,256]{1,0:T(8,128)(2,1)S(1)}, bf16[424,256]{1,0:T(8,128)(2,1)S(1)}, u32[]{:S(2)}, u32[]{:S(2)}) collective-permute-start(bf16[424,256]{1,0:T(8,128)(2,1)S(1)} %get-tuple-element.226), channel_id=1, source_target_pairs={{0,8},{1,9},{2,10},{3,11},{4,12},{5,13},{6,14},{7,15},{8,0},{9,1},... | collective-permute-start | bytes 651272 | tf_op jit(solution)/shard_map/ppermute | solution.py:758
  53.5 2.5 %collective-permute-start.13 = (bf16[424,256]{1,0:T(8,128)(2,1)S(1)}, bf16[424,256]{1,0:T(8,128)(2,1)S(1)}, u32[]{:S(2)}, u32[]{:S(2)}) collective-permute-start(bf16[424,256]{1,0:T(8,128)(2,1)S(1)} %get-tuple-element.227), channel_id=1, source_target_pairs={{0,24},{1,25},{2,26},{3,27},{4,28},{5,29},{6,30},{7,31},{8,16},{9,... | collective-permute-start | bytes 651272 | tf_op jit(solution)/shard_map/ppermute | solution.py:758
  57.1 2.6 %collective-permute-start.12 = (bf16[424,256]{1,0:T(8,128)(2,1)S(1)}, bf16[424,256]{1,0:T(8,128)(2,1)S(1)}, u32[]{:S(2)}, u32[]{:S(2)}) collective-permute-start(bf16[424,256]{1,0:T(8,128)(2,1)S(1)} %get-tuple-element.228), channel_id=1, source_target_pairs={{0,16},{1,17},{2,18},{3,19},{4,20},{5,21},{6,22},{7,23},{8,24},{9,... | collective-permute-start | bytes 651272 | tf_op jit(solution)/shard_map/ppermute | solution.py:758
  59.7 7.2 %conv1_back.1 = (bf16[4,128,512]{2,1,0:T(8,128)(2,1)}, bf16[2,128,512]{2,1,0:T(8,128)(2,1)S(1)}, f32[8,512]{1,0:T(8,128)S(1)}) custom-call(s32[9]{0:T(128)S(1)} %stack.93.place_ref, bf16[2,256,512]{2,1,0:T(8,128)(2,1)S(1)} %get-tuple-element.170.dfull_ref, bf16[2,256,512]{2,1,0:T(8,128)(2,1)S(1)} %get-tuple-element.125.x_ref, ...), custom_call_target="tpu_custom_call" | custom-call | flops 115000000 | bytes 1048576 | tf_op jit(solution)/shard_map/conv1_back/pallas_call | solution.py:421
  68.5 2.0 %conv1_grad_other.1 = bf16[4,288,256]{2,1,0:T(8,128)(2,1)S(1)} custom-call(s32[9]{0:T(128)S(1)} %stack.93.place_ref, bf16[768,2048]{1,0:T(8,128)(2,1)S(1)} %turn.3.s_ref, bf16[2,256,256]{2,1,0:T(8,128)(2,1)S(1)} %get-tuple-element.168.refs_0_, bf16[2,256,256]{2,1,0:T(8,128)(2,1)S(1)} %collective-permute-done.14.refs_1_, ...), custom_call_target="tpu_custom_call" | custom-call | flops 115000000 | bytes 1048576 | tf_op jit(solution)/shard_map/conv1_grad_other/pallas_call | solution.py:524
  70.4 2.0 %conv1_grad.1 = bf16[4,288,256]{2,1,0:T(8,128)(2,1)S(1)} custom-call(s32[9]{0:T(128)S(1)} %stack.93.place_ref, bf16[768,2048]{1,0:T(8,128)(2,1)S(1)} %turn.3.s_ref, bf16[2,256,256]{2,1,0:T(8,128)(2,1)S(1)} %get-tuple-element.168.refs_0_, bf16[2,256,256]{2,1,0:T(8,128)(2,1)S(1)} %collective-permute-done.14.refs_1_, ...), custom_call_target="tpu_custom_call" | custom-call | flops 115000000 | bytes 1048576 | tf_op jit(solution)/shard_map/conv1_grad/pallas_call | solution.py:524
  72.4 2.4 %collective-permute-done.12 = bf16[424,256]{1,0:T(8,128)(2,1)S(1)} collective-permute-done((bf16[424,256]{1,0:T(8,128)(2,1)S(1)}, bf16[424,256]{1,0:T(8,128)(2,1)S(1)}, u32[]{:S(2)}, u32[]{:S(2)}) %collective-permute-start.12) | collective-permute-done | bytes 217120 | tf_op jit(solution)/shard_map/ppermute | solution.py:758
  79.1 2.6 %collective-permute-start.19 = (bf16[424,256]{1,0:T(8,128)(2,1)S(1)}, bf16[424,256]{1,0:T(8,128)(2,1)S(1)}, u32[]{:S(2)}, u32[]{:S(2)}) collective-permute-start(bf16[424,256]{1,0:T(8,128)(2,1)S(1)} %fusion.2), channel_id=1, source_target_pairs={{0,24},{1,25},{2,26},{3,27},{4,28},{5,29},{6,30},{7,31},{8,16},{9,... | collective-permute-start | bytes 651272 | tf_op jit(solution)/shard_map/ppermute | solution.py:758
  86.9 2.3 %collective-permute-done.19 = bf16[424,256]{1,0:T(8,128)(2,1)S(1)} collective-permute-done((bf16[424,256]{1,0:T(8,128)(2,1)S(1)}, bf16[424,256]{1,0:T(8,128)(2,1)S(1)}, u32[]{:S(2)}, u32[]{:S(2)}) %collective-permute-start.19) | collective-permute-done | bytes 217120 | tf_op jit(solution)/shard_map/ppermute | solution.py:758
  89.2 9.3 %collective-permute-done.18 = bf16[424,256]{1,0:T(8,128)(2,1)S(1)} collective-permute-done((bf16[424,256]{1,0:T(8,128)(2,1)S(1)}, bf16[424,256]{1,0:T(8,128)(2,1)S(1)}, u32[]{:S(2)}, u32[]{:S(2)}) %collective-permute-start.18) | collective-permute-done | bytes 217120 | tf_op jit(solution)/shard_map/ppermute | solution.py:758
  101.6 2.2 %collective-permute-start.28 = (bf16[288,256]{1,0:T(8,128)(2,1)S(1)}, bf16[288,256]{1,0:T(8,128)(2,1)S(1)}, u32[]{:S(2)}, u32[]{:S(2)}) collective-permute-start(bf16[288,256]{1,0:T(8,128)(2,1)S(1)} %get-tuple-element.231), channel_id=1, source_target_pairs={{0,16},{1,17},{2,18},{3,19},{4,20},{5,21},{6,22},{7,23},{8,24},{9,... | collective-permute-start | bytes 442376 | tf_op jit(solution)/shard_map/ppermute | solution.py:758
  104.6 3.5 %collective-permute-done.30 = f32[13,512]{1,0:T(8,128)S(1)} collective-permute-done((f32[13,512]{1,0:T(8,128)S(1)}, f32[13,512]{1,0:T(8,128)S(1)}, u32[]{:S(2)}, u32[]{:S(2)}) %collective-permute-start.30) | collective-permute-done | bytes 26656 | tf_op jit(solution)/shard_map/ppermute | solution.py:758
  108.4 5.4 %collective-permute-done.28 = bf16[288,256]{1,0:T(8,128)(2,1)S(1)} collective-permute-done((bf16[288,256]{1,0:T(8,128)(2,1)S(1)}, bf16[288,256]{1,0:T(8,128)(2,1)S(1)}, u32[]{:S(2)}, u32[]{:S(2)}) %collective-permute-start.28) | collective-permute-done | bytes 147488 | tf_op jit(solution)/shard_map/ppermute | solution.py:758
  121.3 1.8 %place_rows.1 = (bf16[4,128,512]{2,1,0:T(8,128)(2,1)}, f32[8,128]{1,0:T(8,128)}) custom-call(s32[9]{0:T(128)S(1)} %stack.93.place_ref, bf16[2,128,512]{2,1,0:T(8,128)(2,1)S(1)} %collective-permute-done.24.got_ref, bf16[4,128,512]{2,1,0:T(8,128)(2,1)} %get-tuple-element.190.into_hbm), custom_call_target="tpu_custom_call", output_to_operand_aliasing={{0}: (2, {})} | custom-call | flops 1150000000 | bytes 1048576 | tf_op jit(solution)/shard_map/place_rows/pallas_call | solution.py:447
  123.2 2.4 %collective-permute-done.33 = bf16[288,256]{1,0:T(8,128)(2,1)S(1)} collective-permute-done((bf16[288,256]{1,0:T(8,128)(2,1)S(1)}, bf16[288,256]{1,0:T(8,128)(2,1)S(1)}, u32[]{:S(2)}, u32[]{:S(2)}) %collective-permute-start.33) | collective-permute-done | bytes 147488 | tf_op jit(solution)/shard_map/ppermute | solution.py:758
  125.6 5.1 %collective-permute-done.32 = bf16[288,256]{1,0:T(8,128)(2,1)S(1)} collective-permute-done((bf16[288,256]{1,0:T(8,128)(2,1)S(1)}, bf16[288,256]{1,0:T(8,128)(2,1)S(1)}, u32[]{:S(2)}, u32[]{:S(2)}) %collective-permute-start.32) | collective-permute-done | bytes 147488 | tf_op jit(solution)/shard_map/ppermute | solution.py:758
  131.4 3.9 %collective-permute-done.38 = f32[13,512]{1,0:T(8,128)S(1)} collective-permute-done((f32[13,512]{1,0:T(8,128)S(1)}, f32[13,512]{1,0:T(8,128)S(1)}, u32[]{:S(2)}, u32[]{:S(2)}) %collective-permute-start.38) | collective-permute-done | bytes 26656 | tf_op jit(solution)/shard_map/ppermute | solution.py:758
  135.9 2.7 %conv2_finish.2.refs_2_ = f32[9,512,512]{2,1,0:T(8,128)} custom-call(s32[9]{0:T(128)S(1)} %stack.93.place_ref, bf16[8,424,256]{2,1,0:T(8,128)(2,1)S(1)} %bitcast.95, bf16[8,424,256]{2,1,0:T(8,128)(2,1)S(1)} %collective-permute-done.35.refs_1_.other0), custom_call_target="tpu_custom_call" | custom-call | flops 3449999872 | bytes 1048576 | tf_op jit(solution)/shard_map/conv2_finish/pallas_call | solution.py:687
  140.7 1.8 %collective-permute-done.36.refs_2_ = bf16[4,288,256]{2,1,0:T(8,128)(2,1)S(1)} collective-permute-done((bf16[4,288,256]{2,1,0:T(8,128)(2,1)S(1)}, bf16[4,288,256]{2,1,0:T(8,128)(2,1)S(1)}, u32[]{:S(2)}, u32[]{:S(2)}) %collective-permute-start.36) | collective-permute-done | bytes 589856 | tf_op jit(solution)/shard_map/ppermute | solution.py:758
  147.9 2.7 %conv1_finish.2.refs_4_ = f32[9,512,512]{2,1,0:T(8,128)} custom-call(s32[9]{0:T(128)S(1)} %stack.93.place_ref, bf16[4,288,256]{2,1,0:T(8,128)(2,1)S(1)} %pad_maximum_fusion.3.refs_0_, bf16[4,288,256]{2,1,0:T(8,128)(2,1)S(1)} %collective-permute-done.43.refs_1_, bf16[4,288,256]{2,1,0:T(8,128)(2,1)S(1)} %collective-permute-done.36.refs_2_, ...), custom_call_target="tpu_custom_call" | custom-call | flops 3449999872 | bytes 1048576 | tf_op jit(solution)/shard_map/conv1_finish/pallas_call | solution.py:687
  150.6 2.7 %conv2_finish.3 = f32[9,512,512]{2,1,0:T(8,128)} custom-call(s32[9]{0:T(128)S(1)} %stack.93.place_ref, bf16[8,424,256]{2,1,0:T(8,128)(2,1)S(1)} %collective-permute-done.37.refs_0_.mine1, bf16[8,424,256]{2,1,0:T(8,128)(2,1)S(1)} %collective-permute-done.42.refs_1_.other1, f32[9,512,512]{2,1,0:T(8,128)} %conv2_finish.2.refs_2_), custom_call_target="tpu_custom_call", output_to_operand_aliasing={{}: (3, {})} | custom-call | flops 3449999872 | bytes 1048576 | tf_op jit(solution)/shard_map/conv2_finish/pallas_call | solution.py:687
  153.4 3.7 %attention_finish.1 = (f32[512,512]{1,0:T(8,128)}, f32[512,512]{1,0:T(8,128)}, f32[512,512]{1,0:T(8,128)}, f32[512,512]{1,0:T(8,128)}, f32[32,256]{1,0:T(8,128)}) custom-call(s32[9]{0:T(128)S(1)} %stack.93.place_ref, bf16[8,424,256]{2,1,0:T(8,128)(2,1)S(1)} %bitcast.96, bf16[8,424,256]{2,1,0:T(8,128)(2,1)S(1)} %collective-permute-done.35.refs_1_.other0, ...), custom_call_target="tpu_custom_call" | custom-call | flops 3449999872 | bytes 1048576 | tf_op jit(solution)/shard_map/attention_finish/pallas_call | solution.py:660
  157.1 2.5 %collective-permute-done.41.refs_2_ = bf16[4,288,256]{2,1,0:T(8,128)(2,1)S(1)} collective-permute-done((bf16[4,288,256]{2,1,0:T(8,128)(2,1)S(1)}, bf16[4,288,256]{2,1,0:T(8,128)(2,1)S(1)}, u32[]{:S(2)}, u32[]{:S(2)}) %collective-permute-start.41) | collective-permute-done | bytes 589856 | tf_op jit(solution)/shard_map/ppermute | solution.py:758
  162.5 2.7 %conv1_finish.3 = f32[9,512,512]{2,1,0:T(8,128)} custom-call(s32[9]{0:T(128)S(1)} %stack.93.place_ref, bf16[4,288,256]{2,1,0:T(8,128)(2,1)S(1)} %collective-permute-done.40.refs_0_, bf16[4,288,256]{2,1,0:T(8,128)(2,1)S(1)} %collective-permute-done.45.refs_1_, ...), custom_call_target="tpu_custom_call", output_to_operand_aliasing={{}: (5, {})} | custom-call | flops 3449999872 | bytes 1048576 | tf_op jit(solution)/shard_map/conv1_finish/pallas_call | solution.py:687
  (112 shorter events, 53.0 us)
Async XLA Ops:
  11.3 14.3 %collective-permute-start.1 = (bf16[2,2,256,256]{3,2,1,0:T(8,128)(2,1)S(1)}, bf16[2,2,256,256]{3,2,1,0:T(8,128)(2,1)S(1)}, u32[]{:S(2)}, u32[]{:S(2)}) collective-permute-start(bf16[2,2,256,256]{3,2,1,0:T(8,128)(2,1)S(1)} %get-tuple-element.142), channel_id=1, source_target_pairs={{0,1},{1,0},{2,3},{3,2},{4,5},{5,4},{6,7},{7,6},{8,9},{9,8},{10,11... | collective-permute-start | bytes 1572872 | tf_op jit(solution)/shard_map/ppermute | solution.py:762
  11.4 14.2 %collective-permute-start.3 = (bf16[2,2,256,256]{3,2,1,0:T(8,128)(2,1)S(1)}, bf16[2,2,256,256]{3,2,1,0:T(8,128)(2,1)S(1)}, u32[]{:S(2)}, u32[]{:S(2)}) collective-permute-start(bf16[2,2,256,256]{3,2,1,0:T(8,128)(2,1)S(1)} %get-tuple-element.143), channel_id=1, source_target_pairs={{0,5},{1,2},{2,7},{3,0},{4,1},{5,6},{6,3},{7,4},{8,13},{9,10},{10,... | collective-permute-start | bytes 1572872 | tf_op jit(solution)/shard_map/ppermute | solution.py:766
  14.1 12.5 %collective-permute-start.2 = (bf16[2,2,256,256]{3,2,1,0:T(8,128)(2,1)S(1)}, bf16[2,2,256,256]{3,2,1,0:T(8,128)(2,1)S(1)}, u32[]{:S(2)}, u32[]{:S(2)}) collective-permute-start(bf16[2,2,256,256]{3,2,1,0:T(8,128)(2,1)S(1)} %get-tuple-element.127.near_ref), channel_id=1, source_target_pairs={{0,2},{1,5},{2,0},{3,7},{4,6},{5,1},{6,4},{7,3},{8,10},{9,13},{10,... | collective-permute-start | bytes 1572872 | tf_op jit(solution)/shard_map/ppermute | solution.py:758
  27.0 7.8 %collective-permute-start.8 = (bf16[2,256,256]{2,1,0:T(8,128)(2,1)S(1)}, bf16[2,256,256]{2,1,0:T(8,128)(2,1)S(1)}, u32[]{:S(2)}, u32[]{:S(2)}) collective-permute-start(bf16[2,256,256]{2,1,0:T(8,128)(2,1)S(1)} %get-tuple-element.149), channel_id=1, source_target_pairs={{0,5},{1,2},{2,7},{3,0},{4,1},{5,6},{6,3},{7,4},{8,13},{9,10},{10,... | collective-permute-start | bytes 786440 | tf_op jit(solution)/shard_map/ppermute | solution.py:766
  28.8 6.8 %collective-permute-start.7 = (bf16[2,256,256]{2,1,0:T(8,128)(2,1)S(1)}, bf16[2,256,256]{2,1,0:T(8,128)(2,1)S(1)}, u32[]{:S(2)}, u32[]{:S(2)}) collective-permute-start(bf16[2,256,256]{2,1,0:T(8,128)(2,1)S(1)} %get-tuple-element.148.refs_0_), channel_id=1, source_target_pairs={{0,2},{1,5},{2,0},{3,7},{4,6},{5,1},{6,4},{7,3},{8,10},{9,13},{10,... | collective-permute-start | bytes 786440 | tf_op jit(solution)/shard_map/ppermute | solution.py:758
  30.6 11.5 %collective-permute-start.5 = (bf16[8,136,256]{2,1,0:T(8,128)(2,1)S(1)}, bf16[8,136,256]{2,1,0:T(8,128)(2,1)S(1)}, u32[]{:S(2)}, u32[]{:S(2)}) collective-permute-start(bf16[8,136,256]{2,1,0:T(8,128)(2,1)S(1)} %slice.105), channel_id=1, source_target_pairs={{0,2},{1,5},{2,0},{3,7},{4,6},{5,1},{6,4},{7,3},{8,10},{9,13},{10,... | collective-permute-start | bytes 1671176 | tf_op jit(solution)/shard_map/ppermute | solution.py:758
  37.5 13.3 %collective-permute-start.10 = (bf16[4,288,256]{2,1,0:T(8,128)(2,1)S(1)}, bf16[4,288,256]{2,1,0:T(8,128)(2,1)S(1)}, u32[]{:S(2)}, u32[]{:S(2)}) collective-permute-start(bf16[4,288,256]{2,1,0:T(8,128)(2,1)S(1)} %conv2_grad_other.1), channel_id=1, source_target_pairs={{0,4},{1,3},{2,6},{3,1},{4,0},{5,7},{6,2},{7,5},{8,12},{9,11},{10,... | collective-permute-start | bytes 1769480 | tf_op jit(solution)/shard_map/ppermute | solution.py:758
  42.3 8.8 %collective-permute-start.9 = (bf16[4,136,256]{2,1,0:T(8,128)(2,1)S(1)}, bf16[4,136,256]{2,1,0:T(8,128)(2,1)S(1)}, u32[]{:S(2)}, u32[]{:S(2)}) collective-permute-start(bf16[4,136,256]{2,1,0:T(8,128)(2,1)S(1)} %slice.107), channel_id=1, source_target_pairs={{0,4},{1,3},{2,6},{3,1},{4,0},{5,7},{6,2},{7,5},{8,12},{9,11},{10,... | collective-permute-start | bytes 835592 | tf_op jit(solution)/shard_map/ppermute | solution.py:758
  48.4 20.1 %collective-permute-start.16 = (bf16[2,256,256]{2,1,0:T(8,128)(2,1)S(1)}, bf16[2,256,256]{2,1,0:T(8,128)(2,1)S(1)}, u32[]{:S(2)}, u32[]{:S(2)}) collective-permute-start(bf16[2,256,256]{2,1,0:T(8,128)(2,1)S(1)} %get-tuple-element.169), channel_id=1, source_target_pairs={{0,5},{1,2},{2,7},{3,0},{4,1},{5,6},{6,3},{7,4},{8,13},{9,10},{10,... | collective-permute-start | bytes 786440 | tf_op jit(solution)/shard_map/ppermute | solution.py:766
  50.3 18.2 %collective-permute-start.14 = (bf16[2,256,256]{2,1,0:T(8,128)(2,1)S(1)}, bf16[2,256,256]{2,1,0:T(8,128)(2,1)S(1)}, u32[]{:S(2)}, u32[]{:S(2)}) collective-permute-start(bf16[2,256,256]{2,1,0:T(8,128)(2,1)S(1)} %get-tuple-element.169), channel_id=1, source_target_pairs={{0,1},{1,0},{2,3},{3,2},{4,5},{5,4},{6,7},{7,6},{8,9},{9,8},{10,11... | collective-permute-start | bytes 786440 | tf_op jit(solution)/shard_map/ppermute | solution.py:762
  50.3 6.8 %collective-permute-start.15 = (bf16[2,256,256]{2,1,0:T(8,128)(2,1)S(1)}, bf16[2,256,256]{2,1,0:T(8,128)(2,1)S(1)}, u32[]{:S(2)}, u32[]{:S(2)}) collective-permute-start(bf16[2,256,256]{2,1,0:T(8,128)(2,1)S(1)} %get-tuple-element.168.refs_0_), channel_id=1, source_target_pairs={{0,2},{1,5},{2,0},{3,7},{4,6},{5,1},{6,4},{7,3},{8,10},{9,13},{10,... | collective-permute-start | bytes 786440 | tf_op jit(solution)/shard_map/ppermute | solution.py:758
  51.3 21.1 %collective-permute-start.11 = (bf16[424,256]{1,0:T(8,128)(2,1)S(1)}, bf16[424,256]{1,0:T(8,128)(2,1)S(1)}, u32[]{:S(2)}, u32[]{:S(2)}) collective-permute-start(bf16[424,256]{1,0:T(8,128)(2,1)S(1)} %get-tuple-element.226), channel_id=1, source_target_pairs={{0,8},{1,9},{2,10},{3,11},{4,12},{5,13},{6,14},{7,15},{8,0},{9,1},... | collective-permute-start | bytes 651272 | tf_op jit(solution)/shard_map/ppermute | solution.py:758
  53.5 18.9 %collective-permute-start.13 = (bf16[424,256]{1,0:T(8,128)(2,1)S(1)}, bf16[424,256]{1,0:T(8,128)(2,1)S(1)}, u32[]{:S(2)}, u32[]{:S(2)}) collective-permute-start(bf16[424,256]{1,0:T(8,128)(2,1)S(1)} %get-tuple-element.227), channel_id=1, source_target_pairs={{0,24},{1,25},{2,26},{3,27},{4,28},{5,29},{6,30},{7,31},{8,16},{9,... | collective-permute-start | bytes 651272 | tf_op jit(solution)/shard_map/ppermute | solution.py:758
  57.1 17.7 %collective-permute-start.12 = (bf16[424,256]{1,0:T(8,128)(2,1)S(1)}, bf16[424,256]{1,0:T(8,128)(2,1)S(1)}, u32[]{:S(2)}, u32[]{:S(2)}) collective-permute-start(bf16[424,256]{1,0:T(8,128)(2,1)S(1)} %get-tuple-element.228), channel_id=1, source_target_pairs={{0,16},{1,17},{2,18},{3,19},{4,20},{5,21},{6,22},{7,23},{8,24},{9,... | collective-permute-start | bytes 651272 | tf_op jit(solution)/shard_map/ppermute | solution.py:758
  75.0 6.8 %collective-permute-start.20 = (bf16[288,256]{1,0:T(8,128)(2,1)S(1)}, bf16[288,256]{1,0:T(8,128)(2,1)S(1)}, u32[]{:S(2)}, u32[]{:S(2)}) collective-permute-start(bf16[288,256]{1,0:T(8,128)(2,1)S(1)} %get-tuple-element.236), channel_id=1, source_target_pairs={{0,4},{1,3},{2,6},{3,1},{4,0},{5,7},{6,2},{7,5},{8,12},{9,11},{10,... | collective-permute-start | bytes 442376 | tf_op jit(solution)/shard_map/ppermute | solution.py:758
  79.1 10.1 %collective-permute-start.19 = (bf16[424,256]{1,0:T(8,128)(2,1)S(1)}, bf16[424,256]{1,0:T(8,128)(2,1)S(1)}, u32[]{:S(2)}, u32[]{:S(2)}) collective-permute-start(bf16[424,256]{1,0:T(8,128)(2,1)S(1)} %fusion.2), channel_id=1, source_target_pairs={{0,24},{1,25},{2,26},{3,27},{4,28},{5,29},{6,30},{7,31},{8,16},{9,... | collective-permute-start | bytes 651272 | tf_op jit(solution)/shard_map/ppermute | solution.py:758
  81.7 16.8 %collective-permute-start.18 = (bf16[424,256]{1,0:T(8,128)(2,1)S(1)}, bf16[424,256]{1,0:T(8,128)(2,1)S(1)}, u32[]{:S(2)}, u32[]{:S(2)}) collective-permute-start(bf16[424,256]{1,0:T(8,128)(2,1)S(1)} %fusion.2), channel_id=1, source_target_pairs={{0,16},{1,17},{2,18},{3,19},{4,20},{5,21},{6,22},{7,23},{8,24},{9,... | collective-permute-start | bytes 651272 | tf_op jit(solution)/shard_map/ppermute | solution.py:758
  81.8 16.8 %collective-permute-start.17 = (bf16[424,256]{1,0:T(8,128)(2,1)S(1)}, bf16[424,256]{1,0:T(8,128)(2,1)S(1)}, u32[]{:S(2)}, u32[]{:S(2)}) collective-permute-start(bf16[424,256]{1,0:T(8,128)(2,1)S(1)} %fusion.2), channel_id=1, source_target_pairs={{0,8},{1,9},{2,10},{3,11},{4,12},{5,13},{6,14},{7,15},{8,0},{9,1},... | collective-permute-start | bytes 651272 | tf_op jit(solution)/shard_map/ppermute | solution.py:758
  85.2 13.5 %collective-permute-start.24 = (bf16[2,128,512]{2,1,0:T(8,128)(2,1)S(1)}, bf16[2,128,512]{2,1,0:T(8,128)(2,1)S(1)}, u32[]{:S(2)}, u32[]{:S(2)}) collective-permute-start(bf16[2,128,512]{2,1,0:T(8,128)(2,1)S(1)} %get-tuple-element.178), channel_id=1, source_target_pairs={{0,1},{1,0},{2,3},{3,2},{4,5},{5,4},{6,7},{7,6},{8,9},{9,8},{10,11... | collective-permute-start | bytes 786440 | tf_op jit(solution)/shard_map/ppermute | solution.py:762
  98.6 15.3 %collective-permute-start.26 = (bf16[4,424,256]{2,1,0:T(8,128)(2,1)S(1)}, bf16[4,424,256]{2,1,0:T(8,128)(2,1)S(1)}, u32[]{:S(2)}, u32[]{:S(2)}) collective-permute-start(bf16[4,424,256]{2,1,0:T(8,128)(2,1)S(1)} %pad_maximum_fusion.1), channel_id=1, source_target_pairs={{0,4},{1,3},{2,6},{3,1},{4,0},{5,7},{6,2},{7,5},{8,12},{9,11},{10,... | collective-permute-start | bytes 2605064 | tf_op jit(solution)/shard_map/ppermute | solution.py:758
  100.3 7.9 %collective-permute-start.27 = (bf16[288,256]{1,0:T(8,128)(2,1)S(1)}, bf16[288,256]{1,0:T(8,128)(2,1)S(1)}, u32[]{:S(2)}, u32[]{:S(2)}) collective-permute-start(bf16[288,256]{1,0:T(8,128)(2,1)S(1)} %get-tuple-element.229), channel_id=1, source_target_pairs={{0,8},{1,9},{2,10},{3,11},{4,12},{5,13},{6,14},{7,15},{8,0},{9,1},... | collective-permute-start | bytes 442376 | tf_op jit(solution)/shard_map/ppermute | solution.py:758
  100.3 8.1 %collective-permute-start.29 = (bf16[288,256]{1,0:T(8,128)(2,1)S(1)}, bf16[288,256]{1,0:T(8,128)(2,1)S(1)}, u32[]{:S(2)}, u32[]{:S(2)}) collective-permute-start(bf16[288,256]{1,0:T(8,128)(2,1)S(1)} %get-tuple-element.230), channel_id=1, source_target_pairs={{0,24},{1,25},{2,26},{3,27},{4,28},{5,29},{6,30},{7,31},{8,16},{9,... | collective-permute-start | bytes 442376 | tf_op jit(solution)/shard_map/ppermute | solution.py:758
  101.6 12.2 %collective-permute-start.28 = (bf16[288,256]{1,0:T(8,128)(2,1)S(1)}, bf16[288,256]{1,0:T(8,128)(2,1)S(1)}, u32[]{:S(2)}, u32[]{:S(2)}) collective-permute-start(bf16[288,256]{1,0:T(8,128)(2,1)S(1)} %get-tuple-element.231), channel_id=1, source_target_pairs={{0,16},{1,17},{2,18},{3,19},{4,20},{5,21},{6,22},{7,23},{8,24},{9,... | collective-permute-start | bytes 442376 | tf_op jit(solution)/shard_map/ppermute | solution.py:758
  114.1 16.7 %collective-permute-start.35 = (bf16[8,424,256]{2,1,0:T(8,128)(2,1)S(1)}, bf16[8,424,256]{2,1,0:T(8,128)(2,1)S(1)}, u32[]{:S(2)}, u32[]{:S(2)}) collective-permute-start(bf16[8,424,256]{2,1,0:T(8,128)(2,1)S(1)} %bitcast.93), channel_id=1, source_target_pairs={{0,1},{1,0},{2,3},{3,2},{4,5},{5,4},{6,7},{7,6},{8,9},{9,8},{10,11... | collective-permute-start | bytes 5210120 | tf_op jit(solution)/shard_map/ppermute | solution.py:762
  114.2 26.5 %collective-permute-start.37 = (bf16[8,424,256]{2,1,0:T(8,128)(2,1)S(1)}, bf16[8,424,256]{2,1,0:T(8,128)(2,1)S(1)}, u32[]{:S(2)}, u32[]{:S(2)}) collective-permute-start(bf16[8,424,256]{2,1,0:T(8,128)(2,1)S(1)} %bitcast.94), channel_id=1, source_target_pairs={{0,2},{1,5},{2,0},{3,7},{4,6},{5,1},{6,4},{7,3},{8,10},{9,13},{10,... | collective-permute-start | bytes 5210120 | tf_op jit(solution)/shard_map/ppermute | solution.py:758
  116.9 8.7 %collective-permute-start.33 = (bf16[288,256]{1,0:T(8,128)(2,1)S(1)}, bf16[288,256]{1,0:T(8,128)(2,1)S(1)}, u32[]{:S(2)}, u32[]{:S(2)}) collective-permute-start(bf16[288,256]{1,0:T(8,128)(2,1)S(1)} %fusion.5), channel_id=1, source_target_pairs={{0,24},{1,25},{2,26},{3,27},{4,28},{5,29},{6,30},{7,31},{8,16},{9,... | collective-permute-start | bytes 442376 | tf_op jit(solution)/shard_map/ppermute | solution.py:758
  118.5 12.2 %collective-permute-start.32 = (bf16[288,256]{1,0:T(8,128)(2,1)S(1)}, bf16[288,256]{1,0:T(8,128)(2,1)S(1)}, u32[]{:S(2)}, u32[]{:S(2)}) collective-permute-start(bf16[288,256]{1,0:T(8,128)(2,1)S(1)} %fusion.5), channel_id=1, source_target_pairs={{0,16},{1,17},{2,18},{3,19},{4,20},{5,21},{6,22},{7,23},{8,24},{9,... | collective-permute-start | bytes 442376 | tf_op jit(solution)/shard_map/ppermute | solution.py:758
  119.7 10.9 %collective-permute-start.31 = (bf16[288,256]{1,0:T(8,128)(2,1)S(1)}, bf16[288,256]{1,0:T(8,128)(2,1)S(1)}, u32[]{:S(2)}, u32[]{:S(2)}) collective-permute-start(bf16[288,256]{1,0:T(8,128)(2,1)S(1)} %fusion.5), channel_id=1, source_target_pairs={{0,8},{1,9},{2,10},{3,11},{4,12},{5,13},{6,14},{7,15},{8,0},{9,1},... | collective-permute-start | bytes 442376 | tf_op jit(solution)/shard_map/ppermute | solution.py:758
  130.8 11.8 %collective-permute-start.36 = (bf16[4,288,256]{2,1,0:T(8,128)(2,1)S(1)}, bf16[4,288,256]{2,1,0:T(8,128)(2,1)S(1)}, u32[]{:S(2)}, u32[]{:S(2)}) collective-permute-start(bf16[4,288,256]{2,1,0:T(8,128)(2,1)S(1)} %pad_maximum_fusion.3.refs_0_), channel_id=1, source_target_pairs={{0,4},{1,3},{2,6},{3,1},{4,0},{5,7},{6,2},{7,5},{8,12},{9,11},{10,... | collective-permute-start | bytes 1769480 | tf_op jit(solution)/shard_map/ppermute | solution.py:758
  142.5 8.1 %collective-permute-start.42 = (bf16[8,424,256]{2,1,0:T(8,128)(2,1)S(1)}, bf16[8,424,256]{2,1,0:T(8,128)(2,1)S(1)}, u32[]{:S(2)}, u32[]{:S(2)}) collective-permute-start(bf16[8,424,256]{2,1,0:T(8,128)(2,1)S(1)} %collective-permute-done.37.refs_0_.mine1), channel_id=1, source_target_pairs={{0,1},{1,0},{2,3},{3,2},{4,5},{5,4},{6,7},{7,6},{8,9},{9,8},{10,11... | collective-permute-start | bytes 5210120 | tf_op jit(solution)/shard_map/ppermute | solution.py:762
  143.4 13.7 %collective-permute-start.40 = (bf16[4,288,256]{2,1,0:T(8,128)(2,1)S(1)}, bf16[4,288,256]{2,1,0:T(8,128)(2,1)S(1)}, u32[]{:S(2)}, u32[]{:S(2)}) collective-permute-start(bf16[4,288,256]{2,1,0:T(8,128)(2,1)S(1)} %pad_maximum_fusion.3.refs_0_), channel_id=1, source_target_pairs={{0,2},{1,5},{2,0},{3,7},{4,6},{5,1},{6,4},{7,3},{8,10},{9,13},{10,... | collective-permute-start | bytes 1769480 | tf_op jit(solution)/shard_map/ppermute | solution.py:758
  144.6 15.0 %collective-permute-start.41 = (bf16[4,288,256]{2,1,0:T(8,128)(2,1)S(1)}, bf16[4,288,256]{2,1,0:T(8,128)(2,1)S(1)}, u32[]{:S(2)}, u32[]{:S(2)}) collective-permute-start(bf16[4,288,256]{2,1,0:T(8,128)(2,1)S(1)} %collective-permute-done.36.refs_2_), channel_id=1, source_target_pairs={{0,2},{1,5},{2,0},{3,7},{4,6},{5,1},{6,4},{7,3},{8,10},{9,13},{10,... | collective-permute-start | bytes 1769480 | tf_op jit(solution)/shard_map/ppermute | solution.py:758
  (16 other events, 66.4 us)
